TPU v7x, 512 devices: a whole 4x4x16 slice. The times are simulated.
512 devices in a mesh: ctx: 64 (over z, x), head: 8 (over y, core).
Axes of the slice: x: 4, y: 4, z: 16, core: 2. Of those that a mesh axis runs over, the one named last changes fastest.
Arguments:
- queries: bfloat16 [16384, 4096], P('ctx', 'head'), may hold values from -6 to 6
- keys: bfloat16 [16384, 4096], P('ctx', 'head'), may hold values from -6 to 6
- values: bfloat16 [16384, 4096], P('ctx', 'head'), may hold values from -6 to 6
- out_grad: bfloat16 [16384, 4096], P('ctx', 'head'), may hold values from -48 to 48
- outputs: bfloat16 [16384, 4096], P('ctx', 'head'), may hold values from -1.5 to 1.5
- log_norms: float32 [16384, 32], P('ctx', 'head'), may hold values from 4 to 7
- selected: int32 [128, 32, 3], P('ctx', 'head'), may hold values from -1 to 125, as said below
Outputs:
- grad_queries: bfloat16 [16384, 4096], P(('ctx', 'head'))
- grad_keys: bfloat16 [16384, 4096], P('ctx', 'head')
- grad_values: bfloat16 [16384, 4096], P('ctx', 'head')
Inputs may be any that keep to these rules, and one draw needn't show every extreme that they name: `selected`: -1 marks no block; every other entry is a block held by a lower index of ctx than the query block's own, and the entries other than -1 of one query block and head differ. Among all entries of one index of ctx and one group of 4 heads, at most 2 name blocks held by any one other index of ctx; blocks may repeat across query blocks and heads.
All inputs are finite; a program needn't handle non-finite values.
Results may differ from a plain program's by a relative error of at most 0.0057.
Values may be sent and summed in bfloat16 or wider, within the bound.
No kernel may reach another device: no remote copies, remote signals or barrier semaphores. Data moves between devices by JAX's collectives and lax.ppermute only.
A program may use at most 64 MiB of HBM per device.

v0:
```python
import jax
import jax.numpy as jnp
from jax import lax
from jax.sharding import PartitionSpec as P

PER_PEER = 2


def joined_along(blocks, dim):
    blocks = jnp.moveaxis(blocks, 0, dim)
    lengths = blocks.shape
    return blocks.reshape(*lengths[:dim], lengths[dim] * lengths[dim + 1], *lengths[dim + 2 :])


def from_everyone(array, axis):
    count = lax.axis_size(axis)
    return lax.all_to_all(
        jnp.broadcast_to(array[None], (count, *array.shape)), axis, 0, 0, tiled=True
    )


def gathered_copies(array, axis, dim):
    return joined_along(from_everyone(array, axis), dim)


def to_pairs(matrix, blocks, heads):
    row_count, full_width = matrix.shape
    block_len = row_count // blocks
    head_dim = full_width // heads
    shaped = matrix.reshape(blocks, block_len, heads, head_dim)
    return jnp.transpose(shaped, (0, 2, 1, 3)).reshape(blocks * heads, block_len, head_dim)


def stat_pairs(matrix, blocks):
    row_count, heads = matrix.shape
    shaped = matrix.reshape(blocks, row_count // blocks, heads)
    return jnp.transpose(shaped, (0, 2, 1)).reshape(blocks * heads, row_count // blocks)


def from_pairs(pairs, blocks, heads):
    block_len, head_dim = (pairs.shape[1], pairs.shape[2])
    shaped = pairs.reshape(blocks, heads, block_len, head_dim)
    return jnp.transpose(shaped, (0, 2, 1, 3)).reshape(blocks * block_len, heads * head_dim)


def pair_grads(query_rows, key_rows, value_rows, grad_rows, norms, deltas, factor, causal):
    block_scores = (
        jnp.einsum("nsd,ntd->nst", query_rows, key_rows, preferred_element_type=jnp.float32)
        * factor
    )
    weights = jnp.exp(block_scores - norms[:, :, None])
    if causal:
        position = jnp.arange(block_scores.shape[1])
        lower = position[:, None] >= position[None, :]
        weights = jnp.where(lower[None], weights, 0.0)
    dweights = jnp.einsum("nsd,ntd->nst", grad_rows, value_rows, preferred_element_type=jnp.float32)
    dscores = weights * (dweights - deltas[:, :, None])
    weights_b = weights.astype(jnp.bfloat16)
    dscores_b = dscores.astype(jnp.bfloat16)
    grad_v = jnp.einsum("nst,nsd->ntd", weights_b, grad_rows, preferred_element_type=jnp.float32)
    grad_k = (
        jnp.einsum("nst,nsd->ntd", dscores_b, query_rows, preferred_element_type=jnp.float32)
        * factor
    )
    grad_q = (
        jnp.einsum("nst,ntd->nsd", dscores_b, key_rows, preferred_element_type=jnp.float32) * factor
    )
    return (grad_q, grad_k, grad_v)


def live_order(live, group):
    order = jnp.argsort(1 - live.astype(jnp.int32), stable=True)
    turns = (jnp.sum(live.astype(jnp.int32)) + group - 1) // group
    return (order, turns)


def one_hot(targets, alive, pair_count):
    hits = (jnp.arange(pair_count, dtype=jnp.int32)[:, None] == targets[None, :]) & alive[None, :]
    return hits.astype(jnp.bfloat16)


def shards(queries, keys, values, out_grad, outputs, log_norms, selected):
    blocks, heads, top_count = selected.shape
    row_count, full_width = queries.shape
    head_dim = full_width // heads
    pair_count = blocks * heads
    factor = head_dim ** (-0.5)
    ctx_count = lax.axis_size("ctx")
    own_index = lax.axis_index("ctx")
    group = min(8, ctx_count)
    slot_total = ctx_count * PER_PEER
    query_pairs = to_pairs(queries, blocks, heads)
    key_pairs = to_pairs(keys, blocks, heads)
    value_pairs = to_pairs(values, blocks, heads)
    grad_pairs = to_pairs(out_grad, blocks, heads)
    delta_rows = jnp.sum(
        (out_grad.astype(jnp.float32) * outputs.astype(jnp.float32)).reshape(
            row_count, heads, head_dim
        ),
        axis=2,
    )
    norm_pairs = stat_pairs(log_norms, blocks)
    delta_pairs = stat_pairs(delta_rows, blocks)
    block_len = query_pairs.shape[1]
    grad_q, grad_k, grad_v = pair_grads(
        query_pairs, key_pairs, value_pairs, grad_pairs, norm_pairs, delta_pairs, factor, True
    )
    table = gathered_copies(selected, "ctx", 0).reshape(ctx_count, pair_count * top_count)
    select_count = table.shape[1]
    select_ids = jnp.arange(select_count, dtype=jnp.int32)
    place_ids = jnp.arange(slot_total, dtype=jnp.int32)
    mine = selected.reshape(select_count)
    mine_owner = jnp.where(mine >= 0, mine // blocks, -1)
    same_owner = (mine_owner[:, None] == mine_owner[None, :]) & (mine_owner[None, :] >= 0)
    before = select_ids[None, :] < select_ids[:, None]
    mine_rank = jnp.sum((same_owner & before).astype(jnp.int32), axis=1)
    mine_place = jnp.where(mine_owner >= 0, mine_owner * PER_PEER + mine_rank, -1)
    place_match = mine_place[None, :] == place_ids[:, None]
    mine_live = jnp.any(place_match, axis=1)
    mine_query = jnp.sum(jnp.where(place_match, select_ids[None, :], 0), axis=1) // top_count
    theirs_match = (table >= 0) & (table // blocks == own_index)
    theirs_rank = jnp.cumsum(theirs_match.astype(jnp.int32), axis=1) - 1
    live_parts = []
    select_parts = []
    block_parts = []
    for slot_rank in range(PER_PEER):
        slot_hit = theirs_match & (theirs_rank == slot_rank)
        live_parts.append(jnp.any(slot_hit, axis=1))
        select_parts.append(jnp.sum(jnp.where(slot_hit, select_ids[None, :], 0), axis=1))
        block_parts.append(jnp.sum(jnp.where(slot_hit, table % blocks, 0), axis=1))
    theirs_live = jnp.stack(live_parts, axis=1).reshape(slot_total)
    theirs_select = jnp.stack(select_parts, axis=1).reshape(slot_total)
    theirs_block = jnp.stack(block_parts, axis=1).reshape(slot_total)
    theirs_key = theirs_block * heads + theirs_select // top_count % heads
    empty_pairs = jnp.zeros((pair_count, block_len, head_dim), jnp.float32)
    packed = jnp.concatenate([query_pairs, grad_pairs], axis=2)
    outgoing = jnp.where(mine_live[:, None, None], packed[mine_query], jnp.zeros((), jnp.bfloat16))
    stats = jnp.stack([norm_pairs[mine_query], delta_pairs[mine_query]], axis=1)
    stats = jnp.where(mine_live[:, None, None], stats, 0.0)
    arrived = lax.all_to_all(outgoing, "ctx", split_axis=0, concat_axis=0, tiled=True)
    arrived_stats = lax.all_to_all(stats, "ctx", split_axis=0, concat_axis=0, tiled=True)
    order, turns = live_order(theirs_live, group)

    def owner_turn(turn, carry):
        acc_k, acc_v, partial_value = carry
        picked = lax.dynamic_slice_in_dim(order, turn * group, group)
        alive = theirs_live[picked]
        target = theirs_key[picked]
        rows_in = arrived[picked]
        stats_in = arrived_stats[picked]
        part_q, part_k, part_v = pair_grads(
            rows_in[:, :, :head_dim],
            key_pairs[target],
            value_pairs[target],
            rows_in[:, :, head_dim:],
            stats_in[:, 0],
            stats_in[:, 1],
            factor,
            False,
        )
        hits = one_hot(target, alive, pair_count)
        acc_k = acc_k + jnp.einsum(
            "pg,gsd->psd", hits, part_k.astype(jnp.bfloat16), preferred_element_type=jnp.float32
        )
        acc_v = acc_v + jnp.einsum(
            "pg,gsd->psd", hits, part_v.astype(jnp.bfloat16), preferred_element_type=jnp.float32
        )
        rounded = jnp.where(
            alive[:, None, None], part_q.astype(jnp.bfloat16), jnp.zeros((), jnp.bfloat16)
        )
        partial_value = partial_value.at[picked].set(rounded)
        return (acc_k, acc_v, partial_value)

    empty_slots = jnp.zeros((slot_total, block_len, head_dim), jnp.bfloat16)
    acc_k, acc_v, partial_value = lax.fori_loop(
        0, turns, owner_turn, (empty_pairs, empty_pairs, empty_slots)
    )
    returned = lax.all_to_all(partial_value, "ctx", split_axis=0, concat_axis=0, tiled=True)
    grad_q = grad_q + jnp.einsum(
        "pc,csd->psd",
        one_hot(mine_query, mine_live, pair_count),
        returned,
        preferred_element_type=jnp.float32,
    )
    grad_k = grad_k + acc_k
    grad_v = grad_v + acc_v
    final_q = from_pairs(grad_q, blocks, heads).astype(jnp.bfloat16)
    final_k = from_pairs(grad_k, blocks, heads).astype(jnp.bfloat16)
    final_v = from_pairs(grad_v, blocks, heads).astype(jnp.bfloat16)
    spread_q = lax.all_to_all(final_q, "head", split_axis=0, concat_axis=1, tiled=True)
    return (spread_q, final_k, final_v)


def solution(mesh):
    placed = (
        P("ctx", "head"),
        P("ctx", "head"),
        P("ctx", "head"),
        P("ctx", "head"),
        P("ctx", "head"),
        P("ctx", "head"),
        P("ctx", "head", None),
    )
    return jax.shard_map(
        shards,
        mesh=mesh,
        in_specs=placed,
        out_specs=(P(("ctx", "head"), None), P("ctx", "head"), P("ctx", "head")),
        check_vma=False,
    )
```

profile of v0, /device:TPU:1, one launch (start us, length us, event | category | flops | bytes accessed | tf_op | source)
XLA Modules:
  0.0 846.8 jit_solution(9142265592058130374)
XLA Ops:
  2.1 19.1 %all-to-all-start = ((s32[64,2,4,3]{2,1,3,0:T(2,128)}), s32[64,2,4,3]{2,1,3,0:T(2,128)S(1)}, u32[]{:S(2)}, u32[]{:S(2)}) async-start(s32[64,2,4,3]{2,1,3,0:T(2,128)} %broadcast_in_dim.151), calls=%async_computation | async-start | bytes 393216 | tf_op jit(solution)/shard_map/all_to_all | solution.py:17
  28.3 6.2 gather_fusion.6
  34.5 3.9 all-to-all-done
  38.4 11.0 %all-to-all-start.2 = ((f32[128,2,128]{2,1,0:T(2,128)}), f32[128,2,128]{2,1,0:T(2,128)}, u32[]{:S(2)}, u32[]{:S(2)}) async-start(f32[128,2,128]{2,1,0:T(2,128)} %copy.210), calls=%async_computation.2 | async-start | bytes 262144 | tf_op jit(solution)/shard_map/all_to_all | solution.py:141
  49.4 7.2 broadcast_select_fusion
  56.6 7.7 all-to-all-done.2
  64.3 7.2 all-to-all-start.1
  75.2 2.5 sort.17
  77.7 354.9 %all-to-all-done.1 = bf16[128,128,256]{2,1,0:T(8,128)(2,1)} async-done(((bf16[128,128,256]{2,1,0:T(8,128)(2,1)}), bf16[128,128,256]{2,1,0:T(8,128)(2,1)}, u32[]{:S(2)}, u32[]{:S(2)}) %all-to-all-start.1) | async-done | bytes 8388640 | tf_op jit(solution)/shard_map/all_to_all | solution.py:140
  432.6 3.0 broadcast_in_dim.150
  435.7 196.7 %while.14 = (s32[]{:T(128)}, f32[8,128,128]{2,0,1:T(8,128)S(1)}, f32[8,128,128]{2,0,1:T(8,128)S(1)}, bf16[128,128,128]{2,1,0:T(8,128)(2,1)}, s32[]{:T(128)}, /*i...) while((s32[]{:T(128)}, f32[8,128,128]{2,0,1:T(8,128)S(1)}, ...), condition=%wide.region_15.16_spmd, body=%wide.region_13.15_spmd.sunk | while | flops 173803824 | bytes 10535695 | solution.py:175
  437.0 4.0 gather_fusion.3
  449.3 4.0 gather_fusion.3
  461.6 4.0 gather_fusion.3
  473.9 4.0 gather_fusion.3
  486.2 4.0 gather_fusion.3
  498.5 4.0 gather_fusion.3
  510.8 4.0 gather_fusion.3
  523.1 4.0 gather_fusion.3
  535.4 4.0 gather_fusion.3
  547.7 4.0 gather_fusion.3
  560.0 4.0 gather_fusion.3
  572.3 4.0 gather_fusion.3
  584.5 4.0 gather_fusion.3
  596.8 4.0 gather_fusion.3
  609.1 4.0 gather_fusion.3
  621.4 4.0 gather_fusion.3
  632.4 6.0 all-to-all-start.3
  640.1 172.3 %all-to-all-done.3 = bf16[128,128,128]{2,1,0:T(8,128)(2,1)} async-done(((bf16[128,128,128]{2,1,0:T(8,128)(2,1)}), bf16[128,128,128]{2,1,0:T(8,128)(2,1)}, u32[]{:S(2)}, u32[]{:S(2)}) %all-to-all-start.3) | async-done | bytes 4194336 | tf_op jit(solution)/shard_map/all_to_all | solution.py:178
  812.4 4.5 fusion.23
  818.2 21.3 %all-to-all-start.4 = ((bf16[8,32,512]{2,1,0:T(8,128)(2,1)}), bf16[8,32,512]{2,1,0:T(8,128)(2,1)S(1)}, u32[]{:S(2)}, u32[]{:S(2)}) async-start(bf16[8,32,512]{2,1,0:T(8,128)(2,1)} %convert_element_type.89), calls=%async_computation.4 | async-start | bytes 524288 | tf_op jit(solution)/shard_map/all_to_all | solution.py:190
  840.4 5.7 all-to-all-done.4
  (374 shorter events, 147.3 us)
Async XLA Ops:
  0.6 25.3 %copy-start = (f32[256,4]{0,1:T(4,128)S(1)}, f32[256,4]{0,1:T(4,128)}, u32[]{:S(2)}) copy-start(f32[256,4]{0,1:T(4,128)} %param.14) | copy-start | bytes 12292
  0.6 26.0 %copy-start.5 = (bf16[256,512]{1,0:T(8,128)(2,1)S(1)}, bf16[256,512]{1,0:T(8,128)(2,1)}, u32[]{:S(2)}) copy-start(bf16[256,512]{1,0:T(8,128)(2,1)} %param.9) | copy-start | bytes 786436
  2.1 36.3 %all-to-all-start = ((s32[64,2,4,3]{2,1,3,0:T(2,128)}), s32[64,2,4,3]{2,1,3,0:T(2,128)S(1)}, u32[]{:S(2)}, u32[]{:S(2)}) async-start(s32[64,2,4,3]{2,1,3,0:T(2,128)} %broadcast_in_dim.151), calls=%async_computation | async-start | bytes 393216 | tf_op jit(solution)/shard_map/all_to_all | solution.py:17
  26.6 7.9 copy-start.1
  26.8 0.7 copy-start.3
  38.4 25.9 %all-to-all-start.2 = ((f32[128,2,128]{2,1,0:T(2,128)}), f32[128,2,128]{2,1,0:T(2,128)}, u32[]{:S(2)}, u32[]{:S(2)}) async-start(f32[128,2,128]{2,1,0:T(2,128)} %copy.210), calls=%async_computation.2 | async-start | bytes 262144 | tf_op jit(solution)/shard_map/all_to_all | solution.py:141
  56.6 14.9 %copy-start.6 = (bf16[256,512]{1,0:T(8,128)(2,1)S(1)}, bf16[256,512]{1,0:T(8,128)(2,1)}, u32[]{:S(2)}) copy-start(bf16[256,512]{1,0:T(8,128)(2,1)} %param.10) | copy-start | bytes 786436
  56.6 15.0 %copy-start.7 = (bf16[256,512]{1,0:T(8,128)(2,1)S(1)}, bf16[256,512]{1,0:T(8,128)(2,1)}, u32[]{:S(2)}) copy-start(bf16[256,512]{1,0:T(8,128)(2,1)} %param.11) | copy-start | bytes 786436
  64.3 368.2 %all-to-all-start.1 = ((bf16[128,128,256]{2,1,0:T(8,128)(2,1)}), bf16[128,128,256]{2,1,0:T(8,128)(2,1)}, u32[]{:S(2)}, u32[]{:S(2)}) async-start(bf16[128,128,256]{2,1,0:T(8,128)(2,1)} %broadcast_select_fusion), calls=%async_computation.1 | async-start | bytes 16777216 | tf_op jit(solution)/shard_map/all_to_all | solution.py:140
  632.4 6.0 copy-start.4
  632.4 6.4 copy-start.2
  632.4 180.0 %all-to-all-start.3 = ((bf16[128,128,128]{2,1,0:T(8,128)(2,1)}), bf16[128,128,128]{2,1,0:T(8,128)(2,1)}, u32[]{:S(2)}, u32[]{:S(2)}) async-start(bf16[128,128,128]{2,1,0:T(8,128)(2,1)} %get-tuple-element.70), calls=%async_computation.3 | async-start | bytes 8388608 | tf_op jit(solution)/shard_map/all_to_all | solution.py:178
  818.2 27.8 %all-to-all-start.4 = ((bf16[8,32,512]{2,1,0:T(8,128)(2,1)}), bf16[8,32,512]{2,1,0:T(8,128)(2,1)S(1)}, u32[]{:S(2)}, u32[]{:S(2)}) async-start(bf16[8,32,512]{2,1,0:T(8,128)(2,1)} %convert_element_type.89), calls=%async_computation.4 | async-start | bytes 524288 | tf_op jit(solution)/shard_map/all_to_all | solution.py:190
where the time goes:
time: 850 us; the launch traced here: 847 us
  waiting for transfers between devices  544 us (64%)
  local copies, waits for them, and re-layouts  182 us (21%)
  starting transfers between devices  64.6 us (8%)
  matrix products  37.3 us (4%)
  other arithmetic  14.5 us (2%)
    all_to_all x1, waiting for transfers between devices, shards(): lax.all_to_all(outgoing, 'ctx', split_axis=0, concat_axis=0, tiled=True)  355 us
    all_to_all x1, waiting for transfers between devices, shards(): lax.all_to_all(partial_value, 'ctx', split_axis=0, concat_axis=0, tiled=T...  172 us
    gather x16, local copies, waits for them, and re-layouts, owner_turn(): rows_in = arrived[picked]  63.4 us
    scatter x16, local copies, waits for them, and re-layouts, owner_turn(): partial_value = partial_value.at[picked].set(rounded)  35.1 us
    gather x16, local copies, waits for them, and re-layouts, owner_turn(): stats_in = arrived_stats[picked]  23.7 us
    all_to_all x1, starting transfers between devices, shards(): lax.all_to_all(final_q, 'head', split_axis=0, concat_axis=1, tiled=True)  21.3 us
    all_to_all x1, starting transfers between devices, from_everyone(): lax.all_to_all(jnp.broadcast_to(array[None], (count, *array.shape)), axis...  19.1 us
  transfers between devices with their start and end apart: 5, of which 5 were waited for; matrix products, arithmetic and copies ran while one was open for 3% of the time, Pallas kernels for 0%

commit v1 on v0

v1 whole, which is shorter than its diff:
```python
import functools

import jax
import jax.numpy as jnp
from jax import lax
from jax.experimental import pallas as pl
from jax.experimental.pallas import tpu as pltpu
from jax.sharding import Mesh
from jax.sharding import PartitionSpec as P

X_SIZE = 4
BLOCK = 128
STAT_ROWS = 16
PER_PEER = 2
UNROLL = 2
F32 = jnp.float32
BF16 = jnp.bfloat16


def mm(left, right, left_dim, right_dim):
    return lax.dot_general(
        left, right, (((left_dim,), (right_dim,)), ((), ())), preferred_element_type=F32
    )


def three_parts(value):
    high = value.astype(BF16)
    rest = value - high.astype(F32)
    middle = rest.astype(BF16)
    low = (rest - middle.astype(F32)).astype(BF16)
    return high, middle, low


def pack_kernel(blocks, heads, q_ref, g_ref, o_ref, n_ref, out_ref):
    rows = blocks * BLOCK
    out_ref[0:rows, :] = q_ref[...]
    out_ref[rows : 2 * rows, :] = g_ref[...]
    for h in range(heads):
        cols = slice(h * BLOCK, (h + 1) * BLOCK)
        lines = []
        for b in range(blocks):
            at = slice(b * BLOCK, (b + 1) * BLOCK)
            product = g_ref[at, cols].astype(F32) * o_ref[at, cols].astype(F32)
            delta = jnp.sum(product.T, axis=0, keepdims=True)
            norm = jnp.broadcast_to(n_ref[at, h : h + 1], (BLOCK, BLOCK)).T[0:1]
            lines += list(three_parts(norm)) + list(three_parts(delta))
        lines = [line.astype(F32) for line in lines]
        pad = jnp.zeros((STAT_ROWS - len(lines), BLOCK), F32)
        out_ref[2 * rows :, cols] = jnp.concatenate(lines + [pad], axis=0).astype(BF16)


def stat_lines(tile, b):
    tile = tile.astype(F32)

    def line(at):
        return (tile[at : at + 1] + tile[at + 1 : at + 2]) + tile[at + 2 : at + 3]

    if isinstance(b, int):
        return line(6 * b), line(6 * b + 3)
    first = b == 0
    return jnp.where(first, line(0), line(6)), jnp.where(first, line(3), line(9))


def pair_terms(q, g, k, v, norm, delta, factor, keep):
    scores = mm(k, q, 1, 1) * factor
    weights = jnp.where(keep, jnp.exp(scores - norm), 0.0)
    dscores = weights * (mm(v, g, 1, 1) - delta)
    weights_b = weights.astype(BF16)
    dscores_b = dscores.astype(BF16)
    grad_v = mm(weights_b, g, 1, 0)
    grad_k = mm(dscores_b, q, 1, 0) * factor
    grad_q = mm(dscores_b, k, 0, 0) * factor
    return grad_q, grad_k, grad_v


def own_kernel(blocks, heads, factor, pack_ref, k_ref, v_ref, dq_ref, dk_ref, dv_ref):
    rows = blocks * BLOCK
    key_at = lax.broadcasted_iota(jnp.int32, (BLOCK, BLOCK), 0)
    query_at = lax.broadcasted_iota(jnp.int32, (BLOCK, BLOCK), 1)
    keep = key_at <= query_at
    for b in range(blocks):
        for h in range(heads):
            at = slice(b * BLOCK, (b + 1) * BLOCK)
            cols = slice(h * BLOCK, (h + 1) * BLOCK)
            norm, delta = stat_lines(pack_ref[2 * rows :, cols], b)
            grad_q, grad_k, grad_v = pair_terms(
                pack_ref[at, cols],
                pack_ref[rows + b * BLOCK : rows + (b + 1) * BLOCK, cols],
                k_ref[at, cols],
                v_ref[at, cols],
                norm,
                delta,
                factor,
                keep,
            )
            dq_ref[at, cols] = grad_q
            dk_ref[at, cols] = grad_k
            dv_ref[at, cols] = grad_v


def remote_kernel(blocks, factor, slots_ref, pack_ref, kv_ref, dq_ref, dkv_ref, acc_ref, line_ref):
    rows = blocks * BLOCK
    dq_ref[...] = jnp.zeros_like(dq_ref)
    acc_ref[...] = jnp.zeros_like(acc_ref)
    count = slots_ref[0]

    def turn(step, carry):
        done = []
        for u in range(UNROLL):
            slot = step * UNROLL + u
            code = slots_ref[1 + jnp.minimum(slot, count - 1)]
            live = slot < count
            kb = code % blocks
            kx = code // blocks % X_SIZE
            h = code // (blocks * X_SIZE) % 4
            b = code // (blocks * X_SIZE * 4) % blocks
            zq = code // (blocks * X_SIZE * 4 * blocks)
            cols = pl.ds(pl.multiple_of(h * BLOCK, BLOCK), BLOCK)
            q_at = pl.ds(pl.multiple_of(b * BLOCK, BLOCK), BLOCK)
            g_at = pl.ds(pl.multiple_of(rows + b * BLOCK, BLOCK), BLOCK)
            k_at = pl.ds(pl.multiple_of(kb * BLOCK, BLOCK), BLOCK)
            v_at = pl.ds(pl.multiple_of(rows + kb * BLOCK, BLOCK), BLOCK)
            norm, delta = stat_lines(pack_ref[zq, 2 * rows :, cols], b)
            terms = pair_terms(
                pack_ref[zq, q_at, cols],
                pack_ref[zq, g_at, cols],
                kv_ref[kx, k_at, cols],
                kv_ref[kx, v_at, cols],
                norm,
                delta,
                factor,
                live,
            )
            done.append((slot, code, zq, q_at, cols, kx, k_at, v_at, terms))
        for slot, code, zq, q_at, cols, kx, k_at, v_at, (grad_q, grad_k, grad_v) in done:
            acc_ref[kx, k_at, cols] += grad_k
            acc_ref[kx, v_at, cols] += grad_v
            before = slots_ref[1 + jnp.clip(slot - 1, 0, count - 1)]
            span = blocks * X_SIZE
            same = (slot > 0) & (before // span == code // span)
            total = jnp.where(same, line_ref[...], 0.0) + grad_q
            line_ref[...] = total
            dq_ref[zq, q_at, cols] = total.astype(BF16)
        return carry

    lax.fori_loop(0, (count + UNROLL - 1) // UNROLL, turn, 0)
    dkv_ref[...] = acc_ref[...].astype(BF16)


def slot_codes(table, plane, blocks):
    z_count, block_count, heads, top_count = table.shape
    slot_total = z_count * X_SIZE * PER_PEER
    span = blocks * X_SIZE
    flat = table.reshape(-1)
    total = flat.shape[0]
    ids = jnp.arange(total, dtype=jnp.int32)
    hit = (flat >= 0) & (flat // span == plane)
    code = (ids // top_count) * span + flat % span
    earlier = (ids[None, :] <= ids[:, None]) & hit[None, :]
    place = jnp.sum(earlier.astype(jnp.int32), axis=1) - 1
    match = (place[None, :] == jnp.arange(slot_total, dtype=jnp.int32)[:, None]) & hit[None, :]
    codes = jnp.sum(jnp.where(match, code[None, :], 0), axis=1)
    return jnp.concatenate([jnp.sum(hit.astype(jnp.int32))[None], codes])


def shards(queries, keys, values, out_grad, outputs, log_norms, selected):
    blocks, heads, top_count = selected.shape
    rows, width = queries.shape
    factor = (width // heads) ** (-0.5)
    z_count = lax.axis_size("z")
    x_count = lax.axis_size("x")
    params = pltpu.CompilerParams(vmem_limit_bytes=56 * 1024 * 1024)
    pack = pl.pallas_call(
        functools.partial(pack_kernel, blocks, heads),
        out_shape=jax.ShapeDtypeStruct((2 * rows + STAT_ROWS, width), BF16),
        compiler_params=params,
        name="pack",
    )(queries, out_grad, outputs, log_norms)
    packs = lax.all_gather(pack, "z")
    table = lax.all_to_all(
        jnp.broadcast_to(selected[None], (z_count, *selected.shape)), "z", 0, 0, tiled=True
    )
    both = jnp.concatenate([keys, values], axis=0)
    kvs = lax.all_to_all(
        jnp.broadcast_to(both[None], (x_count, *both.shape)), "x", 0, 0, tiled=True
    )
    own = jax.ShapeDtypeStruct((rows, width), F32)
    own_q, own_k, own_v = pl.pallas_call(
        functools.partial(own_kernel, blocks, heads, factor),
        out_shape=(own, own, own),
        compiler_params=params,
        name="own",
    )(pack, keys, values)
    codes = slot_codes(table, lax.axis_index("z"), blocks)
    part_q, part_kv = pl.pallas_call(
        functools.partial(remote_kernel, blocks, factor),
        in_specs=[
            pl.BlockSpec(memory_space=pltpu.SMEM),
            pl.BlockSpec(memory_space=pltpu.VMEM),
            pl.BlockSpec(memory_space=pltpu.VMEM),
        ],
        out_specs=(
            pl.BlockSpec(memory_space=pltpu.VMEM),
            pl.BlockSpec(memory_space=pltpu.VMEM),
        ),
        out_shape=(
            jax.ShapeDtypeStruct((z_count, rows, width), BF16),
            jax.ShapeDtypeStruct((x_count, 2 * rows, width), BF16),
        ),
        scratch_shapes=[
            pltpu.VMEM((x_count, 2 * rows, width), F32),
            pltpu.VMEM((BLOCK, BLOCK), F32),
        ],
        compiler_params=params,
        name="remote",
    )(codes, packs, kvs)
    sum_q = lax.psum_scatter(part_q, "z", scatter_dimension=0)
    back = lax.all_to_all(part_kv, "x", 0, 0, tiled=True).astype(F32)
    sum_kv = jnp.sum(back, axis=0)
    final_k = (sum_kv[:rows] + own_k).astype(BF16)
    final_v = (sum_kv[rows:] + own_v).astype(BF16)
    final_q = (sum_q.astype(F32) + own_q).astype(BF16)
    spread_q = lax.all_to_all(final_q, "head", split_axis=0, concat_axis=1, tiled=True)
    return spread_q, final_k, final_v


def solution(mesh):
    ctx_count, head_count = mesh.devices.shape
    grid = mesh.devices.reshape(ctx_count // X_SIZE, X_SIZE, head_count)
    fine = Mesh(grid, ("z", "x", "head"))
    placed = P(("z", "x"), "head")
    return jax.shard_map(
        shards,
        mesh=fine,
        in_specs=(placed,) * 6 + (P(("z", "x"), "head", None),),
        out_specs=(P(("z", "x", "head"), None), placed, placed),
        check_vma=False,
    )
```

time: 850 us -> 255 us (0.30)
  waiting for transfers between devices: 544 us -> 147 us
  local copies, waits for them, and re-layouts: 182 us -> 4.99 us
  Pallas kernels: 0 us -> 42.5 us
  matrix products: 37.3 us -> 0 us
  starting transfers between devices: 64.6 us -> 38.8 us
  between operations: 1.77 us -> 14.1 us
    all_to_all x4 -> x3, waiting for transfers between devices: 539 us -> 53.6 us  [the longest x1 21.2 us: shards(): lax.all_to_all(jnp.broadcast_to(both[None], (x_count, *both.shape)), 'x',...]
    gather x99 -> x0, local copies, waits for them, and re-layouts: 134 us -> none  [the longest x16 63.4 us: owner_turn(): rows_in = arrived[picked]]
    all_gather x0 -> x1, waiting for transfers between devices: none -> 56.6 us  [shards(): packs = lax.all_gather(pack, 'z')]
    pallas_call x0 -> x3, Pallas kernels: none -> 42.5 us  [the longest x1 35.8 us: shards(): pl.pallas_call(functools.partial(remote_kernel, blocks, factor), in_specs...]
    dot_general x118 -> x0, matrix products: 37.3 us -> none  [the longest x17 5.34 us: pair_grads(): jnp.einsum('nsd,ntd->nst', query_rows, key_rows, preferred_element_type=j...]
    scatter x16 -> x0, local copies, waits for them, and re-layouts: 35.1 us -> none  [owner_turn(): partial_value = partial_value.at[picked].set(rounded)]
    reduce_scatter x0 -> x1, waiting for transfers between devices: none -> 32.3 us  [shards(): sum_q = lax.psum_scatter(part_q, 'z', scatter_dimension=0)]
    all_to_all x4 -> x3, starting transfers between devices: 43.2 us -> 23.4 us  [the longest x1 15.7 us: shards(): lax.all_to_all(jnp.broadcast_to(selected[None], (z_count, *selected.shape...]
  transfers between devices with their start and end apart: 5 -> 6, of which waited for: 5 -> 6; matrix products, arithmetic and copies ran while one was open for 3% -> 3% of each run, Pallas kernels for 0% -> 2%
where the time goes in v1:
time: 255 us; the launch traced here: 254 us
  waiting for transfers between devices  147 us (58%)
  Pallas kernels  42.5 us (17%)
  starting transfers between devices  38.8 us (15%)
  between operations  14.1 us (6%)
  other arithmetic  6.74 us (3%)
  local copies, waits for them, and re-layouts  4.99 us (2%)
    all_gather x1, waiting for transfers between devices, shards(): packs = lax.all_gather(pack, 'z')  56.6 us
    pallas_call x1, Pallas kernels, shards(): pl.pallas_call(functools.partial(remote_kernel, blocks, factor), in_specs...  35.8 us
    reduce_scatter x1, waiting for transfers between devices, shards(): sum_q = lax.psum_scatter(part_q, 'z', scatter_dimension=0)  32.3 us
    all_to_all x1, waiting for transfers between devices, shards(): lax.all_to_all(jnp.broadcast_to(both[None], (x_count, *both.shape)), 'x',...  21.2 us
    all_to_all x1, waiting for transfers between devices, shards(): back = lax.all_to_all(part_kv, 'x', 0, 0, tiled=True).astype(F32)  20.6 us
    all_to_all x1, starting transfers between devices, shards(): lax.all_to_all(jnp.broadcast_to(selected[None], (z_count, *selected.shape...  15.7 us
    all_to_all x1, starting transfers between devices, shards(): lax.all_to_all(final_q, 'head', split_axis=0, concat_axis=1, tiled=True)  15.4 us
    all_to_all x1, waiting for transfers between devices, shards(): lax.all_to_all(jnp.broadcast_to(selected[None], (z_count, *selected.shape...  11.7 us
  transfers between devices with their start and end apart: 6, of which 6 were waited for; matrix products, arithmetic and copies ran while one was open for 3% of the time, Pallas kernels for 2%

profile of v1, /device:TPU:1, one launch (start us, length us, event | category | flops | bytes accessed | tf_op | source)
XLA Modules:
  0.0 254.0 jit_solution(16889295950344533920)
XLA Ops:
  7.2 0.0 copy-start.1
  7.2 0.0 copy-start.2
  7.2 0.0 all-gather.3.cloned.1.call-start
  7.2 1.5 copy.20.n_ref
  8.8 2.6 %pack.1.pack_ref = bf16[528,512]{1,0:T(8,128)(2,1)} custom-call(bf16[256,512]{1,0:T(8,128)(2,1)} %q_ref.1, bf16[256,512]{1,0:T(8,128)(2,1)} %g_ref.1, bf16[256,512]{1,0:T(8,128)(2,1)} %o_ref.1, f32[256,4]{1,0:T(8,128)} %copy.20.n_ref), custom_call_target="tpu_custom_call" | custom-call | tf_op jit(solution)/shard_map/pack/pallas_call | solution.py:173
  11.4 0.0 all-gather.3.cloned.1.call-update
  11.4 0.6 broadcast_in_dim.14
  12.0 15.7 %all-to-all-start = ((s32[16,2,4,3]{2,1,3,0:T(2,128)}), s32[16,2,4,3]{2,1,3,0:T(2,128)S(1)}, u32[]{:S(2)}, u32[]{:S(2)}) async-start(s32[16,2,4,3]{2,1,3,0:T(2,128)} %broadcast_in_dim.14), calls=%async_computation | async-start | bytes 98304 | tf_op jit(solution)/shard_map/all_to_all | solution.py:180
  27.8 0.0 copy-done.1
  27.8 11.7 %all-to-all-done = s32[16,2,4,3]{2,1,3,0:T(2,128)S(1)} async-done(((s32[16,2,4,3]{2,1,3,0:T(2,128)}), s32[16,2,4,3]{2,1,3,0:T(2,128)S(1)}, u32[]{:S(2)}, u32[]{:S(2)}) %all-to-all-start) | async-done | bytes 1568 | tf_op jit(solution)/shard_map/all_to_all | solution.py:180
  39.5 1.6 broadcast_in_dim.18
  41.1 4.0 %all-to-all-start.1 = ((bf16[4,512,512]{2,1,0:T(8,128)(2,1)}), bf16[4,512,512]{2,1,0:T(8,128)(2,1)S(1)}, u32[]{:S(2)}, u32[]{:S(2)}) async-start(bf16[4,512,512]{2,1,0:T(8,128)(2,1)} %broadcast_in_dim.18), calls=%async_computation.1 | async-start | bytes 4194304 | tf_op jit(solution)/shard_map/all_to_all | solution.py:184
  45.1 0.3 copy.19
  45.4 0.2 reshape.89
  45.7 0.1 convert_reduce_fusion.1
  45.8 0.1 select_reduce_fusion
  45.9 0.8 fusion.5
  46.7 1.3 pad_add_fusion.slots_ref
  48.0 21.2 %all-to-all-done.1.kv_ref = bf16[4,512,512]{2,1,0:T(8,128)(2,1)S(1)} async-done(((bf16[4,512,512]{2,1,0:T(8,128)(2,1)}), bf16[4,512,512]{2,1,0:T(8,128)(2,1)S(1)}, u32[]{:S(2)}, u32[]{:S(2)}) %all-to-all-start.1) | async-done | bytes 2097184 | tf_op jit(solution)/shard_map/all_to_all | solution.py:184
  69.3 56.6 %all-gather.3.cloned.1.call-done = bf16[8448,512]{1,0:T(8,128)(2,1)} async-done(((bf16[528,512]{1,0:T(8,128)(2,1)}), bf16[8448,512]{1,0:T(8,128)(2,1)}) %all-gather.3.cloned.1.call-update) | async-done | bytes 8650768 | tf_op jit(solution)/shard_map/all_gather | solution.py:179
  125.8 35.8 %remote.1 = (bf16[16,256,512]{2,1,0:T(8,128)(2,1)}, bf16[4,512,512]{2,1,0:T(8,128)(2,1)}) custom-call(s32[129]{0:T(256)} %pad_add_fusion.slots_ref, bf16[16,528,512]{2,1,0:T(8,128)(2,1)} %bitcast.9, bf16[4,512,512]{2,1,0:T(8,128)(2,1)} %copy-done), custom_call_target="tpu_custom_call" | custom-call | tf_op jit(solution)/shard_map/remote/pallas_call | solution.py:195
  161.7 0.0 reduce-scatter.2.cloned.1.call-update
  161.7 3.6 %all-to-all-start.3 = ((bf16[4,512,512]{2,1,0:T(8,128)(2,1)}), bf16[4,512,512]{2,1,0:T(8,128)(2,1)S(1)}, u32[]{:S(2)}, u32[]{:S(2)}) async-start(bf16[4,512,512]{2,1,0:T(8,128)(2,1)} %get-tuple-element.10), calls=%async_computation.4 | async-start | bytes 4194304 | tf_op jit(solution)/shard_map/all_to_all | solution.py:218
  165.3 4.1 %own.1 = (f32[256,512]{1,0:T(8,128)}, f32[256,512]{1,0:T(8,128)}, f32[256,512]{1,0:T(8,128)}) custom-call(bf16[528,512]{1,0:T(8,128)(2,1)} %pack.1.pack_ref, bf16[256,512]{1,0:T(8,128)(2,1)} %k_ref.1, bf16[256,512]{1,0:T(8,128)(2,1)} %v_ref.1), custom_call_target="tpu_custom_call" | custom-call | tf_op jit(solution)/shard_map/own/pallas_call | solution.py:188
  169.4 20.6 %all-to-all-done.3 = bf16[4,512,512]{2,1,0:T(8,128)(2,1)S(1)} async-done(((bf16[4,512,512]{2,1,0:T(8,128)(2,1)}), bf16[4,512,512]{2,1,0:T(8,128)(2,1)S(1)}, u32[]{:S(2)}, u32[]{:S(2)}) %all-to-all-start.3) | async-done | bytes 2097184 | tf_op jit(solution)/shard_map/all_to_all | solution.py:218
  190.1 0.3 convert_reduce_fusion
  190.4 32.3 %reduce-scatter.2.cloned.1.call-done = bf16[1,256,512]{2,1,0:T(8,128)(2,1)} async-done(((bf16[16,256,512]{2,1,0:T(8,128)(2,1)}), bf16[1,256,512]{2,1,0:T(8,128)(2,1)}) %reduce-scatter.2.cloned.1.call-update) | async-done | bytes 262160 | tf_op jit(solution)/shard_map/reduce_scatter | solution.py:217
  222.7 1.9 fusion.3
  224.6 15.4 %all-to-all-start.2 = ((bf16[8,32,512]{2,1,0:T(8,128)(2,1)}), bf16[8,32,512]{2,1,0:T(8,128)(2,1)S(1)}, u32[]{:S(2)}, u32[]{:S(2)}) async-start(bf16[8,32,512]{2,1,0:T(8,128)(2,1)} %bitcast.3), calls=%async_computation.3 | async-start | bytes 524288 | tf_op jit(solution)/shard_map/all_to_all | solution.py:223
  239.9 2.1 fusion.1
  242.1 4.4 %all-to-all-done.2 = bf16[8,32,512]{2,1,0:T(8,128)(2,1)S(1)} async-done(((bf16[8,32,512]{2,1,0:T(8,128)(2,1)}), bf16[8,32,512]{2,1,0:T(8,128)(2,1)S(1)}, u32[]{:S(2)}, u32[]{:S(2)}) %all-to-all-start.2) | async-done | bytes 262176 | tf_op jit(solution)/shard_map/all_to_all | solution.py:223
  246.5 0.7 copy.22
  (9 shorter events, 0.1 us)
Async XLA Ops:
  7.2 4.2 %copy-start.3 = (s32[2,4,3]{1,0,2:T(2,128)S(1)}, s32[2,4,3]{1,0,2:T(2,128)}, u32[]{:S(2)}) copy-start(s32[2,4,3]{1,0,2:T(2,128)} %param.13) | copy-start | bytes 292
  7.2 20.6 %copy-start.1 = (bf16[256,512]{1,0:T(8,128)(2,1)S(1)}, bf16[256,512]{1,0:T(8,128)(2,1)}, u32[]{:S(2)}) copy-start(bf16[256,512]{1,0:T(8,128)(2,1)} %k_ref.1) | copy-start | bytes 786436
  7.2 20.6 %copy-start.2 = (bf16[256,512]{1,0:T(8,128)(2,1)S(1)}, bf16[256,512]{1,0:T(8,128)(2,1)}, u32[]{:S(2)}) copy-start(bf16[256,512]{1,0:T(8,128)(2,1)} %v_ref.1) | copy-start | bytes 786436
  7.2 118.6 %all-gather.3.cloned.1.call-start = ((), (), s32[]{:S(2)}) async-start(), calls=%async_computation.6 | async-start | bytes 9191424 | tf_op jit(solution)/shard_map/all_gather | solution.py:179
  12.0 27.5 %all-to-all-start = ((s32[16,2,4,3]{2,1,3,0:T(2,128)}), s32[16,2,4,3]{2,1,3,0:T(2,128)S(1)}, u32[]{:S(2)}, u32[]{:S(2)}) async-start(s32[16,2,4,3]{2,1,3,0:T(2,128)} %broadcast_in_dim.14), calls=%async_computation | async-start | bytes 98304 | tf_op jit(solution)/shard_map/all_to_all | solution.py:180
  41.1 28.2 %all-to-all-start.1 = ((bf16[4,512,512]{2,1,0:T(8,128)(2,1)}), bf16[4,512,512]{2,1,0:T(8,128)(2,1)S(1)}, u32[]{:S(2)}, u32[]{:S(2)}) async-start(bf16[4,512,512]{2,1,0:T(8,128)(2,1)} %broadcast_in_dim.18), calls=%async_computation.1 | async-start | bytes 4194304 | tf_op jit(solution)/shard_map/all_to_all | solution.py:184
  45.1 177.6 %reduce-scatter.2.cloned.1.call-start = ((), (), s32[]{:S(2)}) async-start(), calls=%async_computation.5 | async-start | bytes 4456448 | tf_op jit(solution)/shard_map/reduce_scatter | solution.py:217
  69.3 56.6 %copy-start = (bf16[4,512,512]{2,1,0:T(8,128)(2,1)}, bf16[4,512,512]{2,1,0:T(8,128)(2,1)S(1)}, u32[]{:S(2)}) copy-start(bf16[4,512,512]{2,1,0:T(8,128)(2,1)S(1)} %all-to-all-done.1.kv_ref) | copy-start | bytes 6291460
  161.7 28.4 %all-to-all-start.3 = ((bf16[4,512,512]{2,1,0:T(8,128)(2,1)}), bf16[4,512,512]{2,1,0:T(8,128)(2,1)S(1)}, u32[]{:S(2)}, u32[]{:S(2)}) async-start(bf16[4,512,512]{2,1,0:T(8,128)(2,1)} %get-tuple-element.10), calls=%async_computation.4 | async-start | bytes 4194304 | tf_op jit(solution)/shard_map/all_to_all | solution.py:218
  224.6 21.9 %all-to-all-start.2 = ((bf16[8,32,512]{2,1,0:T(8,128)(2,1)}), bf16[8,32,512]{2,1,0:T(8,128)(2,1)S(1)}, u32[]{:S(2)}, u32[]{:S(2)}) async-start(bf16[8,32,512]{2,1,0:T(8,128)(2,1)} %bitcast.3), calls=%async_computation.3 | async-start | bytes 524288 | tf_op jit(solution)/shard_map/all_to_all | solution.py:223
Sparse Core Ops, SparseCore 0:
  11.5 114.2 all-gather.2
  161.8 60.8 reduce-scatter.1

commit v2 on v1

--- a/solution.py
+++ b/solution.py
@@ -12,7 +12,8 @@
 BLOCK = 128
 STAT_ROWS = 16
 PER_PEER = 2
-UNROLL = 2
+PAIR = 2
+UNROLL = 4
 F32 = jnp.float32
 BF16 = jnp.bfloat16
 
@@ -42,7 +43,7 @@
             at = slice(b * BLOCK, (b + 1) * BLOCK)
             product = g_ref[at, cols].astype(F32) * o_ref[at, cols].astype(F32)
             delta = jnp.sum(product.T, axis=0, keepdims=True)
-            norm = jnp.broadcast_to(n_ref[at, h : h + 1], (BLOCK, BLOCK)).T[0:1]
+            norm = n_ref[h : h + 1, at]
             lines += list(three_parts(norm)) + list(three_parts(delta))
         lines = [line.astype(F32) for line in lines]
         pad = jnp.zeros((STAT_ROWS - len(lines), BLOCK), F32)
@@ -98,11 +99,26 @@
             dv_ref[at, cols] = grad_v
 
 
-def remote_kernel(blocks, factor, slots_ref, pack_ref, kv_ref, dq_ref, dkv_ref, acc_ref, line_ref):
+def remote_kernel(blocks, heads, factor, owners, *refs):
+    slots_ref, packs_ref, own_k_ref, own_v_ref = refs[:4]
+    kv_refs = refs[4 : 4 + owners]
+    dq_ref, near_ref = refs[4 + owners : 6 + owners]
+    far_refs = refs[6 + owners : 5 + 2 * owners]
+    acc_ref, line_ref, pack_ref, kv_ref, sems = refs[5 + 2 * owners :]
     rows = blocks * BLOCK
+    span = blocks * owners
+    loads = [pltpu.make_async_copy(packs_ref, pack_ref, sems.at[owners])]
+    for at in range(owners):
+        loads.append(pltpu.make_async_copy(kv_refs[at], kv_ref.at[at], sems.at[at]))
+    for load in loads:
+        load.start()
     dq_ref[...] = jnp.zeros_like(dq_ref)
-    acc_ref[...] = jnp.zeros_like(acc_ref)
+    acc_ref[0, :rows] = own_k_ref[...]
+    acc_ref[0, rows:] = own_v_ref[...]
+    acc_ref[1:] = jnp.zeros((owners - 1, *acc_ref.shape[1:]), F32)
     count = slots_ref[0]
+    for load in loads:
+        load.wait()
 
     def turn(step, carry):
         done = []
@@ -111,10 +127,10 @@
             code = slots_ref[1 + jnp.minimum(slot, count - 1)]
             live = slot < count
             kb = code % blocks
-            kx = code // blocks % X_SIZE
-            h = code // (blocks * X_SIZE) % 4
-            b = code // (blocks * X_SIZE * 4) % blocks
-            zq = code // (blocks * X_SIZE * 4 * blocks)
+            kx = code // blocks % owners
+            h = code // span % heads
+            b = code // (span * heads) % blocks
+            zq = code // (span * heads * blocks)
             cols = pl.ds(pl.multiple_of(h * BLOCK, BLOCK), BLOCK)
             q_at = pl.ds(pl.multiple_of(b * BLOCK, BLOCK), BLOCK)
             g_at = pl.ds(pl.multiple_of(rows + b * BLOCK, BLOCK), BLOCK)
@@ -136,7 +152,6 @@
             acc_ref[kx, k_at, cols] += grad_k
             acc_ref[kx, v_at, cols] += grad_v
             before = slots_ref[1 + jnp.clip(slot - 1, 0, count - 1)]
-            span = blocks * X_SIZE
             same = (slot > 0) & (before // span == code // span)
             total = jnp.where(same, line_ref[...], 0.0) + grad_q
             line_ref[...] = total
@@ -144,18 +159,21 @@
         return carry
 
     lax.fori_loop(0, (count + UNROLL - 1) // UNROLL, turn, 0)
-    dkv_ref[...] = acc_ref[...].astype(BF16)
-
-
-def slot_codes(table, plane, blocks):
-    z_count, block_count, heads, top_count = table.shape
-    slot_total = z_count * X_SIZE * PER_PEER
-    span = blocks * X_SIZE
+    near_ref[...] = acc_ref[0]
+    for at in range(1, owners):
+        far_refs[at - 1][...] = acc_ref[at].astype(BF16)
+
+
+def slot_codes(table, j, p, x, owners):
+    ring, blocks, heads, top_count = table.shape
+    slot_total = ring * owners * PER_PEER
+    span = blocks * owners
     flat = table.reshape(-1)
-    total = flat.shape[0]
-    ids = jnp.arange(total, dtype=jnp.int32)
-    hit = (flat >= 0) & (flat // span == plane)
-    code = (ids // top_count) * span + flat % span
+    ids = jnp.arange(flat.shape[0], dtype=jnp.int32)
+    hit = (flat >= 0) & (flat // span == j)
+    owner = flat % span // blocks
+    near = (owner % X_SIZE - x) % X_SIZE * PAIR + (owner // X_SIZE - p) % PAIR
+    code = ids // top_count * span + near * blocks + flat % blocks
     earlier = (ids[None, :] <= ids[:, None]) & hit[None, :]
     place = jnp.sum(earlier.astype(jnp.int32), axis=1) - 1
     match = (place[None, :] == jnp.arange(slot_total, dtype=jnp.int32)[:, None]) & hit[None, :]
@@ -167,23 +185,26 @@
     blocks, heads, top_count = selected.shape
     rows, width = queries.shape
     factor = (width // heads) ** (-0.5)
-    z_count = lax.axis_size("z")
-    x_count = lax.axis_size("x")
+    ring = lax.axis_size("j")
+    owners = lax.axis_size("p") * lax.axis_size("x")
     params = pltpu.CompilerParams(vmem_limit_bytes=56 * 1024 * 1024)
     pack = pl.pallas_call(
         functools.partial(pack_kernel, blocks, heads),
         out_shape=jax.ShapeDtypeStruct((2 * rows + STAT_ROWS, width), BF16),
         compiler_params=params,
         name="pack",
-    )(queries, out_grad, outputs, log_norms)
-    packs = lax.all_gather(pack, "z")
+    )(queries, out_grad, outputs, log_norms.T)
+    packs = lax.all_gather(pack, "j")
+    pack, selected, keys, values = lax.optimization_barrier((pack, selected, keys, values))
     table = lax.all_to_all(
-        jnp.broadcast_to(selected[None], (z_count, *selected.shape)), "z", 0, 0, tiled=True
+        jnp.broadcast_to(selected[None], (ring, *selected.shape)), "j", 0, 0, tiled=True
     )
     both = jnp.concatenate([keys, values], axis=0)
-    kvs = lax.all_to_all(
-        jnp.broadcast_to(both[None], (x_count, *both.shape)), "x", 0, 0, tiled=True
-    )
+    swapped = lax.ppermute(both, "p", [(i, (i + 1) % PAIR) for i in range(PAIR)])
+    kvs = [both, swapped]
+    for shift in range(1, X_SIZE):
+        back = [(i, (i - shift) % X_SIZE) for i in range(X_SIZE)]
+        kvs += [lax.ppermute(both, "x", back), lax.ppermute(swapped, "x", back)]
     own = jax.ShapeDtypeStruct((rows, width), F32)
     own_q, own_k, own_v = pl.pallas_call(
         functools.partial(own_kernel, blocks, heads, factor),
@@ -191,34 +212,44 @@
         compiler_params=params,
         name="own",
     )(pack, keys, values)
-    codes = slot_codes(table, lax.axis_index("z"), blocks)
-    part_q, part_kv = pl.pallas_call(
-        functools.partial(remote_kernel, blocks, factor),
-        in_specs=[
-            pl.BlockSpec(memory_space=pltpu.SMEM),
-            pl.BlockSpec(memory_space=pltpu.VMEM),
-            pl.BlockSpec(memory_space=pltpu.VMEM),
-        ],
-        out_specs=(
-            pl.BlockSpec(memory_space=pltpu.VMEM),
-            pl.BlockSpec(memory_space=pltpu.VMEM),
-        ),
+    codes = slot_codes(table, lax.axis_index("j"), lax.axis_index("p"), lax.axis_index("x"), owners)
+    packs, kvs, codes, own_q, own_k, own_v = lax.optimization_barrier(
+        (packs, kvs, codes, own_q, own_k, own_v)
+    )
+    anywhere = pl.BlockSpec(memory_space=pl.ANY)
+    vmem = pl.BlockSpec(memory_space=pltpu.VMEM)
+    part_q, near, *far = pl.pallas_call(
+        functools.partial(remote_kernel, blocks, heads, factor, owners),
+        in_specs=[pl.BlockSpec(memory_space=pltpu.SMEM), anywhere, vmem, vmem] + [anywhere] * owners,
+        out_specs=(vmem,) * (owners + 1),
         out_shape=(
-            jax.ShapeDtypeStruct((z_count, rows, width), BF16),
-            jax.ShapeDtypeStruct((x_count, 2 * rows, width), BF16),
-        ),
+            jax.ShapeDtypeStruct((ring, rows, width), BF16),
+            jax.ShapeDtypeStruct((2 * rows, width), F32),
+        )
+        + (jax.ShapeDtypeStruct((2 * rows, width), BF16),) * (owners - 1),
         scratch_shapes=[
-            pltpu.VMEM((x_count, 2 * rows, width), F32),
+            pltpu.VMEM((owners, 2 * rows, width), F32),
             pltpu.VMEM((BLOCK, BLOCK), F32),
+            pltpu.VMEM((ring, 2 * rows + STAT_ROWS, width), BF16),
+            pltpu.VMEM((owners, 2 * rows, width), BF16),
+            pltpu.SemaphoreType.DMA((owners + 1,)),
         ],
         compiler_params=params,
         name="remote",
-    )(codes, packs, kvs)
-    sum_q = lax.psum_scatter(part_q, "z", scatter_dimension=0)
-    back = lax.all_to_all(part_kv, "x", 0, 0, tiled=True).astype(F32)
-    sum_kv = jnp.sum(back, axis=0)
-    final_k = (sum_kv[:rows] + own_k).astype(BF16)
-    final_v = (sum_kv[rows:] + own_v).astype(BF16)
+    )(codes, packs, own_k, own_v, *kvs)
+    sum_q = lax.psum_scatter(part_q, "j", scatter_dimension=0)
+    sum_kv = near
+    for at in range(1, owners):
+        shift, other = at // PAIR, at % PAIR
+        pairs = [
+            (p * X_SIZE + x, (p + other) % PAIR * X_SIZE + (x + shift) % X_SIZE)
+            for p in range(PAIR)
+            for x in range(X_SIZE)
+        ]
+        sum_kv = sum_kv + lax.ppermute(far[at - 1], ("p", "x"), pairs).astype(F32)
+    final_k = sum_kv[:rows].astype(BF16)
+    final_v = sum_kv[rows:].astype(BF16)
+    sum_q, final_k, final_v = lax.optimization_barrier((sum_q, final_k, final_v))
     final_q = (sum_q.astype(F32) + own_q).astype(BF16)
     spread_q = lax.all_to_all(final_q, "head", split_axis=0, concat_axis=1, tiled=True)
     return spread_q, final_k, final_v
@@ -226,13 +257,14 @@
 
 def solution(mesh):
     ctx_count, head_count = mesh.devices.shape
-    grid = mesh.devices.reshape(ctx_count // X_SIZE, X_SIZE, head_count)
-    fine = Mesh(grid, ("z", "x", "head"))
-    placed = P(("z", "x"), "head")
+    grid = mesh.devices.reshape(ctx_count // (PAIR * X_SIZE), PAIR, X_SIZE, head_count)
+    fine = Mesh(grid, ("j", "p", "x", "head"))
+    ctx = ("j", "p", "x")
+    placed = P(ctx, "head")
     return jax.shard_map(
         shards,
         mesh=fine,
-        in_specs=(placed,) * 6 + (P(("z", "x"), "head", None),),
-        out_specs=(P(("z", "x", "head"), None), placed, placed),
+        in_specs=(placed,) * 6 + (P(ctx, "head", None),),
+        out_specs=(P((*ctx, "head"), None), placed, placed),
         check_vma=False,
     )

time: 255 us -> 256 us (level)
  starting transfers between devices: 38.8 us -> 73.4 us
  waiting for transfers between devices: 147 us -> 115 us
  Pallas kernels: 42.5 us -> 29 us
  blocking collectives: 0 us -> 10.5 us
    ppermute x0 -> x14, waiting for transfers between devices: none -> 83.4 us  [the longest x7 60.2 us: shards(): sum_kv = sum_kv + lax.ppermute(far[at - 1], ('p', 'x'), pairs).astype(F32)]
    ppermute x0 -> x14, starting transfers between devices: none -> 59.4 us  [the longest x7 35 us: shards(): sum_kv = sum_kv + lax.ppermute(far[at - 1], ('p', 'x'), pairs).astype(F32)]
    all_to_all x4 -> x1, waiting for transfers between devices: 57.9 us -> 1.04 us  [shards(): lax.all_to_all(jnp.broadcast_to(selected[None], (ring, *selected.shape)),...]
    reduce_scatter x1, waiting for transfers between devices: 32.3 us -> 0.01 us  [shards(): sum_q = lax.psum_scatter(part_q, 'j', scatter_dimension=0)]
    all_gather x1, waiting for transfers between devices: 56.6 us -> 30.9 us  [shards(): packs = lax.all_gather(pack, 'j')]
    all_to_all x4 -> x1, starting transfers between devices: 38.7 us -> 13.9 us  [shards(): lax.all_to_all(jnp.broadcast_to(selected[None], (ring, *selected.shape)),...]
    pallas_call x1, Pallas kernels: 35.8 us -> 22.7 us  [shards(): pl.pallas_call(functools.partial(remote_kernel, blocks, heads, factor, ow...]
    all_to_all x0 -> x1, blocking collectives: none -> 10.5 us  [shards(): lax.all_to_all(final_q, 'head', split_axis=0, concat_axis=1, tiled=True)]
  transfers between devices with their start and end apart: 6 -> 17, of which waited for: 6 -> 10; matrix products, arithmetic and copies ran while one was open for 3% -> 3% of each run, Pallas kernels for 2% -> 2%
where the time goes in v2:
time: 256 us; the launch traced here: 254 us
  waiting for transfers between devices  115 us (45%)
  starting transfers between devices  73.4 us (29%)
  Pallas kernels  29 us (11%)
  between operations  14.3 us (6%)
  blocking collectives  10.5 us (4%)
  local copies, waits for them, and re-layouts  5.98 us (2%)
  other arithmetic  5.13 us (2%)
    ppermute x7, waiting for transfers between devices, shards(): sum_kv = sum_kv + lax.ppermute(far[at - 1], ('p', 'x'), pairs).astype(F32)  60.2 us
    ppermute x7, starting transfers between devices, shards(): sum_kv = sum_kv + lax.ppermute(far[at - 1], ('p', 'x'), pairs).astype(F32)  35 us
    all_gather x1, waiting for transfers between devices, shards(): packs = lax.all_gather(pack, 'j')  30.9 us
    ppermute x6, waiting for transfers between devices, shards(): kvs += [lax.ppermute(both, 'x', back), lax.ppermute(swapped, 'x', back)]  23.3 us
    pallas_call x1, Pallas kernels, shards(): pl.pallas_call(functools.partial(remote_kernel, blocks, heads, factor, ow...  22.7 us
    ppermute x6, starting transfers between devices, shards(): kvs += [lax.ppermute(both, 'x', back), lax.ppermute(swapped, 'x', back)]  20 us
    all_to_all x1, starting transfers between devices, shards(): lax.all_to_all(jnp.broadcast_to(selected[None], (ring, *selected.shape)),...  13.9 us
    all_to_all x1, blocking collectives, shards(): lax.all_to_all(final_q, 'head', split_axis=0, concat_axis=1, tiled=True)  10.5 us
  transfers between devices with their start and end apart: 17, of which 10 were waited for; matrix products, arithmetic and copies ran while one was open for 3% of the time, Pallas kernels for 2%

profile of v2, /device:TPU:1, one launch (start us, length us, event | category | flops | bytes accessed | tf_op | source)
XLA Modules:
  0.0 253.7 jit_solution(3329121917253668988)
XLA Ops:
  7.2 2.2 pack.1.pack_ref
  9.4 1.0 constant_dynamic-update-slice_fusion.1
  11.3 4.4 %collective-permute-start = (bf16[512,512]{1,0:T(8,128)(2,1)S(1)}, bf16[512,512]{1,0:T(8,128)(2,1)S(1)}, u32[]{:S(2)}, u32[]{:S(2)}) collective-permute-start(bf16[512,512]{1,0:T(8,128)(2,1)S(1)} %constant_dynamic-update-slice_fusion.refs_4_), channel_id=1, source_target_pairs={{0,32},{32,0},{1,33},{33,1},{2,34},{34,2},{3,35},{35,3},{4,36},{36... | collective-permute-start | bytes 1572872 | tf_op jit(solution)/shard_map/ppermute | solution.py:203
  15.7 3.1 %collective-permute-start.5 = (bf16[512,512]{1,0:T(8,128)(2,1)S(1)}, bf16[512,512]{1,0:T(8,128)(2,1)S(1)}, u32[]{:S(2)}, u32[]{:S(2)}) collective-permute-start(bf16[512,512]{1,0:T(8,128)(2,1)S(1)} %constant_dynamic-update-slice_fusion.refs_4_), channel_id=1, source_target_pairs={{0,8},{8,16},{16,24},{24,0},{1,9},{9,17},{17,25},{25,1},{2,10},{10... | collective-permute-start | bytes 1572872 | tf_op jit(solution)/shard_map/ppermute | solution.py:207
  18.9 1.3 broadcast_in_dim.12
  20.2 13.9 %all-to-all-start = ((s32[8,2,4,3]{2,1,3,0:T(2,128)}), s32[8,2,4,3]{2,1,3,0:T(2,128)S(1)}, u32[]{:S(2)}, u32[]{:S(2)}) async-start(s32[8,2,4,3]{2,1,3,0:T(2,128)} %broadcast_in_dim.12), calls=%async_computation | async-start | bytes 49152 | tf_op jit(solution)/shard_map/all_to_all | solution.py:199
  34.1 4.4 %collective-permute-start.3 = (bf16[512,512]{1,0:T(8,128)(2,1)S(1)}, bf16[512,512]{1,0:T(8,128)(2,1)S(1)}, u32[]{:S(2)}, u32[]{:S(2)}) collective-permute-start(bf16[512,512]{1,0:T(8,128)(2,1)S(1)} %constant_dynamic-update-slice_fusion.refs_4_), channel_id=1, source_target_pairs={{0,16},{8,24},{16,0},{24,8},{1,17},{9,25},{17,1},{25,9},{2,18},{10... | collective-permute-start | bytes 1572872 | tf_op jit(solution)/shard_map/ppermute | solution.py:207
  38.5 3.1 %collective-permute-start.1 = (bf16[512,512]{1,0:T(8,128)(2,1)S(1)}, bf16[512,512]{1,0:T(8,128)(2,1)S(1)}, u32[]{:S(2)}, u32[]{:S(2)}) collective-permute-start(bf16[512,512]{1,0:T(8,128)(2,1)S(1)} %constant_dynamic-update-slice_fusion.refs_4_), channel_id=1, source_target_pairs={{0,24},{8,0},{16,8},{24,16},{1,25},{9,1},{17,9},{25,17},{2,26},{10... | collective-permute-start | bytes 1572872 | tf_op jit(solution)/shard_map/ppermute | solution.py:207
  41.6 4.2 %own.1 = (f32[256,512]{1,0:T(8,128)}, f32[256,512]{1,0:T(8,128)}, f32[256,512]{1,0:T(8,128)}) custom-call(bf16[528,512]{1,0:T(8,128)(2,1)} %pack.1.pack_ref, bf16[256,512]{1,0:T(8,128)(2,1)} %k_ref, bf16[256,512]{1,0:T(8,128)(2,1)} %v_ref), custom_call_target="tpu_custom_call" | custom-call | tf_op jit(solution)/shard_map/own/pallas_call | solution.py:209
  45.7 1.0 all-to-all-done
  47.3 3.2 %collective-permute-start.6 = (bf16[512,512]{1,0:T(8,128)(2,1)S(1)}, bf16[512,512]{1,0:T(8,128)(2,1)S(1)}, u32[]{:S(2)}, u32[]{:S(2)}) collective-permute-start(bf16[512,512]{1,0:T(8,128)(2,1)S(1)} %collective-permute-done.refs_5_), channel_id=1, source_target_pairs={{0,8},{8,16},{16,24},{24,0},{1,9},{9,17},{17,25},{25,1},{2,10},{10... | collective-permute-start | bytes 1572872 | tf_op jit(solution)/shard_map/ppermute | solution.py:207
  50.5 2.4 collective-permute-start.4
  52.9 3.9 %collective-permute-start.2 = (bf16[512,512]{1,0:T(8,128)(2,1)S(1)}, bf16[512,512]{1,0:T(8,128)(2,1)}, u32[]{:S(2)}, u32[]{:S(2)}) collective-permute-start(bf16[512,512]{1,0:T(8,128)(2,1)S(1)} %collective-permute-done.refs_5_), channel_id=1, source_target_pairs={{0,24},{8,0},{16,8},{24,16},{1,25},{9,1},{17,9},{25,17},{2,26},{10... | collective-permute-start | bytes 1572872 | tf_op jit(solution)/shard_map/ppermute | solution.py:207
  57.7 1.3 pad_add_fusion.refs_0_
  59.0 3.0 %collective-permute-done.1.refs_6_ = bf16[512,512]{1,0:T(8,128)(2,1)S(1)} collective-permute-done((bf16[512,512]{1,0:T(8,128)(2,1)S(1)}, bf16[512,512]{1,0:T(8,128)(2,1)S(1)}, u32[]{:S(2)}, u32[]{:S(2)}) %collective-permute-start.1) | collective-permute-done | bytes 524320 | tf_op jit(solution)/shard_map/ppermute | solution.py:207
  62.8 8.1 %collective-permute-done.4.refs_9_ = bf16[512,512]{1,0:T(8,128)(2,1)S(1)} collective-permute-done((bf16[512,512]{1,0:T(8,128)(2,1)S(1)}, bf16[512,512]{1,0:T(8,128)(2,1)S(1)}, u32[]{:S(2)}, u32[]{:S(2)}) %collective-permute-start.4) | collective-permute-done | bytes 524320 | tf_op jit(solution)/shard_map/ppermute | solution.py:207
  71.7 11.4 %collective-permute-done.2.refs_7_ = bf16[512,512]{1,0:T(8,128)(2,1)} collective-permute-done((bf16[512,512]{1,0:T(8,128)(2,1)S(1)}, bf16[512,512]{1,0:T(8,128)(2,1)}, u32[]{:S(2)}, u32[]{:S(2)}) %collective-permute-start.2) | collective-permute-done | bytes 524320 | tf_op jit(solution)/shard_map/ppermute | solution.py:207
  83.1 30.9 %all-gather.3.cloned.1.call-done = bf16[4224,512]{1,0:T(8,128)(2,1)} async-done(((bf16[528,512]{1,0:T(8,128)(2,1)}), bf16[4224,512]{1,0:T(8,128)(2,1)}) %all-gather.3.cloned.1.call-update) | async-done | bytes 4325392 | tf_op jit(solution)/shard_map/all_gather | solution.py:197
  114.0 22.7 %remote.1 = (bf16[8,256,512]{2,1,0:T(8,128)(2,1)}, f32[512,512]{1,0:T(8,128)}, bf16[512,512]{1,0:T(8,128)(2,1)}, bf16[512,512]{1,0:T(8,128)(2,1)}, bf16[512,512]...) custom-call(s32[129]{0:T(256)} %pad_add_fusion.refs_0_, ...), custom_call_target="tpu_custom_call" | custom-call | tf_op jit(solution)/shard_map/remote/pallas_call | solution.py:221
  136.7 7.1 %collective-permute-start.7 = (bf16[512,512]{1,0:T(8,128)(2,1)}, bf16[512,512]{1,0:T(8,128)(2,1)S(1)}, u32[]{:S(2)}, u32[]{:S(2)}) collective-permute-start(bf16[512,512]{1,0:T(8,128)(2,1)} %get-tuple-element.56), channel_id=1, source_target_pairs={{0,32},{8,40},{16,48},{24,56},{32,0},{40,8},{48,16},{56,24},{1,33}... | collective-permute-start | bytes 1572872 | tf_op jit(solution)/shard_map/ppermute | solution.py:249
  143.9 3.1 %collective-permute-start.8 = (bf16[512,512]{1,0:T(8,128)(2,1)}, bf16[512,512]{1,0:T(8,128)(2,1)S(1)}, u32[]{:S(2)}, u32[]{:S(2)}) collective-permute-start(bf16[512,512]{1,0:T(8,128)(2,1)} %get-tuple-element.57), channel_id=1, source_target_pairs={{0,8},{8,16},{16,24},{24,0},{32,40},{40,48},{48,56},{56,32},{1,9},... | collective-permute-start | bytes 1572872 | tf_op jit(solution)/shard_map/ppermute | solution.py:249
  147.0 3.6 %collective-permute-start.9 = (bf16[512,512]{1,0:T(8,128)(2,1)}, bf16[512,512]{1,0:T(8,128)(2,1)S(1)}, u32[]{:S(2)}, u32[]{:S(2)}) collective-permute-start(bf16[512,512]{1,0:T(8,128)(2,1)} %get-tuple-element.58), channel_id=1, source_target_pairs={{0,40},{8,48},{16,56},{24,32},{32,8},{40,16},{48,24},{56,0},{1,41}... | collective-permute-start | bytes 1572872 | tf_op jit(solution)/shard_map/ppermute | solution.py:249
  150.6 2.6 %collective-permute-start.10 = (bf16[512,512]{1,0:T(8,128)(2,1)}, bf16[512,512]{1,0:T(8,128)(2,1)S(1)}, u32[]{:S(2)}, u32[]{:S(2)}) collective-permute-start(bf16[512,512]{1,0:T(8,128)(2,1)} %get-tuple-element.59), channel_id=1, source_target_pairs={{0,16},{8,24},{16,0},{24,8},{32,48},{40,56},{48,32},{56,40},{1,17}... | collective-permute-start | bytes 1572872 | tf_op jit(solution)/shard_map/ppermute | solution.py:249
  153.2 5.4 %collective-permute-start.11 = (bf16[512,512]{1,0:T(8,128)(2,1)}, bf16[512,512]{1,0:T(8,128)(2,1)S(1)}, u32[]{:S(2)}, u32[]{:S(2)}) collective-permute-start(bf16[512,512]{1,0:T(8,128)(2,1)} %get-tuple-element.60), channel_id=1, source_target_pairs={{0,48},{8,56},{16,32},{24,40},{32,16},{40,24},{48,0},{56,8},{1,49}... | collective-permute-start | bytes 1572872 | tf_op jit(solution)/shard_map/ppermute | solution.py:249
  159.0 4.3 %collective-permute-start.12 = (bf16[512,512]{1,0:T(8,128)(2,1)}, bf16[512,512]{1,0:T(8,128)(2,1)S(1)}, u32[]{:S(2)}, u32[]{:S(2)}) collective-permute-start(bf16[512,512]{1,0:T(8,128)(2,1)} %get-tuple-element.61), channel_id=1, source_target_pairs={{0,24},{8,0},{16,8},{24,16},{32,56},{40,32},{48,40},{56,48},{1,25}... | collective-permute-start | bytes 1572872 | tf_op jit(solution)/shard_map/ppermute | solution.py:249
  163.4 8.9 %collective-permute-start.13 = (bf16[512,512]{1,0:T(8,128)(2,1)}, bf16[512,512]{1,0:T(8,128)(2,1)S(1)}, u32[]{:S(2)}, u32[]{:S(2)}) collective-permute-start(bf16[512,512]{1,0:T(8,128)(2,1)} %get-tuple-element.62), channel_id=1, source_target_pairs={{0,56},{8,32},{16,40},{24,48},{32,24},{40,0},{48,8},{56,16},{1,57}... | collective-permute-start | bytes 1572872 | tf_op jit(solution)/shard_map/ppermute | solution.py:249
  172.3 21.9 %collective-permute-done.9 = bf16[512,512]{1,0:T(8,128)(2,1)S(1)} collective-permute-done((bf16[512,512]{1,0:T(8,128)(2,1)}, bf16[512,512]{1,0:T(8,128)(2,1)S(1)}, u32[]{:S(2)}, u32[]{:S(2)}) %collective-permute-start.9) | collective-permute-done | bytes 524320 | tf_op jit(solution)/shard_map/ppermute | solution.py:249
  194.2 26.2 %collective-permute-done.11 = bf16[512,512]{1,0:T(8,128)(2,1)S(1)} collective-permute-done((bf16[512,512]{1,0:T(8,128)(2,1)}, bf16[512,512]{1,0:T(8,128)(2,1)S(1)}, u32[]{:S(2)}, u32[]{:S(2)}) %collective-permute-start.11) | collective-permute-done | bytes 524320 | tf_op jit(solution)/shard_map/ppermute | solution.py:249
  220.4 11.7 %collective-permute-done.13 = bf16[512,512]{1,0:T(8,128)(2,1)S(1)} collective-permute-done((bf16[512,512]{1,0:T(8,128)(2,1)}, bf16[512,512]{1,0:T(8,128)(2,1)S(1)}, u32[]{:S(2)}, u32[]{:S(2)}) %collective-permute-start.13) | collective-permute-done | bytes 524320 | tf_op jit(solution)/shard_map/ppermute | solution.py:249
  232.0 1.8 add_convert_fusion
  234.6 1.0 add_convert_fusion.1
  235.7 10.5 %all_to_all.24 = bf16[8,32,512]{2,1,0:T(8,128)(2,1)S(1)} all-to-all(bf16[8,32,512]{2,1,0:T(8,128)(2,1)S(1)} %bitcast.10), channel_id=1, replica_groups=mesh['j'=8,'p'=2,'x'=4,'head'=8] {'head'}, dimensions={0} | all-to-all | bytes 524288 | tf_op jit(solution)/shard_map/all_to_all | solution.py:254
  (39 shorter events, 6.1 us)
Async XLA Ops:
  7.2 106.8 %all-gather.3.cloned.1.call-start = ((), (), s32[]{:S(2)}) async-start(), calls=%async_computation.4 | async-start | bytes 4866048 | tf_op jit(solution)/shard_map/all_gather | solution.py:197
  11.3 102.7 %copy-start = (bf16[512,512]{1,0:T(8,128)(2,1)}, bf16[512,512]{1,0:T(8,128)(2,1)S(1)}, u32[]{:S(2)}) copy-start(bf16[512,512]{1,0:T(8,128)(2,1)S(1)} %constant_dynamic-update-slice_fusion.refs_4_) | copy-start | bytes 1572868
  11.3 35.9 %collective-permute-start = (bf16[512,512]{1,0:T(8,128)(2,1)S(1)}, bf16[512,512]{1,0:T(8,128)(2,1)S(1)}, u32[]{:S(2)}, u32[]{:S(2)}) collective-permute-start(bf16[512,512]{1,0:T(8,128)(2,1)S(1)} %constant_dynamic-update-slice_fusion.refs_4_), channel_id=1, source_target_pairs={{0,32},{32,0},{1,33},{33,1},{2,34},{34,2},{3,35},{35,3},{4,36},{36... | collective-permute-start | bytes 1572872 | tf_op jit(solution)/shard_map/ppermute | solution.py:203
  15.7 37.2 %collective-permute-start.5 = (bf16[512,512]{1,0:T(8,128)(2,1)S(1)}, bf16[512,512]{1,0:T(8,128)(2,1)S(1)}, u32[]{:S(2)}, u32[]{:S(2)}) collective-permute-start(bf16[512,512]{1,0:T(8,128)(2,1)S(1)} %constant_dynamic-update-slice_fusion.refs_4_), channel_id=1, source_target_pairs={{0,8},{8,16},{16,24},{24,0},{1,9},{9,17},{17,25},{25,1},{2,10},{10... | collective-permute-start | bytes 1572872 | tf_op jit(solution)/shard_map/ppermute | solution.py:207
  20.2 26.6 %all-to-all-start = ((s32[8,2,4,3]{2,1,3,0:T(2,128)}), s32[8,2,4,3]{2,1,3,0:T(2,128)S(1)}, u32[]{:S(2)}, u32[]{:S(2)}) async-start(s32[8,2,4,3]{2,1,3,0:T(2,128)} %broadcast_in_dim.12), calls=%async_computation | async-start | bytes 49152 | tf_op jit(solution)/shard_map/all_to_all | solution.py:199
  34.1 200.6 %reduce-scatter.2.cloned.1.call-start = ((), (), s32[]{:S(2)}) async-start(), calls=%async_computation.3 | async-start | bytes 2359296 | tf_op jit(solution)/shard_map/reduce_scatter | solution.py:240
  34.1 24.9 %collective-permute-start.3 = (bf16[512,512]{1,0:T(8,128)(2,1)S(1)}, bf16[512,512]{1,0:T(8,128)(2,1)S(1)}, u32[]{:S(2)}, u32[]{:S(2)}) collective-permute-start(bf16[512,512]{1,0:T(8,128)(2,1)S(1)} %constant_dynamic-update-slice_fusion.refs_4_), channel_id=1, source_target_pairs={{0,16},{8,24},{16,0},{24,8},{1,17},{9,25},{17,1},{25,9},{2,18},{10... | collective-permute-start | bytes 1572872 | tf_op jit(solution)/shard_map/ppermute | solution.py:207
  38.5 23.6 %collective-permute-start.1 = (bf16[512,512]{1,0:T(8,128)(2,1)S(1)}, bf16[512,512]{1,0:T(8,128)(2,1)S(1)}, u32[]{:S(2)}, u32[]{:S(2)}) collective-permute-start(bf16[512,512]{1,0:T(8,128)(2,1)S(1)} %constant_dynamic-update-slice_fusion.refs_4_), channel_id=1, source_target_pairs={{0,24},{8,0},{16,8},{24,16},{1,25},{9,1},{17,9},{25,17},{2,26},{10... | collective-permute-start | bytes 1572872 | tf_op jit(solution)/shard_map/ppermute | solution.py:207
  47.3 66.7 %copy-start.1 = (bf16[512,512]{1,0:T(8,128)(2,1)}, bf16[512,512]{1,0:T(8,128)(2,1)S(1)}, u32[]{:S(2)}) copy-start(bf16[512,512]{1,0:T(8,128)(2,1)S(1)} %collective-permute-done.refs_5_) | copy-start | bytes 1572868
  47.3 15.5 %collective-permute-start.6 = (bf16[512,512]{1,0:T(8,128)(2,1)S(1)}, bf16[512,512]{1,0:T(8,128)(2,1)S(1)}, u32[]{:S(2)}, u32[]{:S(2)}) collective-permute-start(bf16[512,512]{1,0:T(8,128)(2,1)S(1)} %collective-permute-done.refs_5_), channel_id=1, source_target_pairs={{0,8},{8,16},{16,24},{24,0},{1,9},{9,17},{17,25},{25,1},{2,10},{10... | collective-permute-start | bytes 1572872 | tf_op jit(solution)/shard_map/ppermute | solution.py:207
  50.5 20.4 %collective-permute-start.4 = (bf16[512,512]{1,0:T(8,128)(2,1)S(1)}, bf16[512,512]{1,0:T(8,128)(2,1)S(1)}, u32[]{:S(2)}, u32[]{:S(2)}) collective-permute-start(bf16[512,512]{1,0:T(8,128)(2,1)S(1)} %collective-permute-done.refs_5_), channel_id=1, source_target_pairs={{0,16},{8,24},{16,0},{24,8},{1,17},{9,25},{17,1},{25,9},{2,18},{10... | collective-permute-start | bytes 1572872 | tf_op jit(solution)/shard_map/ppermute | solution.py:207
  52.9 61.1 %copy-start.2 = (bf16[512,512]{1,0:T(8,128)(2,1)}, bf16[512,512]{1,0:T(8,128)(2,1)S(1)}, u32[]{:S(2)}) copy-start(bf16[512,512]{1,0:T(8,128)(2,1)S(1)} %collective-permute-done.5.refs_10_) | copy-start | bytes 1572868
  52.9 30.2 %collective-permute-start.2 = (bf16[512,512]{1,0:T(8,128)(2,1)S(1)}, bf16[512,512]{1,0:T(8,128)(2,1)}, u32[]{:S(2)}, u32[]{:S(2)}) collective-permute-start(bf16[512,512]{1,0:T(8,128)(2,1)S(1)} %collective-permute-done.refs_5_), channel_id=1, source_target_pairs={{0,24},{8,0},{16,8},{24,16},{1,25},{9,1},{17,9},{25,17},{2,26},{10... | collective-permute-start | bytes 1572872 | tf_op jit(solution)/shard_map/ppermute | solution.py:207
  59.0 55.0 %copy-start.3 = (bf16[512,512]{1,0:T(8,128)(2,1)}, bf16[512,512]{1,0:T(8,128)(2,1)S(1)}, u32[]{:S(2)}) copy-start(bf16[512,512]{1,0:T(8,128)(2,1)S(1)} %collective-permute-done.3.refs_8_) | copy-start | bytes 1572868
  62.1 52.0 %copy-start.4 = (bf16[512,512]{1,0:T(8,128)(2,1)}, bf16[512,512]{1,0:T(8,128)(2,1)S(1)}, u32[]{:S(2)}) copy-start(bf16[512,512]{1,0:T(8,128)(2,1)S(1)} %collective-permute-done.1.refs_6_) | copy-start | bytes 1572868
  62.8 51.2 %copy-start.5 = (bf16[512,512]{1,0:T(8,128)(2,1)}, bf16[512,512]{1,0:T(8,128)(2,1)S(1)}, u32[]{:S(2)}) copy-start(bf16[512,512]{1,0:T(8,128)(2,1)S(1)} %collective-permute-done.6.refs_11_) | copy-start | bytes 1572868
  70.9 0.8 copy-start.6
  136.7 97.9 %copy-start.7 = (f32[256,512]{1,0:T(8,128)S(1)}, f32[256,512]{1,0:T(8,128)}, u32[]{:S(2)}) copy-start(f32[256,512]{1,0:T(8,128)} %get-tuple-element.64) | copy-start | bytes 1572868
  136.7 22.3 %collective-permute-start.7 = (bf16[512,512]{1,0:T(8,128)(2,1)}, bf16[512,512]{1,0:T(8,128)(2,1)S(1)}, u32[]{:S(2)}, u32[]{:S(2)}) collective-permute-start(bf16[512,512]{1,0:T(8,128)(2,1)} %get-tuple-element.56), channel_id=1, source_target_pairs={{0,32},{8,40},{16,48},{24,56},{32,0},{40,8},{48,16},{56,24},{1,33}... | collective-permute-start | bytes 1572872 | tf_op jit(solution)/shard_map/ppermute | solution.py:249
  143.9 19.5 %collective-permute-start.8 = (bf16[512,512]{1,0:T(8,128)(2,1)}, bf16[512,512]{1,0:T(8,128)(2,1)S(1)}, u32[]{:S(2)}, u32[]{:S(2)}) collective-permute-start(bf16[512,512]{1,0:T(8,128)(2,1)} %get-tuple-element.57), channel_id=1, source_target_pairs={{0,8},{8,16},{16,24},{24,0},{32,40},{40,48},{48,56},{56,32},{1,9},... | collective-permute-start | bytes 1572872 | tf_op jit(solution)/shard_map/ppermute | solution.py:249
  147.0 47.2 %collective-permute-start.9 = (bf16[512,512]{1,0:T(8,128)(2,1)}, bf16[512,512]{1,0:T(8,128)(2,1)S(1)}, u32[]{:S(2)}, u32[]{:S(2)}) collective-permute-start(bf16[512,512]{1,0:T(8,128)(2,1)} %get-tuple-element.58), channel_id=1, source_target_pairs={{0,40},{8,48},{16,56},{24,32},{32,8},{40,16},{48,24},{56,0},{1,41}... | collective-permute-start | bytes 1572872 | tf_op jit(solution)/shard_map/ppermute | solution.py:249
  150.6 43.5 %collective-permute-start.10 = (bf16[512,512]{1,0:T(8,128)(2,1)}, bf16[512,512]{1,0:T(8,128)(2,1)S(1)}, u32[]{:S(2)}, u32[]{:S(2)}) collective-permute-start(bf16[512,512]{1,0:T(8,128)(2,1)} %get-tuple-element.59), channel_id=1, source_target_pairs={{0,16},{8,24},{16,0},{24,8},{32,48},{40,56},{48,32},{56,40},{1,17}... | collective-permute-start | bytes 1572872 | tf_op jit(solution)/shard_map/ppermute | solution.py:249
  153.2 67.1 %collective-permute-start.11 = (bf16[512,512]{1,0:T(8,128)(2,1)}, bf16[512,512]{1,0:T(8,128)(2,1)S(1)}, u32[]{:S(2)}, u32[]{:S(2)}) collective-permute-start(bf16[512,512]{1,0:T(8,128)(2,1)} %get-tuple-element.60), channel_id=1, source_target_pairs={{0,48},{8,56},{16,32},{24,40},{32,16},{40,24},{48,0},{56,8},{1,49}... | collective-permute-start | bytes 1572872 | tf_op jit(solution)/shard_map/ppermute | solution.py:249
  159.0 61.3 %collective-permute-start.12 = (bf16[512,512]{1,0:T(8,128)(2,1)}, bf16[512,512]{1,0:T(8,128)(2,1)S(1)}, u32[]{:S(2)}, u32[]{:S(2)}) collective-permute-start(bf16[512,512]{1,0:T(8,128)(2,1)} %get-tuple-element.61), channel_id=1, source_target_pairs={{0,24},{8,0},{16,8},{24,16},{32,56},{40,32},{48,40},{56,48},{1,25}... | collective-permute-start | bytes 1572872 | tf_op jit(solution)/shard_map/ppermute | solution.py:249
  163.4 68.7 %collective-permute-start.13 = (bf16[512,512]{1,0:T(8,128)(2,1)}, bf16[512,512]{1,0:T(8,128)(2,1)S(1)}, u32[]{:S(2)}, u32[]{:S(2)}) collective-permute-start(bf16[512,512]{1,0:T(8,128)(2,1)} %get-tuple-element.62), channel_id=1, source_target_pairs={{0,56},{8,32},{16,40},{24,48},{32,24},{40,0},{48,8},{56,16},{1,57}... | collective-permute-start | bytes 1572872 | tf_op jit(solution)/shard_map/ppermute | solution.py:249
Sparse Core Ops, SparseCore 0:
  10.1 103.8 all-gather.2
  136.9 79.4 reduce-scatter.1

commit v3 on v2

--- a/solution.py
+++ b/solution.py
@@ -16,6 +16,7 @@
 UNROLL = 4
 F32 = jnp.float32
 BF16 = jnp.bfloat16
+PARAMS = pltpu.CompilerParams(vmem_limit_bytes=56 * 1024 * 1024)
 
 
 def mm(left, right, left_dim, right_dim):
@@ -99,12 +100,16 @@
             dv_ref[at, cols] = grad_v
 
 
+def low_bits(value, size):
+    return value & (size - 1), value >> (size.bit_length() - 1)
+
+
 def remote_kernel(blocks, heads, factor, owners, *refs):
     slots_ref, packs_ref, own_k_ref, own_v_ref = refs[:4]
     kv_refs = refs[4 : 4 + owners]
-    dq_ref, near_ref = refs[4 + owners : 6 + owners]
-    far_refs = refs[6 + owners : 5 + 2 * owners]
-    acc_ref, line_ref, pack_ref, kv_ref, sems = refs[5 + 2 * owners :]
+    dq_out, near_out = refs[4 + owners : 6 + owners]
+    far_outs = refs[6 + owners : 5 + owners + owners // PAIR]
+    dq_ref, acc_ref, far_ref, line_ref, pack_ref, kv_ref, sems = refs[5 + owners + owners // PAIR :]
     rows = blocks * BLOCK
     span = blocks * owners
     loads = [pltpu.make_async_copy(packs_ref, pack_ref, sems.at[owners])]
@@ -124,13 +129,12 @@
         done = []
         for u in range(UNROLL):
             slot = step * UNROLL + u
-            code = slots_ref[1 + jnp.minimum(slot, count - 1)]
             live = slot < count
-            kb = code % blocks
-            kx = code // blocks % owners
-            h = code // span % heads
-            b = code // (span * heads) % blocks
-            zq = code // (span * heads * blocks)
+            code = slots_ref[1 + jnp.where(live, slot, count - 1)]
+            kb, rest = low_bits(code, blocks)
+            kx, rest = low_bits(rest, owners)
+            h, rest = low_bits(rest, heads)
+            b, zq = low_bits(rest, blocks)
             cols = pl.ds(pl.multiple_of(h * BLOCK, BLOCK), BLOCK)
             q_at = pl.ds(pl.multiple_of(b * BLOCK, BLOCK), BLOCK)
             g_at = pl.ds(pl.multiple_of(rows + b * BLOCK, BLOCK), BLOCK)
@@ -147,21 +151,36 @@
                 factor,
                 live,
             )
-            done.append((slot, code, zq, q_at, cols, kx, k_at, v_at, terms))
-        for slot, code, zq, q_at, cols, kx, k_at, v_at, (grad_q, grad_k, grad_v) in done:
+            before = slots_ref[jnp.where(live, slot, count)]
+            shift = span.bit_length() - 1
+            same = (slot > 0) & ((before >> shift) == (code >> shift))
+            done.append((same, zq, q_at, cols, kx, k_at, v_at, terms))
+        for same, zq, q_at, cols, kx, k_at, v_at, (grad_q, grad_k, grad_v) in done:
             acc_ref[kx, k_at, cols] += grad_k
             acc_ref[kx, v_at, cols] += grad_v
-            before = slots_ref[1 + jnp.clip(slot - 1, 0, count - 1)]
-            same = (slot > 0) & (before // span == code // span)
             total = jnp.where(same, line_ref[...], 0.0) + grad_q
             line_ref[...] = total
             dq_ref[zq, q_at, cols] = total.astype(BF16)
         return carry
 
     lax.fori_loop(0, (count + UNROLL - 1) // UNROLL, turn, 0)
-    near_ref[...] = acc_ref[0]
-    for at in range(1, owners):
-        far_refs[at - 1][...] = acc_ref[at].astype(BF16)
+    stores = [
+        pltpu.make_async_copy(dq_ref, dq_out, sems.at[0]),
+        pltpu.make_async_copy(acc_ref.at[pl.ds(0, PAIR)], near_out, sems.at[1]),
+    ]
+    for store in stores:
+        store.start()
+    for at in range(PAIR, owners):
+        far_ref[at - PAIR] = acc_ref[at].astype(BF16)
+        if at % PAIR == PAIR - 1:
+            first = at - 2 * PAIR + 1
+            turned = pltpu.make_async_copy(
+                far_ref.at[pl.ds(first, PAIR)], far_outs[first // PAIR], sems.at[at]
+            )
+            turned.start()
+            stores.append(turned)
+    for store in stores:
+        store.wait()
 
 
 def slot_codes(table, j, p, x, owners):
@@ -181,17 +200,42 @@
     return jnp.concatenate([jnp.sum(hit.astype(jnp.int32))[None], codes])
 
 
+def remote_call(codes, packs, own_k, own_v, kvs, blocks, heads, factor, rows, width, ring, owners):
+    anywhere = pl.BlockSpec(memory_space=pl.ANY)
+    vmem = pl.BlockSpec(memory_space=pltpu.VMEM)
+    return pl.pallas_call(
+        functools.partial(remote_kernel, blocks, heads, factor, owners),
+        in_specs=[pl.BlockSpec(memory_space=pltpu.SMEM), anywhere, vmem, vmem] + [anywhere] * owners,
+        out_specs=(anywhere,) * (X_SIZE + 1),
+        out_shape=(
+            jax.ShapeDtypeStruct((ring, rows, width), BF16),
+            jax.ShapeDtypeStruct((PAIR, 2 * rows, width), F32),
+        )
+        + (jax.ShapeDtypeStruct((PAIR, 2 * rows, width), BF16),) * (X_SIZE - 1),
+        scratch_shapes=[
+            pltpu.VMEM((ring, rows, width), BF16),
+            pltpu.VMEM((owners, 2 * rows, width), F32),
+            pltpu.VMEM((owners - PAIR, 2 * rows, width), BF16),
+            pltpu.VMEM((BLOCK, BLOCK), F32),
+            pltpu.VMEM((ring, 2 * rows + STAT_ROWS, width), BF16),
+            pltpu.VMEM((owners, 2 * rows, width), BF16),
+            pltpu.SemaphoreType.DMA((owners + 1,)),
+        ],
+        compiler_params=PARAMS,
+        name="remote",
+    )(codes, packs, own_k, own_v, *kvs)
+
+
 def shards(queries, keys, values, out_grad, outputs, log_norms, selected):
     blocks, heads, top_count = selected.shape
     rows, width = queries.shape
     factor = (width // heads) ** (-0.5)
     ring = lax.axis_size("j")
     owners = lax.axis_size("p") * lax.axis_size("x")
-    params = pltpu.CompilerParams(vmem_limit_bytes=56 * 1024 * 1024)
     pack = pl.pallas_call(
         functools.partial(pack_kernel, blocks, heads),
         out_shape=jax.ShapeDtypeStruct((2 * rows + STAT_ROWS, width), BF16),
-        compiler_params=params,
+        compiler_params=PARAMS,
         name="pack",
     )(queries, out_grad, outputs, log_norms.T)
     packs = lax.all_gather(pack, "j")
@@ -209,47 +253,25 @@
     own_q, own_k, own_v = pl.pallas_call(
         functools.partial(own_kernel, blocks, heads, factor),
         out_shape=(own, own, own),
-        compiler_params=params,
+        compiler_params=PARAMS,
         name="own",
     )(pack, keys, values)
     codes = slot_codes(table, lax.axis_index("j"), lax.axis_index("p"), lax.axis_index("x"), owners)
     packs, kvs, codes, own_q, own_k, own_v = lax.optimization_barrier(
         (packs, kvs, codes, own_q, own_k, own_v)
     )
-    anywhere = pl.BlockSpec(memory_space=pl.ANY)
-    vmem = pl.BlockSpec(memory_space=pltpu.VMEM)
-    part_q, near, *far = pl.pallas_call(
-        functools.partial(remote_kernel, blocks, heads, factor, owners),
-        in_specs=[pl.BlockSpec(memory_space=pltpu.SMEM), anywhere, vmem, vmem] + [anywhere] * owners,
-        out_specs=(vmem,) * (owners + 1),
-        out_shape=(
-            jax.ShapeDtypeStruct((ring, rows, width), BF16),
-            jax.ShapeDtypeStruct((2 * rows, width), F32),
-        )
-        + (jax.ShapeDtypeStruct((2 * rows, width), BF16),) * (owners - 1),
-        scratch_shapes=[
-            pltpu.VMEM((owners, 2 * rows, width), F32),
-            pltpu.VMEM((BLOCK, BLOCK), F32),
-            pltpu.VMEM((ring, 2 * rows + STAT_ROWS, width), BF16),
-            pltpu.VMEM((owners, 2 * rows, width), BF16),
-            pltpu.SemaphoreType.DMA((owners + 1,)),
-        ],
-        compiler_params=params,
-        name="remote",
-    )(codes, packs, own_k, own_v, *kvs)
+    part_q, near, *far = remote_call(
+        codes, packs, own_k, own_v, kvs, blocks, heads, factor, rows, width, ring, owners
+    )
     sum_q = lax.psum_scatter(part_q, "j", scatter_dimension=0)
     sum_kv = near
-    for at in range(1, owners):
-        shift, other = at // PAIR, at % PAIR
-        pairs = [
-            (p * X_SIZE + x, (p + other) % PAIR * X_SIZE + (x + shift) % X_SIZE)
-            for p in range(PAIR)
-            for x in range(X_SIZE)
-        ]
-        sum_kv = sum_kv + lax.ppermute(far[at - 1], ("p", "x"), pairs).astype(F32)
-    final_k = sum_kv[:rows].astype(BF16)
-    final_v = sum_kv[rows:].astype(BF16)
-    sum_q, final_k, final_v = lax.optimization_barrier((sum_q, final_k, final_v))
+    for shift in range(1, X_SIZE):
+        ahead = [(i, (i + shift) % X_SIZE) for i in range(X_SIZE)]
+        sum_kv = sum_kv + lax.ppermute(far[shift - 1], "x", ahead).astype(F32)
+    crossed = lax.ppermute(sum_kv[1].astype(BF16), "p", [(i, (i + 1) % PAIR) for i in range(PAIR)])
+    final_kv = sum_kv[0] + crossed.astype(F32)
+    final_k = final_kv[:rows].astype(BF16)
+    final_v = final_kv[rows:].astype(BF16)
     final_q = (sum_q.astype(F32) + own_q).astype(BF16)
     spread_q = lax.all_to_all(final_q, "head", split_axis=0, concat_axis=1, tiled=True)
     return spread_q, final_k, final_v

time: 256 us -> 235 us (0.918)
  blocking collectives: 10.5 us -> 0 us
  starting transfers between devices: 73.4 us -> 63.7 us
  waiting for transfers between devices: 115 us -> 118 us
    ppermute x7 -> x4, starting transfers between devices: 35 us -> 18.6 us  [the longest x3 13 us: shards(): sum_kv = sum_kv + lax.ppermute(far[shift - 1], 'x', ahead).astype(F32)]
    all_to_all x1 -> x0, blocking collectives: 10.5 us -> none  [shards(): lax.all_to_all(final_q, 'head', split_axis=0, concat_axis=1, tiled=True)]
    ppermute x7 -> x4, waiting for transfers between devices: 60.2 us -> 52.1 us  [the longest x3 41.1 us: shards(): sum_kv = sum_kv + lax.ppermute(far[shift - 1], 'x', ahead).astype(F32)]
    all_to_all x0 -> x1, starting transfers between devices: none -> 5.94 us  [shards(): lax.all_to_all(final_q, 'head', split_axis=0, concat_axis=1, tiled=True)]
    all_to_all x0 -> x1, waiting for transfers between devices: none -> 5.68 us  [shards(): lax.all_to_all(final_q, 'head', split_axis=0, concat_axis=1, tiled=True)]
    all_gather x1, waiting for transfers between devices: 30.9 us -> 36.2 us  [shards(): packs = lax.all_gather(pack, 'j')]
  transfers between devices with their start and end apart: 17 -> 15, of which waited for: 10 -> 9; matrix products, arithmetic and copies ran while one was open for 3% -> 3% of each run, Pallas kernels for 2% -> 2%
where the time goes in v3:
time: 235 us; the launch traced here: 233 us
  waiting for transfers between devices  118 us (50%)
  starting transfers between devices  63.7 us (27%)
  Pallas kernels  28.1 us (12%)
  between operations  14.3 us (6%)
  other arithmetic  4.92 us (2%)
  local copies, waits for them, and re-layouts  4.41 us (2%)
    ppermute x3, waiting for transfers between devices, shards(): sum_kv = sum_kv + lax.ppermute(far[shift - 1], 'x', ahead).astype(F32)  41.1 us
    all_gather x1, waiting for transfers between devices, shards(): packs = lax.all_gather(pack, 'j')  36.2 us
    ppermute x6, waiting for transfers between devices, shards(): kvs += [lax.ppermute(both, 'x', back), lax.ppermute(swapped, 'x', back)]  23.5 us
    pallas_call x1, Pallas kernels, remote_call(): pl.pallas_call(functools.partial(remote_kernel, blocks, heads, factor, ow...  21.7 us
    ppermute x6, starting transfers between devices, shards(): kvs += [lax.ppermute(both, 'x', back), lax.ppermute(swapped, 'x', back)]  20.8 us
    all_to_all x1, starting transfers between devices, shards(): lax.all_to_all(jnp.broadcast_to(selected[None], (ring, *selected.shape)),...  13.9 us
    ppermute x3, starting transfers between devices, shards(): sum_kv = sum_kv + lax.ppermute(far[shift - 1], 'x', ahead).astype(F32)  13 us
    ppermute x1, waiting for transfers between devices, shards(): lax.ppermute(sum_kv[1].astype(BF16), 'p', [(i, (i + 1) % PAIR) for i in r...  11 us
  transfers between devices with their start and end apart: 15, of which 9 were waited for; matrix products, arithmetic and copies ran while one was open for 3% of the time, Pallas kernels for 2%

profile of v3, /device:TPU:1, one launch (start us, length us, event | category | flops | bytes accessed | tf_op | source)
XLA Modules:
  0.0 233.0 jit_solution(4308860137016872081)
XLA Ops:
  7.2 2.2 pack.1.pack_ref
  9.4 1.0 constant_dynamic-update-slice_fusion.1
  10.5 4.4 %collective-permute-start = (bf16[512,512]{1,0:T(8,128)(2,1)S(1)}, bf16[512,512]{1,0:T(8,128)(2,1)S(1)}, u32[]{:S(2)}, u32[]{:S(2)}) collective-permute-start(bf16[512,512]{1,0:T(8,128)(2,1)S(1)} %constant_dynamic-update-slice_fusion.refs_4_), channel_id=1, source_target_pairs={{0,32},{32,0},{1,33},{33,1},{2,34},{34,2},{3,35},{35,3},{4,36},{36... | collective-permute-start | bytes 1572872 | tf_op jit(solution)/shard_map/ppermute | solution.py:247
  14.8 3.1 %collective-permute-start.5 = (bf16[512,512]{1,0:T(8,128)(2,1)S(1)}, bf16[512,512]{1,0:T(8,128)(2,1)S(1)}, u32[]{:S(2)}, u32[]{:S(2)}) collective-permute-start(bf16[512,512]{1,0:T(8,128)(2,1)S(1)} %constant_dynamic-update-slice_fusion.refs_4_), channel_id=1, source_target_pairs={{0,8},{8,16},{16,24},{24,0},{1,9},{9,17},{17,25},{25,1},{2,10},{10... | collective-permute-start | bytes 1572872 | tf_op jit(solution)/shard_map/ppermute | solution.py:251
  18.6 13.9 %all-to-all-start = ((s32[8,2,4,3]{2,1,3,0:T(2,128)}), s32[8,2,4,3]{2,1,3,0:T(2,128)S(1)}, u32[]{:S(2)}, u32[]{:S(2)}) async-start(s32[8,2,4,3]{2,1,3,0:T(2,128)} %broadcast_in_dim.12), calls=%async_computation | async-start | bytes 49152 | tf_op jit(solution)/shard_map/all_to_all | solution.py:243
  32.5 4.4 %collective-permute-start.3 = (bf16[512,512]{1,0:T(8,128)(2,1)S(1)}, bf16[512,512]{1,0:T(8,128)(2,1)S(1)}, u32[]{:S(2)}, u32[]{:S(2)}) collective-permute-start(bf16[512,512]{1,0:T(8,128)(2,1)S(1)} %constant_dynamic-update-slice_fusion.refs_4_), channel_id=1, source_target_pairs={{0,16},{8,24},{16,0},{24,8},{1,17},{9,25},{17,1},{25,9},{2,18},{10... | collective-permute-start | bytes 1572872 | tf_op jit(solution)/shard_map/ppermute | solution.py:251
  36.9 3.1 %collective-permute-start.1 = (bf16[512,512]{1,0:T(8,128)(2,1)S(1)}, bf16[512,512]{1,0:T(8,128)(2,1)S(1)}, u32[]{:S(2)}, u32[]{:S(2)}) collective-permute-start(bf16[512,512]{1,0:T(8,128)(2,1)S(1)} %constant_dynamic-update-slice_fusion.refs_4_), channel_id=1, source_target_pairs={{0,24},{8,0},{16,8},{24,16},{1,25},{9,1},{17,9},{25,17},{2,26},{10... | collective-permute-start | bytes 1572872 | tf_op jit(solution)/shard_map/ppermute | solution.py:251
  40.0 4.2 %own.1 = (f32[256,512]{1,0:T(8,128)}, f32[256,512]{1,0:T(8,128)}, f32[256,512]{1,0:T(8,128)}) custom-call(bf16[528,512]{1,0:T(8,128)(2,1)} %pack.1.pack_ref, bf16[256,512]{1,0:T(8,128)(2,1)} %k_ref, bf16[256,512]{1,0:T(8,128)(2,1)} %v_ref), custom_call_target="tpu_custom_call" | custom-call | tf_op jit(solution)/shard_map/own/pallas_call | solution.py:253
  44.7 3.2 %collective-permute-start.6 = (bf16[512,512]{1,0:T(8,128)(2,1)S(1)}, bf16[512,512]{1,0:T(8,128)(2,1)S(1)}, u32[]{:S(2)}, u32[]{:S(2)}) collective-permute-start(bf16[512,512]{1,0:T(8,128)(2,1)S(1)} %collective-permute-done.refs_5_), channel_id=1, source_target_pairs={{0,8},{8,16},{16,24},{24,0},{1,9},{9,17},{17,25},{25,1},{2,10},{10... | collective-permute-start | bytes 1572872 | tf_op jit(solution)/shard_map/ppermute | solution.py:251
  47.9 3.2 %collective-permute-start.4 = (bf16[512,512]{1,0:T(8,128)(2,1)S(1)}, bf16[512,512]{1,0:T(8,128)(2,1)S(1)}, u32[]{:S(2)}, u32[]{:S(2)}) collective-permute-start(bf16[512,512]{1,0:T(8,128)(2,1)S(1)} %collective-permute-done.refs_5_), channel_id=1, source_target_pairs={{0,16},{8,24},{16,0},{24,8},{1,17},{9,25},{17,1},{25,9},{2,18},{10... | collective-permute-start | bytes 1572872 | tf_op jit(solution)/shard_map/ppermute | solution.py:251
  51.1 3.9 %collective-permute-start.2 = (bf16[512,512]{1,0:T(8,128)(2,1)S(1)}, bf16[512,512]{1,0:T(8,128)(2,1)}, u32[]{:S(2)}, u32[]{:S(2)}) collective-permute-start(bf16[512,512]{1,0:T(8,128)(2,1)S(1)} %collective-permute-done.refs_5_), channel_id=1, source_target_pairs={{0,24},{8,0},{16,8},{24,16},{1,25},{9,1},{17,9},{25,17},{2,26},{10... | collective-permute-start | bytes 1572872 | tf_op jit(solution)/shard_map/ppermute | solution.py:251
  55.3 0.7 fusion.6
  56.0 1.3 pad_add_fusion.refs_0_
  57.3 3.2 %collective-permute-done.1.refs_6_ = bf16[512,512]{1,0:T(8,128)(2,1)S(1)} collective-permute-done((bf16[512,512]{1,0:T(8,128)(2,1)S(1)}, bf16[512,512]{1,0:T(8,128)(2,1)S(1)}, u32[]{:S(2)}, u32[]{:S(2)}) %collective-permute-start.1) | collective-permute-done | bytes 524320 | tf_op jit(solution)/shard_map/ppermute | solution.py:251
  60.5 9.1 %collective-permute-done.4.refs_9_ = bf16[512,512]{1,0:T(8,128)(2,1)S(1)} collective-permute-done((bf16[512,512]{1,0:T(8,128)(2,1)S(1)}, bf16[512,512]{1,0:T(8,128)(2,1)S(1)}, u32[]{:S(2)}, u32[]{:S(2)}) %collective-permute-start.4) | collective-permute-done | bytes 524320 | tf_op jit(solution)/shard_map/ppermute | solution.py:251
  69.6 0.8 copy-done.8
  70.4 11.2 %collective-permute-done.2.refs_7_ = bf16[512,512]{1,0:T(8,128)(2,1)} collective-permute-done((bf16[512,512]{1,0:T(8,128)(2,1)S(1)}, bf16[512,512]{1,0:T(8,128)(2,1)}, u32[]{:S(2)}, u32[]{:S(2)}) %collective-permute-start.2) | collective-permute-done | bytes 524320 | tf_op jit(solution)/shard_map/ppermute | solution.py:251
  81.6 36.2 %all-gather.3.cloned.1.call-done = bf16[4224,512]{1,0:T(8,128)(2,1)} async-done(((bf16[528,512]{1,0:T(8,128)(2,1)}), bf16[4224,512]{1,0:T(8,128)(2,1)}) %all-gather.3.cloned.1.call-update) | async-done | bytes 4325392 | tf_op jit(solution)/shard_map/all_gather | solution.py:241
  117.8 21.7 %remote.1 = (bf16[8,256,512]{2,1,0:T(8,128)(2,1)}, f32[2,512,512]{2,1,0:T(8,128)}, bf16[2,512,512]{2,1,0:T(8,128)(2,1)}, bf16[2,512,512]{2,1,0:T(8,128)(2,1)}, bf16[2,512,512]{2,1,0:T(8,128)(2,1)}) custom-call(s32[129]{0:T(256)} %pad_add_fusion.refs_0_, bf16[8,528,512]{2,1,0:T(8,128)(2,1)} %bitcast.18, f32[256,512]{1,0:T(8,128)} %get-tuple-element.37.refs_2_, ...), custom_call_target="tpu_custom_call" | custom-call | tf_op jit(solution)/shard_map/remote/pallas_call | solution.py:206
  139.5 6.7 %collective-permute-start.7 = (bf16[2,512,512]{2,1,0:T(8,128)(2,1)}, bf16[2,512,512]{2,1,0:T(8,128)(2,1)S(1)}, u32[]{:S(2)}, u32[]{:S(2)}) collective-permute-start(bf16[2,512,512]{2,1,0:T(8,128)(2,1)} %get-tuple-element.50), channel_id=1, source_target_pairs={{0,8},{8,16},{16,24},{24,0},{1,9},{9,17},{17,25},{25,1},{2,10},{10... | collective-permute-start | bytes 3145736 | tf_op jit(solution)/shard_map/ppermute | solution.py:270
  146.3 2.2 collective-permute-start.8
  148.5 4.0 %collective-permute-start.9 = (bf16[2,512,512]{2,1,0:T(8,128)(2,1)}, bf16[2,512,512]{2,1,0:T(8,128)(2,1)S(1)}, u32[]{:S(2)}, u32[]{:S(2)}) collective-permute-start(bf16[2,512,512]{2,1,0:T(8,128)(2,1)} %get-tuple-element.52), channel_id=1, source_target_pairs={{0,24},{8,0},{16,8},{24,16},{1,25},{9,1},{17,9},{25,17},{2,26},{10... | collective-permute-start | bytes 3145736 | tf_op jit(solution)/shard_map/ppermute | solution.py:270
  152.5 17.0 %collective-permute-done.7 = bf16[2,512,512]{2,1,0:T(8,128)(2,1)S(1)} collective-permute-done((bf16[2,512,512]{2,1,0:T(8,128)(2,1)}, bf16[2,512,512]{2,1,0:T(8,128)(2,1)S(1)}, u32[]{:S(2)}, u32[]{:S(2)}) %collective-permute-start.7) | collective-permute-done | bytes 1048608 | tf_op jit(solution)/shard_map/ppermute | solution.py:270
  169.5 22.5 %collective-permute-done.8 = bf16[2,512,512]{2,1,0:T(8,128)(2,1)S(1)} collective-permute-done((bf16[2,512,512]{2,1,0:T(8,128)(2,1)}, bf16[2,512,512]{2,1,0:T(8,128)(2,1)S(1)}, u32[]{:S(2)}, u32[]{:S(2)}) %collective-permute-start.8) | collective-permute-done | bytes 1048608 | tf_op jit(solution)/shard_map/ppermute | solution.py:270
  191.9 1.6 collective-permute-done.9
  194.3 5.6 %collective-permute-start.10 = (bf16[512,512]{1,0:T(8,128)(2,1)S(1)}, bf16[512,512]{1,0:T(8,128)(2,1)S(1)}, u32[]{:S(2)}, u32[]{:S(2)}) collective-permute-start(bf16[512,512]{1,0:T(8,128)(2,1)S(1)} %fusion.2), channel_id=1, source_target_pairs={{0,32},{32,0},{1,33},{33,1},{2,34},{34,2},{3,35},{35,3},{4,36},{36... | collective-permute-start | bytes 1572872 | tf_op jit(solution)/shard_map/ppermute | solution.py:271
  200.0 11.0 %collective-permute-done.10 = bf16[512,512]{1,0:T(8,128)(2,1)S(1)} collective-permute-done((bf16[512,512]{1,0:T(8,128)(2,1)S(1)}, bf16[512,512]{1,0:T(8,128)(2,1)S(1)}, u32[]{:S(2)}, u32[]{:S(2)}) %collective-permute-start.10) | collective-permute-done | bytes 524320 | tf_op jit(solution)/shard_map/ppermute | solution.py:271
  211.2 1.7 fusion.3
  213.0 5.9 %all-to-all-start.1 = ((bf16[8,32,512]{2,1,0:T(8,128)(2,1)}), bf16[8,32,512]{2,1,0:T(8,128)(2,1)S(1)}, u32[]{:S(2)}, u32[]{:S(2)}) async-start(bf16[8,32,512]{2,1,0:T(8,128)(2,1)} %bitcast.4), calls=%async_computation.2 | async-start | bytes 524288 | tf_op jit(solution)/shard_map/all_to_all | solution.py:276
  218.9 0.8 fusion.16
  219.7 5.7 %all-to-all-done.1 = bf16[8,32,512]{2,1,0:T(8,128)(2,1)S(1)} async-done(((bf16[8,32,512]{2,1,0:T(8,128)(2,1)}), bf16[8,32,512]{2,1,0:T(8,128)(2,1)S(1)}, u32[]{:S(2)}, u32[]{:S(2)}) %all-to-all-start.1) | async-done | bytes 262176 | tf_op jit(solution)/shard_map/all_to_all | solution.py:276
  225.4 0.7 copy.18
  (42 shorter events, 2.4 us)
Async XLA Ops:
  7.2 10.8 %copy-start.10 = (s32[2,4,3]{1,0,2:T(2,128)S(1)}, s32[2,4,3]{1,0,2:T(2,128)}, u32[]{:S(2)}) copy-start(s32[2,4,3]{1,0,2:T(2,128)} %param.13) | copy-start | bytes 292
  7.2 3.2 %copy-start.2 = (bf16[256,512]{1,0:T(8,128)(2,1)S(1)}, bf16[256,512]{1,0:T(8,128)(2,1)}, u32[]{:S(2)}) copy-start(bf16[256,512]{1,0:T(8,128)(2,1)} %v_ref) | copy-start | bytes 786436
  7.2 110.5 %all-gather.3.cloned.1.call-start = ((), (), s32[]{:S(2)}) async-start(), calls=%async_computation.4 | async-start | bytes 4866048 | tf_op jit(solution)/shard_map/all_gather | solution.py:241
  10.4 107.3 %copy-start.1 = (bf16[512,512]{1,0:T(8,128)(2,1)}, bf16[512,512]{1,0:T(8,128)(2,1)S(1)}, u32[]{:S(2)}) copy-start(bf16[512,512]{1,0:T(8,128)(2,1)S(1)} %constant_dynamic-update-slice_fusion.refs_4_) | copy-start | bytes 1572868
  10.5 34.2 %collective-permute-start = (bf16[512,512]{1,0:T(8,128)(2,1)S(1)}, bf16[512,512]{1,0:T(8,128)(2,1)S(1)}, u32[]{:S(2)}, u32[]{:S(2)}) collective-permute-start(bf16[512,512]{1,0:T(8,128)(2,1)S(1)} %constant_dynamic-update-slice_fusion.refs_4_), channel_id=1, source_target_pairs={{0,32},{32,0},{1,33},{33,1},{2,34},{34,2},{3,35},{35,3},{4,36},{36... | collective-permute-start | bytes 1572872 | tf_op jit(solution)/shard_map/ppermute | solution.py:247
  14.8 36.3 %collective-permute-start.5 = (bf16[512,512]{1,0:T(8,128)(2,1)S(1)}, bf16[512,512]{1,0:T(8,128)(2,1)S(1)}, u32[]{:S(2)}, u32[]{:S(2)}) collective-permute-start(bf16[512,512]{1,0:T(8,128)(2,1)S(1)} %constant_dynamic-update-slice_fusion.refs_4_), channel_id=1, source_target_pairs={{0,8},{8,16},{16,24},{24,0},{1,9},{9,17},{17,25},{25,1},{2,10},{10... | collective-permute-start | bytes 1572872 | tf_op jit(solution)/shard_map/ppermute | solution.py:251
  18.6 25.6 %all-to-all-start = ((s32[8,2,4,3]{2,1,3,0:T(2,128)}), s32[8,2,4,3]{2,1,3,0:T(2,128)S(1)}, u32[]{:S(2)}, u32[]{:S(2)}) async-start(s32[8,2,4,3]{2,1,3,0:T(2,128)} %broadcast_in_dim.12), calls=%async_computation | async-start | bytes 49152 | tf_op jit(solution)/shard_map/all_to_all | solution.py:243
  32.5 178.7 %reduce-scatter.2.cloned.1.call-start = ((), (), s32[]{:S(2)}) async-start(), calls=%async_computation.3 | async-start | bytes 2359296 | tf_op jit(solution)/shard_map/reduce_scatter | solution.py:266
  32.5 24.7 %collective-permute-start.3 = (bf16[512,512]{1,0:T(8,128)(2,1)S(1)}, bf16[512,512]{1,0:T(8,128)(2,1)S(1)}, u32[]{:S(2)}, u32[]{:S(2)}) collective-permute-start(bf16[512,512]{1,0:T(8,128)(2,1)S(1)} %constant_dynamic-update-slice_fusion.refs_4_), channel_id=1, source_target_pairs={{0,16},{8,24},{16,0},{24,8},{1,17},{9,25},{17,1},{25,9},{2,18},{10... | collective-permute-start | bytes 1572872 | tf_op jit(solution)/shard_map/ppermute | solution.py:251
  36.9 23.6 %collective-permute-start.1 = (bf16[512,512]{1,0:T(8,128)(2,1)S(1)}, bf16[512,512]{1,0:T(8,128)(2,1)S(1)}, u32[]{:S(2)}, u32[]{:S(2)}) collective-permute-start(bf16[512,512]{1,0:T(8,128)(2,1)S(1)} %constant_dynamic-update-slice_fusion.refs_4_), channel_id=1, source_target_pairs={{0,24},{8,0},{16,8},{24,16},{1,25},{9,1},{17,9},{25,17},{2,26},{10... | collective-permute-start | bytes 1572872 | tf_op jit(solution)/shard_map/ppermute | solution.py:251
  44.7 73.0 %copy-start.3 = (bf16[512,512]{1,0:T(8,128)(2,1)}, bf16[512,512]{1,0:T(8,128)(2,1)S(1)}, u32[]{:S(2)}) copy-start(bf16[512,512]{1,0:T(8,128)(2,1)S(1)} %collective-permute-done.refs_5_) | copy-start | bytes 1572868
  44.7 15.8 %collective-permute-start.6 = (bf16[512,512]{1,0:T(8,128)(2,1)S(1)}, bf16[512,512]{1,0:T(8,128)(2,1)S(1)}, u32[]{:S(2)}, u32[]{:S(2)}) collective-permute-start(bf16[512,512]{1,0:T(8,128)(2,1)S(1)} %collective-permute-done.refs_5_), channel_id=1, source_target_pairs={{0,8},{8,16},{16,24},{24,0},{1,9},{9,17},{17,25},{25,1},{2,10},{10... | collective-permute-start | bytes 1572872 | tf_op jit(solution)/shard_map/ppermute | solution.py:251
  47.9 21.7 %collective-permute-start.4 = (bf16[512,512]{1,0:T(8,128)(2,1)S(1)}, bf16[512,512]{1,0:T(8,128)(2,1)S(1)}, u32[]{:S(2)}, u32[]{:S(2)}) collective-permute-start(bf16[512,512]{1,0:T(8,128)(2,1)S(1)} %collective-permute-done.refs_5_), channel_id=1, source_target_pairs={{0,16},{8,24},{16,0},{24,8},{1,17},{9,25},{17,1},{25,9},{2,18},{10... | collective-permute-start | bytes 1572872 | tf_op jit(solution)/shard_map/ppermute | solution.py:251
  51.1 66.6 %copy-start.4 = (bf16[512,512]{1,0:T(8,128)(2,1)}, bf16[512,512]{1,0:T(8,128)(2,1)S(1)}, u32[]{:S(2)}) copy-start(bf16[512,512]{1,0:T(8,128)(2,1)S(1)} %collective-permute-done.5.refs_10_) | copy-start | bytes 1572868
  51.1 30.4 %collective-permute-start.2 = (bf16[512,512]{1,0:T(8,128)(2,1)S(1)}, bf16[512,512]{1,0:T(8,128)(2,1)}, u32[]{:S(2)}, u32[]{:S(2)}) collective-permute-start(bf16[512,512]{1,0:T(8,128)(2,1)S(1)} %collective-permute-done.refs_5_), channel_id=1, source_target_pairs={{0,24},{8,0},{16,8},{24,16},{1,25},{9,1},{17,9},{25,17},{2,26},{10... | collective-permute-start | bytes 1572872 | tf_op jit(solution)/shard_map/ppermute | solution.py:251
  57.3 60.5 %copy-start.5 = (bf16[512,512]{1,0:T(8,128)(2,1)}, bf16[512,512]{1,0:T(8,128)(2,1)S(1)}, u32[]{:S(2)}) copy-start(bf16[512,512]{1,0:T(8,128)(2,1)S(1)} %collective-permute-done.3.refs_8_) | copy-start | bytes 1572868
  60.5 57.3 %copy-start.6 = (bf16[512,512]{1,0:T(8,128)(2,1)}, bf16[512,512]{1,0:T(8,128)(2,1)S(1)}, u32[]{:S(2)}) copy-start(bf16[512,512]{1,0:T(8,128)(2,1)S(1)} %collective-permute-done.1.refs_6_) | copy-start | bytes 1572868
  60.5 57.3 %copy-start.7 = (bf16[512,512]{1,0:T(8,128)(2,1)}, bf16[512,512]{1,0:T(8,128)(2,1)S(1)}, u32[]{:S(2)}) copy-start(bf16[512,512]{1,0:T(8,128)(2,1)S(1)} %collective-permute-done.6.refs_11_) | copy-start | bytes 1572868
  69.6 0.8 copy-start.8
  139.5 54.1 %copy-start = (f32[2,512,512]{2,1,0:T(8,128)S(1)}, f32[2,512,512]{2,1,0:T(8,128)}, u32[]{:S(2)}) copy-start(f32[2,512,512]{2,1,0:T(8,128)} %get-tuple-element.49) | copy-start | bytes 6291460
  139.5 29.9 %collective-permute-start.7 = (bf16[2,512,512]{2,1,0:T(8,128)(2,1)}, bf16[2,512,512]{2,1,0:T(8,128)(2,1)S(1)}, u32[]{:S(2)}, u32[]{:S(2)}) collective-permute-start(bf16[2,512,512]{2,1,0:T(8,128)(2,1)} %get-tuple-element.50), channel_id=1, source_target_pairs={{0,8},{8,16},{16,24},{24,0},{1,9},{9,17},{17,25},{25,1},{2,10},{10... | collective-permute-start | bytes 3145736 | tf_op jit(solution)/shard_map/ppermute | solution.py:270
  146.3 45.7 %collective-permute-start.8 = (bf16[2,512,512]{2,1,0:T(8,128)(2,1)}, bf16[2,512,512]{2,1,0:T(8,128)(2,1)S(1)}, u32[]{:S(2)}, u32[]{:S(2)}) collective-permute-start(bf16[2,512,512]{2,1,0:T(8,128)(2,1)} %get-tuple-element.51), channel_id=1, source_target_pairs={{0,16},{8,24},{16,0},{24,8},{1,17},{9,25},{17,1},{25,9},{2,18},{10... | collective-permute-start | bytes 3145736 | tf_op jit(solution)/shard_map/ppermute | solution.py:270
  148.5 45.1 %collective-permute-start.9 = (bf16[2,512,512]{2,1,0:T(8,128)(2,1)}, bf16[2,512,512]{2,1,0:T(8,128)(2,1)S(1)}, u32[]{:S(2)}, u32[]{:S(2)}) collective-permute-start(bf16[2,512,512]{2,1,0:T(8,128)(2,1)} %get-tuple-element.52), channel_id=1, source_target_pairs={{0,24},{8,0},{16,8},{24,16},{1,25},{9,1},{17,9},{25,17},{2,26},{10... | collective-permute-start | bytes 3145736 | tf_op jit(solution)/shard_map/ppermute | solution.py:270
  194.2 17.0 %copy-start.9 = (f32[256,512]{1,0:T(8,128)S(1)}, f32[256,512]{1,0:T(8,128)}, u32[]{:S(2)}) copy-start(f32[256,512]{1,0:T(8,128)} %get-tuple-element.48) | copy-start | bytes 1572868
  194.3 16.7 %collective-permute-start.10 = (bf16[512,512]{1,0:T(8,128)(2,1)S(1)}, bf16[512,512]{1,0:T(8,128)(2,1)S(1)}, u32[]{:S(2)}, u32[]{:S(2)}) collective-permute-start(bf16[512,512]{1,0:T(8,128)(2,1)S(1)} %fusion.2), channel_id=1, source_target_pairs={{0,32},{32,0},{1,33},{33,1},{2,34},{34,2},{3,35},{35,3},{4,36},{36... | collective-permute-start | bytes 1572872 | tf_op jit(solution)/shard_map/ppermute | solution.py:271
  213.0 12.4 %all-to-all-start.1 = ((bf16[8,32,512]{2,1,0:T(8,128)(2,1)}), bf16[8,32,512]{2,1,0:T(8,128)(2,1)S(1)}, u32[]{:S(2)}, u32[]{:S(2)}) async-start(bf16[8,32,512]{2,1,0:T(8,128)(2,1)} %bitcast.4), calls=%async_computation.2 | async-start | bytes 524288 | tf_op jit(solution)/shard_map/all_to_all | solution.py:276
Sparse Core Ops, SparseCore 0:
  10.1 107.5 all-gather.2
  139.6 63.3 reduce-scatter.1

commit v4 on v3

--- a/solution.py
+++ b/solution.py
@@ -13,7 +13,7 @@
 STAT_ROWS = 16
 PER_PEER = 2
 PAIR = 2
-UNROLL = 4
+UNROLL = 8
 F32 = jnp.float32
 BF16 = jnp.bfloat16
 PARAMS = pltpu.CompilerParams(vmem_limit_bytes=56 * 1024 * 1024)
@@ -64,15 +64,19 @@
 
 
 def pair_terms(q, g, k, v, norm, delta, factor, keep):
-    scores = mm(k, q, 1, 1) * factor
+    blank = jnp.zeros_like(q)
+    queries = jnp.concatenate(
+        [jnp.concatenate([q, blank], axis=1), jnp.concatenate([blank, g], axis=1)], axis=0
+    )
+    products = mm(jnp.concatenate([k, v], axis=1), queries, 1, 1)
+    scores = products[:, :BLOCK] * factor
     weights = jnp.where(keep, jnp.exp(scores - norm), 0.0)
-    dscores = weights * (mm(v, g, 1, 1) - delta)
+    dscores = weights * (products[:, BLOCK:] - delta)
     weights_b = weights.astype(BF16)
     dscores_b = dscores.astype(BF16)
-    grad_v = mm(weights_b, g, 1, 0)
-    grad_k = mm(dscores_b, q, 1, 0) * factor
+    grads = mm(jnp.concatenate([dscores_b, weights_b], axis=1), queries, 1, 0)
     grad_q = mm(dscores_b, k, 0, 0) * factor
-    return grad_q, grad_k, grad_v
+    return grad_q, grads[:, :BLOCK] * factor, grads[:, BLOCK:]
 
 
 def own_kernel(blocks, heads, factor, pack_ref, k_ref, v_ref, dq_ref, dk_ref, dv_ref):
@@ -107,19 +111,20 @@
 def remote_kernel(blocks, heads, factor, owners, *refs):
     slots_ref, packs_ref, own_k_ref, own_v_ref = refs[:4]
     kv_refs = refs[4 : 4 + owners]
-    dq_out, near_out = refs[4 + owners : 6 + owners]
-    far_outs = refs[6 + owners : 5 + owners + owners // PAIR]
-    dq_ref, acc_ref, far_ref, line_ref, pack_ref, kv_ref, sems = refs[5 + owners + owners // PAIR :]
+    dq_out, *part_outs = refs[4 + owners : 5 + 2 * owners]
+    dq_ref, acc_ref, far_ref, line_ref, pack_ref, kv_ref, sems = refs[5 + 2 * owners :]
     rows = blocks * BLOCK
     span = blocks * owners
-    loads = [pltpu.make_async_copy(packs_ref, pack_ref, sems.at[owners])]
+    loads = [
+        pltpu.make_async_copy(packs_ref, pack_ref, sems.at[owners]),
+        pltpu.make_async_copy(own_k_ref, acc_ref.at[0, pl.ds(0, rows)], sems.at[owners + 1]),
+        pltpu.make_async_copy(own_v_ref, acc_ref.at[0, pl.ds(rows, rows)], sems.at[owners + 2]),
+    ]
     for at in range(owners):
         loads.append(pltpu.make_async_copy(kv_refs[at], kv_ref.at[at], sems.at[at]))
     for load in loads:
         load.start()
     dq_ref[...] = jnp.zeros_like(dq_ref)
-    acc_ref[0, :rows] = own_k_ref[...]
-    acc_ref[0, rows:] = own_v_ref[...]
     acc_ref[1:] = jnp.zeros((owners - 1, *acc_ref.shape[1:]), F32)
     count = slots_ref[0]
     for load in loads:
@@ -164,21 +169,16 @@
         return carry
 
     lax.fori_loop(0, (count + UNROLL - 1) // UNROLL, turn, 0)
-    stores = [
-        pltpu.make_async_copy(dq_ref, dq_out, sems.at[0]),
-        pltpu.make_async_copy(acc_ref.at[pl.ds(0, PAIR)], near_out, sems.at[1]),
-    ]
+    stores = [pltpu.make_async_copy(dq_ref, dq_out, sems.at[owners])]
+    for at in range(PAIR):
+        stores.append(pltpu.make_async_copy(acc_ref.at[at], part_outs[at], sems.at[at]))
     for store in stores:
         store.start()
     for at in range(PAIR, owners):
         far_ref[at - PAIR] = acc_ref[at].astype(BF16)
-        if at % PAIR == PAIR - 1:
-            first = at - 2 * PAIR + 1
-            turned = pltpu.make_async_copy(
-                far_ref.at[pl.ds(first, PAIR)], far_outs[first // PAIR], sems.at[at]
-            )
-            turned.start()
-            stores.append(turned)
+        turned = pltpu.make_async_copy(far_ref.at[at - PAIR], part_outs[at], sems.at[at])
+        turned.start()
+        stores.append(turned)
     for store in stores:
         store.wait()
 
@@ -202,24 +202,22 @@
 
 def remote_call(codes, packs, own_k, own_v, kvs, blocks, heads, factor, rows, width, ring, owners):
     anywhere = pl.BlockSpec(memory_space=pl.ANY)
-    vmem = pl.BlockSpec(memory_space=pltpu.VMEM)
+    part = (2 * rows, width)
     return pl.pallas_call(
         functools.partial(remote_kernel, blocks, heads, factor, owners),
-        in_specs=[pl.BlockSpec(memory_space=pltpu.SMEM), anywhere, vmem, vmem] + [anywhere] * owners,
-        out_specs=(anywhere,) * (X_SIZE + 1),
-        out_shape=(
-            jax.ShapeDtypeStruct((ring, rows, width), BF16),
-            jax.ShapeDtypeStruct((PAIR, 2 * rows, width), F32),
-        )
-        + (jax.ShapeDtypeStruct((PAIR, 2 * rows, width), BF16),) * (X_SIZE - 1),
+        in_specs=[pl.BlockSpec(memory_space=pltpu.SMEM)] + [anywhere] * (3 + owners),
+        out_specs=(anywhere,) * (1 + owners),
+        out_shape=(jax.ShapeDtypeStruct((ring, rows, width), BF16),)
+        + (jax.ShapeDtypeStruct(part, F32),) * PAIR
+        + (jax.ShapeDtypeStruct(part, BF16),) * (owners - PAIR),
         scratch_shapes=[
             pltpu.VMEM((ring, rows, width), BF16),
-            pltpu.VMEM((owners, 2 * rows, width), F32),
-            pltpu.VMEM((owners - PAIR, 2 * rows, width), BF16),
+            pltpu.VMEM((owners, *part), F32),
+            pltpu.VMEM((owners - PAIR, *part), BF16),
             pltpu.VMEM((BLOCK, BLOCK), F32),
             pltpu.VMEM((ring, 2 * rows + STAT_ROWS, width), BF16),
-            pltpu.VMEM((owners, 2 * rows, width), BF16),
-            pltpu.SemaphoreType.DMA((owners + 1,)),
+            pltpu.VMEM((owners, *part), BF16),
+            pltpu.SemaphoreType.DMA((owners + 3,)),
         ],
         compiler_params=PARAMS,
         name="remote",
@@ -260,16 +258,26 @@
     packs, kvs, codes, own_q, own_k, own_v = lax.optimization_barrier(
         (packs, kvs, codes, own_q, own_k, own_v)
     )
-    part_q, near, *far = remote_call(
+    part_q, near, near_other, next_a, next_b, far_a, far_b, last_a, last_b = remote_call(
         codes, packs, own_k, own_v, kvs, blocks, heads, factor, rows, width, ring, owners
     )
     sum_q = lax.psum_scatter(part_q, "j", scatter_dimension=0)
-    sum_kv = near
-    for shift in range(1, X_SIZE):
-        ahead = [(i, (i + shift) % X_SIZE) for i in range(X_SIZE)]
-        sum_kv = sum_kv + lax.ppermute(far[shift - 1], "x", ahead).astype(F32)
-    crossed = lax.ppermute(sum_kv[1].astype(BF16), "p", [(i, (i + 1) % PAIR) for i in range(PAIR)])
-    final_kv = sum_kv[0] + crossed.astype(F32)
+    ahead = [(i, (i + 1) % X_SIZE) for i in range(X_SIZE)]
+    behind = [(i, (i - 1) % X_SIZE) for i in range(X_SIZE)]
+
+    def wide(part):
+        return part.astype(F32)
+
+    through_a = lax.ppermute(far_a, "x", ahead)
+    through_b = lax.ppermute(far_b, "x", behind)
+    from_next = lax.ppermute(next_b, "x", ahead)
+    from_last = lax.ppermute(last_a, "x", behind)
+    next_a = (wide(next_a) + wide(through_a)).astype(BF16)
+    last_b = (wide(last_b) + wide(through_b)).astype(BF16)
+    sum_own = near + wide(from_last) + wide(lax.ppermute(next_a, "x", ahead))
+    sum_other = near_other + wide(from_next) + wide(lax.ppermute(last_b, "x", behind))
+    crossed = lax.ppermute(sum_other.astype(BF16), "p", [(i, (i + 1) % PAIR) for i in range(PAIR)])
+    final_kv = sum_own + wide(crossed)
     final_k = final_kv[:rows].astype(BF16)
     final_v = final_kv[rows:].astype(BF16)
     final_q = (sum_q.astype(F32) + own_q).astype(BF16)

time: 235 us -> 223 us (0.949)
  waiting for transfers between devices: 118 us -> 108 us
  Pallas kernels: 28.1 us -> 18.5 us
  starting transfers between devices: 63.7 us -> 68.5 us
    ppermute x4 -> x7, waiting for transfers between devices: 52.1 us -> 43.3 us  [the longest x1 19.9 us: shards(): lax.ppermute(sum_other.astype(BF16), 'p', [(i, (i + 1) % PAIR) for i in r...]
    pallas_call x1, Pallas kernels: 21.7 us -> 13 us  [remote_call(): pl.pallas_call(functools.partial(remote_kernel, blocks, heads, factor, ow...]
    ppermute x4 -> x7, starting transfers between devices: 18.6 us -> 24.6 us  [the longest x1 8.44 us: shards(): through_a = lax.ppermute(far_a, 'x', ahead)]
    all_gather x1, waiting for transfers between devices: 36.2 us -> 31 us  [shards(): packs = lax.all_gather(pack, 'j')]
    reduce_scatter x1, waiting for transfers between devices: 0.02 us -> 2.91 us  [shards(): sum_q = lax.psum_scatter(part_q, 'j', scatter_dimension=0)]
    convert_element_type x0 -> x3, other arithmetic: none -> 2.63 us  [the longest x1 1.24 us: shards(): last_b = (wide(last_b) + wide(through_b)).astype(BF16)]
  transfers between devices with their start and end apart: 15 -> 18, of which waited for: 9 -> 13; matrix products, arithmetic and copies ran while one was open for 3% -> 4% of each run, Pallas kernels for 2% -> 1%
where the time goes in v4:
time: 223 us; the launch traced here: 222 us
  waiting for transfers between devices  108 us (48%)
  starting transfers between devices  68.5 us (31%)
  Pallas kernels  18.5 us (8%)
  between operations  14.3 us (6%)
  other arithmetic  7.01 us (3%)
  local copies, waits for them, and re-layouts  6.01 us (3%)
    all_gather x1, waiting for transfers between devices, shards(): packs = lax.all_gather(pack, 'j')  31 us
    ppermute x6, waiting for transfers between devices, shards(): kvs += [lax.ppermute(both, 'x', back), lax.ppermute(swapped, 'x', back)]  23.2 us
    ppermute x6, starting transfers between devices, shards(): kvs += [lax.ppermute(both, 'x', back), lax.ppermute(swapped, 'x', back)]  20 us
    ppermute x1, waiting for transfers between devices, shards(): lax.ppermute(sum_other.astype(BF16), 'p', [(i, (i + 1) % PAIR) for i in r...  19.9 us
    all_to_all x1, starting transfers between devices, shards(): lax.all_to_all(jnp.broadcast_to(selected[None], (ring, *selected.shape)),...  13.9 us
    pallas_call x1, Pallas kernels, remote_call(): pl.pallas_call(functools.partial(remote_kernel, blocks, heads, factor, ow...  13 us
    ppermute x1, waiting for transfers between devices, shards(): from_last = lax.ppermute(last_a, 'x', behind)  9.09 us
    ppermute x1, starting transfers between devices, shards(): through_a = lax.ppermute(far_a, 'x', ahead)  8.44 us
  transfers between devices with their start and end apart: 18, of which 13 were waited for; matrix products, arithmetic and copies ran while one was open for 4% of the time, Pallas kernels for 1%

profile of v4, /device:TPU:1, one launch (start us, length us, event | category | flops | bytes accessed | tf_op | source)
XLA Modules:
  0.0 222.3 jit_solution(15882287593079819798)
XLA Ops:
  7.2 2.2 pack.1.pack_ref
  11.3 4.4 %collective-permute-start = (bf16[512,512]{1,0:T(8,128)(2,1)S(1)}, bf16[512,512]{1,0:T(8,128)(2,1)S(1)}, u32[]{:S(2)}, u32[]{:S(2)}) collective-permute-start(bf16[512,512]{1,0:T(8,128)(2,1)S(1)} %constant_dynamic-update-slice_fusion.refs_4_), channel_id=1, source_target_pairs={{0,32},{32,0},{1,33},{33,1},{2,34},{34,2},{3,35},{35,3},{4,36},{36... | collective-permute-start | bytes 1572872 | tf_op jit(solution)/shard_map/ppermute | solution.py:245
  15.7 3.1 %collective-permute-start.5 = (bf16[512,512]{1,0:T(8,128)(2,1)S(1)}, bf16[512,512]{1,0:T(8,128)(2,1)S(1)}, u32[]{:S(2)}, u32[]{:S(2)}) collective-permute-start(bf16[512,512]{1,0:T(8,128)(2,1)S(1)} %constant_dynamic-update-slice_fusion.refs_4_), channel_id=1, source_target_pairs={{0,8},{8,16},{16,24},{24,0},{1,9},{9,17},{17,25},{25,1},{2,10},{10... | collective-permute-start | bytes 1572872 | tf_op jit(solution)/shard_map/ppermute | solution.py:249
  20.2 13.9 %all-to-all-start = ((s32[8,2,4,3]{2,1,3,0:T(2,128)}), s32[8,2,4,3]{2,1,3,0:T(2,128)S(1)}, u32[]{:S(2)}, u32[]{:S(2)}) async-start(s32[8,2,4,3]{2,1,3,0:T(2,128)} %broadcast_in_dim.12), calls=%async_computation | async-start | bytes 49152 | tf_op jit(solution)/shard_map/all_to_all | solution.py:241
  34.1 4.4 %collective-permute-start.3 = (bf16[512,512]{1,0:T(8,128)(2,1)S(1)}, bf16[512,512]{1,0:T(8,128)(2,1)S(1)}, u32[]{:S(2)}, u32[]{:S(2)}) collective-permute-start(bf16[512,512]{1,0:T(8,128)(2,1)S(1)} %constant_dynamic-update-slice_fusion.refs_4_), channel_id=1, source_target_pairs={{0,16},{8,24},{16,0},{24,8},{1,17},{9,25},{17,1},{25,9},{2,18},{10... | collective-permute-start | bytes 1572872 | tf_op jit(solution)/shard_map/ppermute | solution.py:249
  38.5 3.1 %collective-permute-start.1 = (bf16[512,512]{1,0:T(8,128)(2,1)S(1)}, bf16[512,512]{1,0:T(8,128)(2,1)S(1)}, u32[]{:S(2)}, u32[]{:S(2)}) collective-permute-start(bf16[512,512]{1,0:T(8,128)(2,1)S(1)} %constant_dynamic-update-slice_fusion.refs_4_), channel_id=1, source_target_pairs={{0,24},{8,0},{16,8},{24,16},{1,25},{9,1},{17,9},{25,17},{2,26},{10... | collective-permute-start | bytes 1572872 | tf_op jit(solution)/shard_map/ppermute | solution.py:249
  41.6 3.3 %own.1 = (f32[256,512]{1,0:T(8,128)}, f32[256,512]{1,0:T(8,128)}, f32[256,512]{1,0:T(8,128)}) custom-call(bf16[528,512]{1,0:T(8,128)(2,1)} %pack.1.pack_ref, bf16[256,512]{1,0:T(8,128)(2,1)} %k_ref, bf16[256,512]{1,0:T(8,128)(2,1)} %v_ref), custom_call_target="tpu_custom_call" | custom-call | tf_op jit(solution)/shard_map/own/pallas_call | solution.py:251
  44.8 2.0 all-to-all-done
  47.3 3.2 %collective-permute-start.6 = (bf16[512,512]{1,0:T(8,128)(2,1)S(1)}, bf16[512,512]{1,0:T(8,128)(2,1)S(1)}, u32[]{:S(2)}, u32[]{:S(2)}) collective-permute-start(bf16[512,512]{1,0:T(8,128)(2,1)S(1)} %collective-permute-done.refs_5_), channel_id=1, source_target_pairs={{0,8},{8,16},{16,24},{24,0},{1,9},{9,17},{17,25},{25,1},{2,10},{10... | collective-permute-start | bytes 1572872 | tf_op jit(solution)/shard_map/ppermute | solution.py:249
  50.5 2.4 %collective-permute-start.4 = (bf16[512,512]{1,0:T(8,128)(2,1)S(1)}, bf16[512,512]{1,0:T(8,128)(2,1)S(1)}, u32[]{:S(2)}, u32[]{:S(2)}) collective-permute-start(bf16[512,512]{1,0:T(8,128)(2,1)S(1)} %collective-permute-done.refs_5_), channel_id=1, source_target_pairs={{0,16},{8,24},{16,0},{24,8},{1,17},{9,25},{17,1},{25,9},{2,18},{10... | collective-permute-start | bytes 1572872 | tf_op jit(solution)/shard_map/ppermute | solution.py:249
  52.9 3.9 %collective-permute-start.2 = (bf16[512,512]{1,0:T(8,128)(2,1)S(1)}, bf16[512,512]{1,0:T(8,128)(2,1)}, u32[]{:S(2)}, u32[]{:S(2)}) collective-permute-start(bf16[512,512]{1,0:T(8,128)(2,1)S(1)} %collective-permute-done.refs_5_), channel_id=1, source_target_pairs={{0,24},{8,0},{16,8},{24,16},{1,25},{9,1},{17,9},{25,17},{2,26},{10... | collective-permute-start | bytes 1572872 | tf_op jit(solution)/shard_map/ppermute | solution.py:249
  59.0 3.0 %collective-permute-done.1.refs_6_ = bf16[512,512]{1,0:T(8,128)(2,1)S(1)} collective-permute-done((bf16[512,512]{1,0:T(8,128)(2,1)S(1)}, bf16[512,512]{1,0:T(8,128)(2,1)S(1)}, u32[]{:S(2)}, u32[]{:S(2)}) %collective-permute-start.1) | collective-permute-done | bytes 524320 | tf_op jit(solution)/shard_map/ppermute | solution.py:249
  62.8 8.1 %collective-permute-done.4.refs_9_ = bf16[512,512]{1,0:T(8,128)(2,1)S(1)} collective-permute-done((bf16[512,512]{1,0:T(8,128)(2,1)S(1)}, bf16[512,512]{1,0:T(8,128)(2,1)S(1)}, u32[]{:S(2)}, u32[]{:S(2)}) %collective-permute-start.4) | collective-permute-done | bytes 524320 | tf_op jit(solution)/shard_map/ppermute | solution.py:249
  71.8 11.4 %collective-permute-done.2.refs_7_ = bf16[512,512]{1,0:T(8,128)(2,1)} collective-permute-done((bf16[512,512]{1,0:T(8,128)(2,1)S(1)}, bf16[512,512]{1,0:T(8,128)(2,1)}, u32[]{:S(2)}, u32[]{:S(2)}) %collective-permute-start.2) | collective-permute-done | bytes 524320 | tf_op jit(solution)/shard_map/ppermute | solution.py:249
  83.1 31.0 %all-gather.3.cloned.1.call-done = bf16[4224,512]{1,0:T(8,128)(2,1)} async-done(((bf16[528,512]{1,0:T(8,128)(2,1)}), bf16[4224,512]{1,0:T(8,128)(2,1)}) %all-gather.3.cloned.1.call-update) | async-done | bytes 4325392 | tf_op jit(solution)/shard_map/all_gather | solution.py:239
  114.1 13.0 %remote.1 = (bf16[8,256,512]{2,1,0:T(8,128)(2,1)}, f32[512,512]{1,0:T(8,128)}, f32[512,512]{1,0:T(8,128)}, bf16[512,512]{1,0:T(8,128)(2,1)}, bf16[512,512]{1,0:T...) custom-call(s32[129]{0:T(256)} %pad_add_fusion.refs_0_, ...), custom_call_target="tpu_custom_call" | custom-call | tf_op jit(solution)/shard_map/remote/pallas_call | solution.py:206
  127.2 3.6 %collective-permute-start.11 = (bf16[512,512]{1,0:T(8,128)(2,1)}, bf16[512,512]{1,0:T(8,128)(2,1)S(1)}, u32[]{:S(2)}, u32[]{:S(2)}) collective-permute-start(bf16[512,512]{1,0:T(8,128)(2,1)} %get-tuple-element.60), channel_id=1, source_target_pairs={{0,24},{8,0},{16,8},{24,16},{1,25},{9,1},{17,9},{25,17},{2,26},{10... | collective-permute-start | bytes 1572872 | tf_op jit(solution)/shard_map/ppermute | solution.py:272
  130.8 8.4 %collective-permute-start.8 = (bf16[512,512]{1,0:T(8,128)(2,1)}, bf16[512,512]{1,0:T(8,128)(2,1)S(1)}, u32[]{:S(2)}, u32[]{:S(2)}) collective-permute-start(bf16[512,512]{1,0:T(8,128)(2,1)} %get-tuple-element.56), channel_id=1, source_target_pairs={{0,8},{8,16},{16,24},{24,0},{1,9},{9,17},{17,25},{25,1},{2,10},{10... | collective-permute-start | bytes 1572872 | tf_op jit(solution)/shard_map/ppermute | solution.py:271
  139.3 3.4 %collective-permute-start.10 = (bf16[512,512]{1,0:T(8,128)(2,1)}, bf16[512,512]{1,0:T(8,128)(2,1)S(1)}, u32[]{:S(2)}, u32[]{:S(2)}) collective-permute-start(bf16[512,512]{1,0:T(8,128)(2,1)} %get-tuple-element.58), channel_id=1, source_target_pairs={{0,8},{8,16},{16,24},{24,0},{1,9},{9,17},{17,25},{25,1},{2,10},{10... | collective-permute-start | bytes 1572872 | tf_op jit(solution)/shard_map/ppermute | solution.py:273
  142.7 7.4 %collective-permute-done.11 = bf16[512,512]{1,0:T(8,128)(2,1)S(1)} collective-permute-done((bf16[512,512]{1,0:T(8,128)(2,1)}, bf16[512,512]{1,0:T(8,128)(2,1)S(1)}, u32[]{:S(2)}, u32[]{:S(2)}) %collective-permute-start.11) | collective-permute-done | bytes 524320 | tf_op jit(solution)/shard_map/ppermute | solution.py:272
  151.3 1.9 collective-permute-start.12
  153.2 3.2 %collective-permute-start.7 = (bf16[512,512]{1,0:T(8,128)(2,1)}, bf16[512,512]{1,0:T(8,128)(2,1)S(1)}, u32[]{:S(2)}, u32[]{:S(2)}) collective-permute-start(bf16[512,512]{1,0:T(8,128)(2,1)} %get-tuple-element.54), channel_id=1, source_target_pairs={{0,24},{8,0},{16,8},{24,16},{1,25},{9,1},{17,9},{25,17},{2,26},{10... | collective-permute-start | bytes 1572872 | tf_op jit(solution)/shard_map/ppermute | solution.py:274
  157.6 2.1 collective-permute-start.9
  159.7 2.7 %collective-permute-done.10 = bf16[512,512]{1,0:T(8,128)(2,1)S(1)} collective-permute-done((bf16[512,512]{1,0:T(8,128)(2,1)}, bf16[512,512]{1,0:T(8,128)(2,1)S(1)}, u32[]{:S(2)}, u32[]{:S(2)}) %collective-permute-start.10) | collective-permute-done | bytes 524320 | tf_op jit(solution)/shard_map/ppermute | solution.py:273
  162.4 4.2 %collective-permute-done.12 = bf16[512,512]{1,0:T(8,128)(2,1)S(1)} collective-permute-done((bf16[512,512]{1,0:T(8,128)(2,1)S(1)}, bf16[512,512]{1,0:T(8,128)(2,1)S(1)}, u32[]{:S(2)}, u32[]{:S(2)}) %collective-permute-start.12) | collective-permute-done | bytes 524320 | tf_op jit(solution)/shard_map/ppermute | solution.py:278
  166.9 1.9 collective-permute-start.13
  168.8 9.1 %collective-permute-done.7 = bf16[512,512]{1,0:T(8,128)(2,1)S(1)} collective-permute-done((bf16[512,512]{1,0:T(8,128)(2,1)}, bf16[512,512]{1,0:T(8,128)(2,1)S(1)}, u32[]{:S(2)}, u32[]{:S(2)}) %collective-permute-start.7) | collective-permute-done | bytes 524320 | tf_op jit(solution)/shard_map/ppermute | solution.py:274
  177.9 19.9 %collective-permute-done.13 = bf16[512,512]{1,0:T(8,128)(2,1)S(1)} collective-permute-done((bf16[512,512]{1,0:T(8,128)(2,1)S(1)}, bf16[512,512]{1,0:T(8,128)(2,1)S(1)}, u32[]{:S(2)}, u32[]{:S(2)}) %collective-permute-start.13) | collective-permute-done | bytes 524320 | tf_op jit(solution)/shard_map/ppermute | solution.py:279
  198.1 2.9 %reduce-scatter.2.cloned.1.call-done = bf16[1,256,512]{2,1,0:T(8,128)(2,1)} async-done(((bf16[8,256,512]{2,1,0:T(8,128)(2,1)}), bf16[1,256,512]{2,1,0:T(8,128)(2,1)}) %reduce-scatter.2.cloned.1.call-update) | async-done | bytes 262160 | tf_op jit(solution)/shard_map/reduce_scatter | solution.py:264
  201.0 1.7 fusion
  202.7 5.5 %all-to-all-start.1 = ((bf16[8,32,512]{2,1,0:T(8,128)(2,1)}), bf16[8,32,512]{2,1,0:T(8,128)(2,1)S(1)}, u32[]{:S(2)}, u32[]{:S(2)}) async-start(bf16[8,32,512]{2,1,0:T(8,128)(2,1)} %bitcast.4), calls=%async_computation.2 | async-start | bytes 524288 | tf_op jit(solution)/shard_map/all_to_all | solution.py:284
  209.1 5.7 %all-to-all-done.1 = bf16[8,32,512]{2,1,0:T(8,128)(2,1)S(1)} async-done(((bf16[8,32,512]{2,1,0:T(8,128)(2,1)}), bf16[8,32,512]{2,1,0:T(8,128)(2,1)S(1)}, u32[]{:S(2)}, u32[]{:S(2)}) %all-to-all-start.1) | async-done | bytes 262176 | tf_op jit(solution)/shard_map/all_to_all | solution.py:284
  (47 shorter events, 12.2 us)
Async XLA Ops:
  7.2 106.9 %all-gather.3.cloned.1.call-start = ((), (), s32[]{:S(2)}) async-start(), calls=%async_computation.4 | async-start | bytes 4866048 | tf_op jit(solution)/shard_map/all_gather | solution.py:239
  11.3 102.7 %copy-start = (bf16[512,512]{1,0:T(8,128)(2,1)}, bf16[512,512]{1,0:T(8,128)(2,1)S(1)}, u32[]{:S(2)}) copy-start(bf16[512,512]{1,0:T(8,128)(2,1)S(1)} %constant_dynamic-update-slice_fusion.refs_4_) | copy-start | bytes 1572868
  11.3 35.9 %collective-permute-start = (bf16[512,512]{1,0:T(8,128)(2,1)S(1)}, bf16[512,512]{1,0:T(8,128)(2,1)S(1)}, u32[]{:S(2)}, u32[]{:S(2)}) collective-permute-start(bf16[512,512]{1,0:T(8,128)(2,1)S(1)} %constant_dynamic-update-slice_fusion.refs_4_), channel_id=1, source_target_pairs={{0,32},{32,0},{1,33},{33,1},{2,34},{34,2},{3,35},{35,3},{4,36},{36... | collective-permute-start | bytes 1572872 | tf_op jit(solution)/shard_map/ppermute | solution.py:245
  15.7 37.2 %collective-permute-start.5 = (bf16[512,512]{1,0:T(8,128)(2,1)S(1)}, bf16[512,512]{1,0:T(8,128)(2,1)S(1)}, u32[]{:S(2)}, u32[]{:S(2)}) collective-permute-start(bf16[512,512]{1,0:T(8,128)(2,1)S(1)} %constant_dynamic-update-slice_fusion.refs_4_), channel_id=1, source_target_pairs={{0,8},{8,16},{16,24},{24,0},{1,9},{9,17},{17,25},{25,1},{2,10},{10... | collective-permute-start | bytes 1572872 | tf_op jit(solution)/shard_map/ppermute | solution.py:249
  20.2 26.6 %all-to-all-start = ((s32[8,2,4,3]{2,1,3,0:T(2,128)}), s32[8,2,4,3]{2,1,3,0:T(2,128)S(1)}, u32[]{:S(2)}, u32[]{:S(2)}) async-start(s32[8,2,4,3]{2,1,3,0:T(2,128)} %broadcast_in_dim.12), calls=%async_computation | async-start | bytes 49152 | tf_op jit(solution)/shard_map/all_to_all | solution.py:241
  34.1 166.9 %reduce-scatter.2.cloned.1.call-start = ((), (), s32[]{:S(2)}) async-start(), calls=%async_computation.3 | async-start | bytes 2359296 | tf_op jit(solution)/shard_map/reduce_scatter | solution.py:264
  34.1 24.9 %collective-permute-start.3 = (bf16[512,512]{1,0:T(8,128)(2,1)S(1)}, bf16[512,512]{1,0:T(8,128)(2,1)S(1)}, u32[]{:S(2)}, u32[]{:S(2)}) collective-permute-start(bf16[512,512]{1,0:T(8,128)(2,1)S(1)} %constant_dynamic-update-slice_fusion.refs_4_), channel_id=1, source_target_pairs={{0,16},{8,24},{16,0},{24,8},{1,17},{9,25},{17,1},{25,9},{2,18},{10... | collective-permute-start | bytes 1572872 | tf_op jit(solution)/shard_map/ppermute | solution.py:249
  38.5 23.6 %collective-permute-start.1 = (bf16[512,512]{1,0:T(8,128)(2,1)S(1)}, bf16[512,512]{1,0:T(8,128)(2,1)S(1)}, u32[]{:S(2)}, u32[]{:S(2)}) collective-permute-start(bf16[512,512]{1,0:T(8,128)(2,1)S(1)} %constant_dynamic-update-slice_fusion.refs_4_), channel_id=1, source_target_pairs={{0,24},{8,0},{16,8},{24,16},{1,25},{9,1},{17,9},{25,17},{2,26},{10... | collective-permute-start | bytes 1572872 | tf_op jit(solution)/shard_map/ppermute | solution.py:249
  47.3 66.8 %copy-start.3 = (bf16[512,512]{1,0:T(8,128)(2,1)}, bf16[512,512]{1,0:T(8,128)(2,1)S(1)}, u32[]{:S(2)}) copy-start(bf16[512,512]{1,0:T(8,128)(2,1)S(1)} %collective-permute-done.refs_5_) | copy-start | bytes 1572868
  47.3 15.5 %collective-permute-start.6 = (bf16[512,512]{1,0:T(8,128)(2,1)S(1)}, bf16[512,512]{1,0:T(8,128)(2,1)S(1)}, u32[]{:S(2)}, u32[]{:S(2)}) collective-permute-start(bf16[512,512]{1,0:T(8,128)(2,1)S(1)} %collective-permute-done.refs_5_), channel_id=1, source_target_pairs={{0,8},{8,16},{16,24},{24,0},{1,9},{9,17},{17,25},{25,1},{2,10},{10... | collective-permute-start | bytes 1572872 | tf_op jit(solution)/shard_map/ppermute | solution.py:249
  50.5 20.4 %collective-permute-start.4 = (bf16[512,512]{1,0:T(8,128)(2,1)S(1)}, bf16[512,512]{1,0:T(8,128)(2,1)S(1)}, u32[]{:S(2)}, u32[]{:S(2)}) collective-permute-start(bf16[512,512]{1,0:T(8,128)(2,1)S(1)} %collective-permute-done.refs_5_), channel_id=1, source_target_pairs={{0,16},{8,24},{16,0},{24,8},{1,17},{9,25},{17,1},{25,9},{2,18},{10... | collective-permute-start | bytes 1572872 | tf_op jit(solution)/shard_map/ppermute | solution.py:249
  52.9 61.2 %copy-start.4 = (bf16[512,512]{1,0:T(8,128)(2,1)}, bf16[512,512]{1,0:T(8,128)(2,1)S(1)}, u32[]{:S(2)}) copy-start(bf16[512,512]{1,0:T(8,128)(2,1)S(1)} %collective-permute-done.5.refs_10_) | copy-start | bytes 1572868
  52.9 30.2 %collective-permute-start.2 = (bf16[512,512]{1,0:T(8,128)(2,1)S(1)}, bf16[512,512]{1,0:T(8,128)(2,1)}, u32[]{:S(2)}, u32[]{:S(2)}) collective-permute-start(bf16[512,512]{1,0:T(8,128)(2,1)S(1)} %collective-permute-done.refs_5_), channel_id=1, source_target_pairs={{0,24},{8,0},{16,8},{24,16},{1,25},{9,1},{17,9},{25,17},{2,26},{10... | collective-permute-start | bytes 1572872 | tf_op jit(solution)/shard_map/ppermute | solution.py:249
  59.0 55.0 %copy-start.5 = (bf16[512,512]{1,0:T(8,128)(2,1)}, bf16[512,512]{1,0:T(8,128)(2,1)S(1)}, u32[]{:S(2)}) copy-start(bf16[512,512]{1,0:T(8,128)(2,1)S(1)} %collective-permute-done.3.refs_8_) | copy-start | bytes 1572868
  62.1 52.0 %copy-start.6 = (bf16[512,512]{1,0:T(8,128)(2,1)}, bf16[512,512]{1,0:T(8,128)(2,1)S(1)}, u32[]{:S(2)}) copy-start(bf16[512,512]{1,0:T(8,128)(2,1)S(1)} %collective-permute-done.1.refs_6_) | copy-start | bytes 1572868
  62.8 51.3 %copy-start.7 = (bf16[512,512]{1,0:T(8,128)(2,1)}, bf16[512,512]{1,0:T(8,128)(2,1)S(1)}, u32[]{:S(2)}) copy-start(bf16[512,512]{1,0:T(8,128)(2,1)S(1)} %collective-permute-done.6.refs_11_) | copy-start | bytes 1572868
  70.9 0.8 copy-start.8
  127.1 39.5 %copy-start.2 = (f32[512,512]{1,0:T(8,128)S(1)}, f32[512,512]{1,0:T(8,128)}, u32[]{:S(2)}) copy-start(f32[512,512]{1,0:T(8,128)} %get-tuple-element.57) | copy-start | bytes 3145732
  127.2 70.6 %copy-start.1 = (f32[512,512]{1,0:T(8,128)S(1)}, f32[512,512]{1,0:T(8,128)}, u32[]{:S(2)}) copy-start(f32[512,512]{1,0:T(8,128)} %get-tuple-element.53) | copy-start | bytes 3145732
  127.2 22.8 %collective-permute-start.11 = (bf16[512,512]{1,0:T(8,128)(2,1)}, bf16[512,512]{1,0:T(8,128)(2,1)S(1)}, u32[]{:S(2)}, u32[]{:S(2)}) collective-permute-start(bf16[512,512]{1,0:T(8,128)(2,1)} %get-tuple-element.60), channel_id=1, source_target_pairs={{0,24},{8,0},{16,8},{24,16},{1,25},{9,1},{17,9},{25,17},{2,26},{10... | collective-permute-start | bytes 1572872 | tf_op jit(solution)/shard_map/ppermute | solution.py:272
  130.8 25.5 %collective-permute-start.8 = (bf16[512,512]{1,0:T(8,128)(2,1)}, bf16[512,512]{1,0:T(8,128)(2,1)S(1)}, u32[]{:S(2)}, u32[]{:S(2)}) collective-permute-start(bf16[512,512]{1,0:T(8,128)(2,1)} %get-tuple-element.56), channel_id=1, source_target_pairs={{0,8},{8,16},{16,24},{24,0},{1,9},{9,17},{17,25},{25,1},{2,10},{10... | collective-permute-start | bytes 1572872 | tf_op jit(solution)/shard_map/ppermute | solution.py:271
  139.3 23.1 %collective-permute-start.10 = (bf16[512,512]{1,0:T(8,128)(2,1)}, bf16[512,512]{1,0:T(8,128)(2,1)S(1)}, u32[]{:S(2)}, u32[]{:S(2)}) collective-permute-start(bf16[512,512]{1,0:T(8,128)(2,1)} %get-tuple-element.58), channel_id=1, source_target_pairs={{0,8},{8,16},{16,24},{24,0},{1,9},{9,17},{17,25},{25,1},{2,10},{10... | collective-permute-start | bytes 1572872 | tf_op jit(solution)/shard_map/ppermute | solution.py:273
  150.0 51.0 %copy-start.9 = (f32[256,512]{1,0:T(8,128)S(1)}, f32[256,512]{1,0:T(8,128)}, u32[]{:S(2)}) copy-start(f32[256,512]{1,0:T(8,128)} %get-tuple-element.52) | copy-start | bytes 1572868
  151.3 15.4 %collective-permute-start.12 = (bf16[512,512]{1,0:T(8,128)(2,1)S(1)}, bf16[512,512]{1,0:T(8,128)(2,1)S(1)}, u32[]{:S(2)}, u32[]{:S(2)}) collective-permute-start(bf16[512,512]{1,0:T(8,128)(2,1)S(1)} %add_convert_fusion.2), channel_id=1, source_target_pairs={{0,24},{8,0},{16,8},{24,16},{1,25},{9,1},{17,9},{25,17},{2,26},{10... | collective-permute-start | bytes 1572872 | tf_op jit(solution)/shard_map/ppermute | solution.py:278
  153.2 24.7 %collective-permute-start.7 = (bf16[512,512]{1,0:T(8,128)(2,1)}, bf16[512,512]{1,0:T(8,128)(2,1)S(1)}, u32[]{:S(2)}, u32[]{:S(2)}) collective-permute-start(bf16[512,512]{1,0:T(8,128)(2,1)} %get-tuple-element.54), channel_id=1, source_target_pairs={{0,24},{8,0},{16,8},{24,16},{1,25},{9,1},{17,9},{25,17},{2,26},{10... | collective-permute-start | bytes 1572872 | tf_op jit(solution)/shard_map/ppermute | solution.py:274
  157.6 20.3 %collective-permute-start.9 = (bf16[512,512]{1,0:T(8,128)(2,1)S(1)}, bf16[512,512]{1,0:T(8,128)(2,1)S(1)}, u32[]{:S(2)}, u32[]{:S(2)}) collective-permute-start(bf16[512,512]{1,0:T(8,128)(2,1)S(1)} %add_convert_fusion.3), channel_id=1, source_target_pairs={{0,8},{8,16},{16,24},{24,0},{1,9},{9,17},{17,25},{25,1},{2,10},{10... | collective-permute-start | bytes 1572872 | tf_op jit(solution)/shard_map/ppermute | solution.py:277
  166.9 30.9 %collective-permute-start.13 = (bf16[512,512]{1,0:T(8,128)(2,1)S(1)}, bf16[512,512]{1,0:T(8,128)(2,1)S(1)}, u32[]{:S(2)}, u32[]{:S(2)}) collective-permute-start(bf16[512,512]{1,0:T(8,128)(2,1)S(1)} %add_convert_fusion.1), channel_id=1, source_target_pairs={{0,32},{32,0},{1,33},{33,1},{2,34},{34,2},{3,35},{35,3},{4,36},{36... | collective-permute-start | bytes 1572872 | tf_op jit(solution)/shard_map/ppermute | solution.py:279
  202.7 12.0 %all-to-all-start.1 = ((bf16[8,32,512]{2,1,0:T(8,128)(2,1)}), bf16[8,32,512]{2,1,0:T(8,128)(2,1)S(1)}, u32[]{:S(2)}, u32[]{:S(2)}) async-start(bf16[8,32,512]{2,1,0:T(8,128)(2,1)} %bitcast.4), calls=%async_computation.2 | async-start | bytes 524288 | tf_op jit(solution)/shard_map/all_to_all | solution.py:284
Sparse Core Ops, SparseCore 0:
  10.1 103.9 all-gather.2
  127.3 73.6 reduce-scatter.1

commit v5 on v4

--- a/solution.py
+++ b/solution.py
@@ -10,7 +10,6 @@
 
 X_SIZE = 4
 BLOCK = 128
-STAT_ROWS = 16
 PER_PEER = 2
 PAIR = 2
 UNROLL = 8
@@ -25,42 +24,14 @@
     )
 
 
-def three_parts(value):
-    high = value.astype(BF16)
-    rest = value - high.astype(F32)
-    middle = rest.astype(BF16)
-    low = (rest - middle.astype(F32)).astype(BF16)
-    return high, middle, low
-
-
-def pack_kernel(blocks, heads, q_ref, g_ref, o_ref, n_ref, out_ref):
-    rows = blocks * BLOCK
-    out_ref[0:rows, :] = q_ref[...]
-    out_ref[rows : 2 * rows, :] = g_ref[...]
-    for h in range(heads):
-        cols = slice(h * BLOCK, (h + 1) * BLOCK)
-        lines = []
-        for b in range(blocks):
-            at = slice(b * BLOCK, (b + 1) * BLOCK)
-            product = g_ref[at, cols].astype(F32) * o_ref[at, cols].astype(F32)
-            delta = jnp.sum(product.T, axis=0, keepdims=True)
-            norm = n_ref[h : h + 1, at]
-            lines += list(three_parts(norm)) + list(three_parts(delta))
-        lines = [line.astype(F32) for line in lines]
-        pad = jnp.zeros((STAT_ROWS - len(lines), BLOCK), F32)
-        out_ref[2 * rows :, cols] = jnp.concatenate(lines + [pad], axis=0).astype(BF16)
-
-
-def stat_lines(tile, b):
-    tile = tile.astype(F32)
-
-    def line(at):
-        return (tile[at : at + 1] + tile[at + 1 : at + 2]) + tile[at + 2 : at + 3]
-
-    if isinstance(b, int):
-        return line(6 * b), line(6 * b + 3)
-    first = b == 0
-    return jnp.where(first, line(0), line(6)), jnp.where(first, line(3), line(9))
+def pack_kernel(q_ref, g_ref, out_ref):
+    rows = q_ref.shape[0]
+    out_ref[:rows] = q_ref[...]
+    out_ref[rows:] = g_ref[...]
+
+
+def stat_row(b, h, heads):
+    return 2 * (b * heads + h)
 
 
 def pair_terms(q, g, k, v, norm, delta, factor, keep):
@@ -79,8 +50,9 @@
     return grad_q, grads[:, :BLOCK] * factor, grads[:, BLOCK:]
 
 
-def own_kernel(blocks, heads, factor, pack_ref, k_ref, v_ref, dq_ref, dk_ref, dv_ref):
-    rows = blocks * BLOCK
+def own_kernel(
+    blocks, heads, factor, q_ref, g_ref, o_ref, n_ref, k_ref, v_ref, stat_ref, dq_ref, dk_ref, dv_ref
+):
     key_at = lax.broadcasted_iota(jnp.int32, (BLOCK, BLOCK), 0)
     query_at = lax.broadcasted_iota(jnp.int32, (BLOCK, BLOCK), 1)
     keep = key_at <= query_at
@@ -88,16 +60,14 @@
         for h in range(heads):
             at = slice(b * BLOCK, (b + 1) * BLOCK)
             cols = slice(h * BLOCK, (h + 1) * BLOCK)
-            norm, delta = stat_lines(pack_ref[2 * rows :, cols], b)
+            product = g_ref[at, cols].astype(F32) * o_ref[at, cols].astype(F32)
+            delta = jnp.sum(product.T, axis=0, keepdims=True)
+            norm = n_ref[h : h + 1, at]
+            row = stat_row(b, h, heads)
+            stat_ref[row : row + 1] = norm
+            stat_ref[row + 1 : row + 2] = delta
             grad_q, grad_k, grad_v = pair_terms(
-                pack_ref[at, cols],
-                pack_ref[rows + b * BLOCK : rows + (b + 1) * BLOCK, cols],
-                k_ref[at, cols],
-                v_ref[at, cols],
-                norm,
-                delta,
-                factor,
-                keep,
+                q_ref[at, cols], g_ref[at, cols], k_ref[at, cols], v_ref[at, cols], norm, delta, factor, keep
             )
             dq_ref[at, cols] = grad_q
             dk_ref[at, cols] = grad_k
@@ -109,10 +79,10 @@
 
 
 def remote_kernel(blocks, heads, factor, owners, *refs):
-    slots_ref, packs_ref, own_k_ref, own_v_ref = refs[:4]
-    kv_refs = refs[4 : 4 + owners]
-    dq_out, *part_outs = refs[4 + owners : 5 + 2 * owners]
-    dq_ref, acc_ref, far_ref, line_ref, pack_ref, kv_ref, sems = refs[5 + 2 * owners :]
+    slots_ref, stat_ref, own_q_ref, packs_ref, own_k_ref, own_v_ref = refs[:6]
+    kv_refs = refs[6 : 6 + owners]
+    dq_out, *part_outs = refs[6 + owners : 7 + 2 * owners]
+    dq_ref, acc_ref, far_ref, line_ref, pack_ref, kv_ref, sems = refs[7 + 2 * owners :]
     rows = blocks * BLOCK
     span = blocks * owners
     loads = [
@@ -124,9 +94,11 @@
         loads.append(pltpu.make_async_copy(kv_refs[at], kv_ref.at[at], sems.at[at]))
     for load in loads:
         load.start()
+    count = slots_ref[0]
+    mine = slots_ref[slots_ref.shape[0] - 1]
     dq_ref[...] = jnp.zeros_like(dq_ref)
+    dq_ref[mine] = own_q_ref[...].astype(BF16)
     acc_ref[1:] = jnp.zeros((owners - 1, *acc_ref.shape[1:]), F32)
-    count = slots_ref[0]
     for load in loads:
         load.wait()
 
@@ -145,7 +117,9 @@
             g_at = pl.ds(pl.multiple_of(rows + b * BLOCK, BLOCK), BLOCK)
             k_at = pl.ds(pl.multiple_of(kb * BLOCK, BLOCK), BLOCK)
             v_at = pl.ds(pl.multiple_of(rows + kb * BLOCK, BLOCK), BLOCK)
-            norm, delta = stat_lines(pack_ref[zq, 2 * rows :, cols], b)
+            row = stat_row(b, h, heads)
+            norm = stat_ref[zq, pl.ds(row, 1), :]
+            delta = stat_ref[zq, pl.ds(row + 1, 1), :]
             terms = pair_terms(
                 pack_ref[zq, q_at, cols],
                 pack_ref[zq, g_at, cols],
@@ -163,7 +137,8 @@
         for same, zq, q_at, cols, kx, k_at, v_at, (grad_q, grad_k, grad_v) in done:
             acc_ref[kx, k_at, cols] += grad_k
             acc_ref[kx, v_at, cols] += grad_v
-            total = jnp.where(same, line_ref[...], 0.0) + grad_q
+            start = jnp.where(zq == mine, own_q_ref[q_at, cols], 0.0)
+            total = jnp.where(same, line_ref[...], start) + grad_q
             line_ref[...] = total
             dq_ref[zq, q_at, cols] = total.astype(BF16)
         return carry
@@ -197,15 +172,17 @@
     place = jnp.sum(earlier.astype(jnp.int32), axis=1) - 1
     match = (place[None, :] == jnp.arange(slot_total, dtype=jnp.int32)[:, None]) & hit[None, :]
     codes = jnp.sum(jnp.where(match, code[None, :], 0), axis=1)
-    return jnp.concatenate([jnp.sum(hit.astype(jnp.int32))[None], codes])
-
-
-def remote_call(codes, packs, own_k, own_v, kvs, blocks, heads, factor, rows, width, ring, owners):
+    return jnp.concatenate([jnp.sum(hit.astype(jnp.int32))[None], codes, j[None]])
+
+
+def remote_call(codes, stats, own_q, packs, own_k, own_v, kvs, blocks, heads, factor, rows, width, ring, owners):
     anywhere = pl.BlockSpec(memory_space=pl.ANY)
     part = (2 * rows, width)
     return pl.pallas_call(
         functools.partial(remote_kernel, blocks, heads, factor, owners),
-        in_specs=[pl.BlockSpec(memory_space=pltpu.SMEM)] + [anywhere] * (3 + owners),
+        in_specs=[pl.BlockSpec(memory_space=pltpu.SMEM)]
+        + [pl.BlockSpec(memory_space=pltpu.VMEM)] * 2
+        + [anywhere] * (3 + owners),
         out_specs=(anywhere,) * (1 + owners),
         out_shape=(jax.ShapeDtypeStruct((ring, rows, width), BF16),)
         + (jax.ShapeDtypeStruct(part, F32),) * PAIR
@@ -215,13 +192,13 @@
             pltpu.VMEM((owners, *part), F32),
             pltpu.VMEM((owners - PAIR, *part), BF16),
             pltpu.VMEM((BLOCK, BLOCK), F32),
-            pltpu.VMEM((ring, 2 * rows + STAT_ROWS, width), BF16),
+            pltpu.VMEM((ring, 2 * rows, width), BF16),
             pltpu.VMEM((owners, *part), BF16),
             pltpu.SemaphoreType.DMA((owners + 3,)),
         ],
         compiler_params=PARAMS,
         name="remote",
-    )(codes, packs, own_k, own_v, *kvs)
+    )(codes, stats, own_q, packs, own_k, own_v, *kvs)
 
 
 def shards(queries, keys, values, out_grad, outputs, log_norms, selected):
@@ -231,16 +208,13 @@
     ring = lax.axis_size("j")
     owners = lax.axis_size("p") * lax.axis_size("x")
     pack = pl.pallas_call(
-        functools.partial(pack_kernel, blocks, heads),
-        out_shape=jax.ShapeDtypeStruct((2 * rows + STAT_ROWS, width), BF16),
+        pack_kernel,
+        out_shape=jax.ShapeDtypeStruct((2 * rows, width), BF16),
         compiler_params=PARAMS,
         name="pack",
-    )(queries, out_grad, outputs, log_norms.T)
+    )(queries, out_grad)
     packs = lax.all_gather(pack, "j")
     pack, selected, keys, values = lax.optimization_barrier((pack, selected, keys, values))
-    table = lax.all_to_all(
-        jnp.broadcast_to(selected[None], (ring, *selected.shape)), "j", 0, 0, tiled=True
-    )
     both = jnp.concatenate([keys, values], axis=0)
     swapped = lax.ppermute(both, "p", [(i, (i + 1) % PAIR) for i in range(PAIR)])
     kvs = [both, swapped]
@@ -248,18 +222,23 @@
         back = [(i, (i - shift) % X_SIZE) for i in range(X_SIZE)]
         kvs += [lax.ppermute(both, "x", back), lax.ppermute(swapped, "x", back)]
     own = jax.ShapeDtypeStruct((rows, width), F32)
-    own_q, own_k, own_v = pl.pallas_call(
+    stats, own_q, own_k, own_v = pl.pallas_call(
         functools.partial(own_kernel, blocks, heads, factor),
-        out_shape=(own, own, own),
+        out_shape=(jax.ShapeDtypeStruct((2 * blocks * heads, BLOCK), F32), own, own, own),
         compiler_params=PARAMS,
         name="own",
-    )(pack, keys, values)
+    )(queries, out_grad, outputs, log_norms.T, keys, values)
+    picks = jnp.pad(selected.reshape(-1).astype(F32), (0, BLOCK * 8 - selected.size))
+    info = jnp.concatenate([stats, picks.reshape(8, BLOCK)], axis=0)
+    stats = lax.all_to_all(jnp.broadcast_to(info[None], (ring, *info.shape)), "j", 0, 0, tiled=True)
+    table = stats[:, 2 * blocks * heads, : selected.size].astype(jnp.int32)
+    table = table.reshape(ring, *selected.shape)
     codes = slot_codes(table, lax.axis_index("j"), lax.axis_index("p"), lax.axis_index("x"), owners)
-    packs, kvs, codes, own_q, own_k, own_v = lax.optimization_barrier(
-        (packs, kvs, codes, own_q, own_k, own_v)
+    packs, kvs, codes, stats, own_q, own_k, own_v = lax.optimization_barrier(
+        (packs, kvs, codes, stats, own_q, own_k, own_v)
     )
     part_q, near, near_other, next_a, next_b, far_a, far_b, last_a, last_b = remote_call(
-        codes, packs, own_k, own_v, kvs, blocks, heads, factor, rows, width, ring, owners
+        codes, stats, own_q, packs, own_k, own_v, kvs, blocks, heads, factor, rows, width, ring, owners
     )
     sum_q = lax.psum_scatter(part_q, "j", scatter_dimension=0)
     ahead = [(i, (i + 1) % X_SIZE) for i in range(X_SIZE)]
@@ -276,12 +255,12 @@
     last_b = (wide(last_b) + wide(through_b)).astype(BF16)
     sum_own = near + wide(from_last) + wide(lax.ppermute(next_a, "x", ahead))
     sum_other = near_other + wide(from_next) + wide(lax.ppermute(last_b, "x", behind))
-    crossed = lax.ppermute(sum_other.astype(BF16), "p", [(i, (i + 1) % PAIR) for i in range(PAIR)])
+    sum_other, sum_own, sum_q = lax.optimization_barrier((sum_other.astype(BF16), sum_own, sum_q))
+    crossed = lax.ppermute(sum_other, "p", [(i, (i + 1) % PAIR) for i in range(PAIR)])
     final_kv = sum_own + wide(crossed)
     final_k = final_kv[:rows].astype(BF16)
     final_v = final_kv[rows:].astype(BF16)
-    final_q = (sum_q.astype(F32) + own_q).astype(BF16)
-    spread_q = lax.all_to_all(final_q, "head", split_axis=0, concat_axis=1, tiled=True)
+    spread_q = lax.all_to_all(sum_q, "head", split_axis=0, concat_axis=1, tiled=True)
     return spread_q, final_k, final_v
 
 

time: 223 us -> 232 us (1.040)
  blocking collectives: 0 us -> 13.6 us
  starting transfers between devices: 68.5 us -> 62.9 us
  Pallas kernels: 18.5 us -> 22.9 us
  waiting for transfers between devices: 108 us -> 105 us
    ppermute x1, waiting for transfers between devices: 0.01 us -> 30.6 us  [shards(): lax.ppermute(both, 'p', [(i, (i + 1) % PAIR) for i in range(PAIR)])]
    ppermute x1, waiting for transfers between devices: 19.9 us -> 0.01 us  [shards(): lax.ppermute(sum_other, 'p', [(i, (i + 1) % PAIR) for i in range(PAIR)])]
    all_to_all x0 -> x1, blocking collectives: none -> 13.6 us  [shards(): lax.all_to_all(sum_q, 'head', split_axis=0, concat_axis=1, tiled=True)]
    reduce_scatter x1, waiting for transfers between devices: 2.91 us -> 11.4 us  [shards(): sum_q = lax.psum_scatter(part_q, 'j', scatter_dimension=0)]
    all_to_all x2 -> x1, waiting for transfers between devices: 7.63 us -> 0.01 us  [shards(): lax.all_to_all(jnp.broadcast_to(info[None], (ring, *info.shape)), 'j', 0,...]
    all_gather x1, waiting for transfers between devices: 31 us -> 23.6 us  [shards(): packs = lax.all_gather(pack, 'j')]
    ppermute x6, waiting for transfers between devices: 23.2 us -> 16.6 us  [shards(): kvs += [lax.ppermute(both, 'x', back), lax.ppermute(swapped, 'x', back)]]
    ppermute x1, starting transfers between devices: 8.44 us -> 1.92 us  [shards(): through_a = lax.ppermute(far_a, 'x', ahead)]
  transfers between devices with their start and end apart: 18 -> 17, of which waited for: 13 -> 10; matrix products, arithmetic and copies ran while one was open for 4% -> 4% of each run, Pallas kernels for 1% -> 2%
where the time goes in v5:
time: 232 us; the launch traced here: 231 us
  waiting for transfers between devices  105 us (45%)
  starting transfers between devices  62.9 us (27%)
  Pallas kernels  22.9 us (10%)
  between operations  14.3 us (6%)
  blocking collectives  13.6 us (6%)
  other arithmetic  6.62 us (3%)
  local copies, waits for them, and re-layouts  5.27 us (2%)
    ppermute x1, waiting for transfers between devices, shards(): lax.ppermute(both, 'p', [(i, (i + 1) % PAIR) for i in range(PAIR)])  30.6 us
    all_gather x1, waiting for transfers between devices, shards(): packs = lax.all_gather(pack, 'j')  23.6 us
    ppermute x6, starting transfers between devices, shards(): kvs += [lax.ppermute(both, 'x', back), lax.ppermute(swapped, 'x', back)]  21.1 us
    pallas_call x1, Pallas kernels, remote_call(): pl.pallas_call(functools.partial(remote_kernel, blocks, heads, factor, ow...  17.5 us
    ppermute x6, waiting for transfers between devices, shards(): kvs += [lax.ppermute(both, 'x', back), lax.ppermute(swapped, 'x', back)]  16.6 us
    all_to_all x1, starting transfers between devices, shards(): lax.all_to_all(jnp.broadcast_to(info[None], (ring, *info.shape)), 'j', 0,...  15.6 us
    all_to_all x1, blocking collectives, shards(): lax.all_to_all(sum_q, 'head', split_axis=0, concat_axis=1, tiled=True)  13.6 us
    reduce_scatter x1, waiting for transfers between devices, shards(): sum_q = lax.psum_scatter(part_q, 'j', scatter_dimension=0)  11.4 us
  transfers between devices with their start and end apart: 17, of which 10 were waited for; matrix products, arithmetic and copies ran while one was open for 4% of the time, Pallas kernels for 2%

profile of v5, /device:TPU:1, one launch (start us, length us, event | category | flops | bytes accessed | tf_op | source)
XLA Modules:
  0.0 231.0 jit_solution(4212383756633169159)
XLA Ops:
  7.2 1.9 pack.1
  10.0 3.5 %own.1 = (f32[16,128]{1,0:T(8,128)}, f32[256,512]{1,0:T(8,128)}, f32[256,512]{1,0:T(8,128)}, f32[256,512]{1,0:T(8,128)}) custom-call(bf16[256,512]{1,0:T(8,128)(2,1)} %q_ref.3, bf16[256,512]{1,0:T(8,128)(2,1)} %g_ref.3, bf16[256,512]{1,0:T(8,128)(2,1)} %o_ref.1, f32[4,256]{1,0:T(4,128)} %bitcast.15, bf16[256,512]{1,0:T(8,128)(2,1)} %k_ref, bf16[256,512]{1,0:T(8,128)(2,1)} %v_ref), custom_call_target="tpu_custom_call" | custom-call | tf_op jit(solution)/shard_map/own/pallas_call | solution.py:225
  14.8 15.6 %all-to-all-start = ((f32[8,24,128]{2,1,0:T(8,128)}), f32[8,24,128]{2,1,0:T(8,128)S(1)}, u32[]{:S(2)}, u32[]{:S(2)}) async-start(f32[8,24,128]{2,1,0:T(8,128)} %broadcast_in_dim.14), calls=%async_computation | async-start | bytes 196608 | tf_op jit(solution)/shard_map/all_to_all | solution.py:233
  31.5 1.0 constant_dynamic-update-slice_fusion.refs_6_
  32.5 2.6 %collective-permute-start = (bf16[512,512]{1,0:T(8,128)(2,1)S(1)}, bf16[512,512]{1,0:T(8,128)(2,1)S(1)}, u32[]{:S(2)}, u32[]{:S(2)}) collective-permute-start(bf16[512,512]{1,0:T(8,128)(2,1)S(1)} %constant_dynamic-update-slice_fusion.refs_6_), channel_id=1, source_target_pairs={{0,32},{32,0},{1,33},{33,1},{2,34},{34,2},{3,35},{35,3},{4,36},{36... | collective-permute-start | bytes 1572872 | tf_op jit(solution)/shard_map/ppermute | solution.py:219
  35.1 3.1 %collective-permute-start.5 = (bf16[512,512]{1,0:T(8,128)(2,1)S(1)}, bf16[512,512]{1,0:T(8,128)(2,1)S(1)}, u32[]{:S(2)}, u32[]{:S(2)}) collective-permute-start(bf16[512,512]{1,0:T(8,128)(2,1)S(1)} %constant_dynamic-update-slice_fusion.refs_6_), channel_id=1, source_target_pairs={{0,8},{8,16},{16,24},{24,0},{1,9},{9,17},{17,25},{25,1},{2,10},{10... | collective-permute-start | bytes 1572872 | tf_op jit(solution)/shard_map/ppermute | solution.py:223
  38.3 4.4 %collective-permute-start.3 = (bf16[512,512]{1,0:T(8,128)(2,1)S(1)}, bf16[512,512]{1,0:T(8,128)(2,1)S(1)}, u32[]{:S(2)}, u32[]{:S(2)}) collective-permute-start(bf16[512,512]{1,0:T(8,128)(2,1)S(1)} %constant_dynamic-update-slice_fusion.refs_6_), channel_id=1, source_target_pairs={{0,16},{8,24},{16,0},{24,8},{1,17},{9,25},{17,1},{25,9},{2,18},{10... | collective-permute-start | bytes 1572872 | tf_op jit(solution)/shard_map/ppermute | solution.py:223
  42.6 3.1 %collective-permute-start.1 = (bf16[512,512]{1,0:T(8,128)(2,1)S(1)}, bf16[512,512]{1,0:T(8,128)(2,1)S(1)}, u32[]{:S(2)}, u32[]{:S(2)}) collective-permute-start(bf16[512,512]{1,0:T(8,128)(2,1)S(1)} %constant_dynamic-update-slice_fusion.refs_6_), channel_id=1, source_target_pairs={{0,24},{8,0},{16,8},{24,16},{1,25},{9,1},{17,9},{25,17},{2,26},{10... | collective-permute-start | bytes 1572872 | tf_op jit(solution)/shard_map/ppermute | solution.py:223
  46.5 30.6 %collective-permute-done.refs_7_ = bf16[512,512]{1,0:T(8,128)(2,1)S(1)} collective-permute-done((bf16[512,512]{1,0:T(8,128)(2,1)S(1)}, bf16[512,512]{1,0:T(8,128)(2,1)S(1)}, u32[]{:S(2)}, u32[]{:S(2)}) %collective-permute-start) | collective-permute-done | bytes 524320 | tf_op jit(solution)/shard_map/ppermute | solution.py:219
  77.1 3.1 %collective-permute-start.6 = (bf16[512,512]{1,0:T(8,128)(2,1)S(1)}, bf16[512,512]{1,0:T(8,128)(2,1)S(1)}, u32[]{:S(2)}, u32[]{:S(2)}) collective-permute-start(bf16[512,512]{1,0:T(8,128)(2,1)S(1)} %collective-permute-done.refs_7_), channel_id=1, source_target_pairs={{0,8},{8,16},{16,24},{24,0},{1,9},{9,17},{17,25},{25,1},{2,10},{10... | collective-permute-start | bytes 1572872 | tf_op jit(solution)/shard_map/ppermute | solution.py:223
  80.2 4.4 %collective-permute-start.4 = (bf16[512,512]{1,0:T(8,128)(2,1)S(1)}, bf16[512,512]{1,0:T(8,128)(2,1)S(1)}, u32[]{:S(2)}, u32[]{:S(2)}) collective-permute-start(bf16[512,512]{1,0:T(8,128)(2,1)S(1)} %collective-permute-done.refs_7_), channel_id=1, source_target_pairs={{0,16},{8,24},{16,0},{24,8},{1,17},{9,25},{17,1},{25,9},{2,18},{10... | collective-permute-start | bytes 1572872 | tf_op jit(solution)/shard_map/ppermute | solution.py:223
  84.7 3.0 %collective-permute-start.2 = (bf16[512,512]{1,0:T(8,128)(2,1)S(1)}, bf16[512,512]{1,0:T(8,128)(2,1)}, u32[]{:S(2)}, u32[]{:S(2)}) collective-permute-start(bf16[512,512]{1,0:T(8,128)(2,1)S(1)} %collective-permute-done.refs_7_), channel_id=1, source_target_pairs={{0,24},{8,0},{16,8},{24,16},{1,25},{9,1},{17,9},{25,17},{2,26},{10... | collective-permute-start | bytes 1572872 | tf_op jit(solution)/shard_map/ppermute | solution.py:223
  88.0 1.3 pad_add_fusion.refs_0_
  89.3 3.4 %collective-permute-done.6.refs_13_ = bf16[512,512]{1,0:T(8,128)(2,1)S(1)} collective-permute-done((bf16[512,512]{1,0:T(8,128)(2,1)S(1)}, bf16[512,512]{1,0:T(8,128)(2,1)S(1)}, u32[]{:S(2)}, u32[]{:S(2)}) %collective-permute-start.6) | collective-permute-done | bytes 524320 | tf_op jit(solution)/shard_map/ppermute | solution.py:223
  92.7 11.9 %collective-permute-done.4.refs_11_ = bf16[512,512]{1,0:T(8,128)(2,1)S(1)} collective-permute-done((bf16[512,512]{1,0:T(8,128)(2,1)S(1)}, bf16[512,512]{1,0:T(8,128)(2,1)S(1)}, u32[]{:S(2)}, u32[]{:S(2)}) %collective-permute-start.4) | collective-permute-done | bytes 524320 | tf_op jit(solution)/shard_map/ppermute | solution.py:223
  105.4 1.3 collective-permute-done.2.refs_9_
  106.7 23.6 %all-gather.3.cloned.1.call-done = bf16[4096,512]{1,0:T(8,128)(2,1)} async-done(((bf16[512,512]{1,0:T(8,128)(2,1)}), bf16[4096,512]{1,0:T(8,128)(2,1)}) %all-gather.3.cloned.1.call-update) | async-done | bytes 4194320 | tf_op jit(solution)/shard_map/all_gather | solution.py:216
  130.3 17.5 %remote.1 = (bf16[8,256,512]{2,1,0:T(8,128)(2,1)}, f32[512,512]{1,0:T(8,128)}, f32[512,512]{1,0:T(8,128)}, bf16[512,512]{1,0:T(8,128)(2,1)}, bf16[512,512]{1,0:T...) custom-call(s32[130]{0:T(256)} %pad_add_fusion.refs_0_, ...), custom_call_target="tpu_custom_call" | custom-call | tf_op jit(solution)/shard_map/remote/pallas_call | solution.py:181
  147.9 6.2 %collective-permute-start.8 = (bf16[512,512]{1,0:T(8,128)(2,1)}, bf16[512,512]{1,0:T(8,128)(2,1)S(1)}, u32[]{:S(2)}, u32[]{:S(2)}) collective-permute-start(bf16[512,512]{1,0:T(8,128)(2,1)} %get-tuple-element.60), channel_id=1, source_target_pairs={{0,24},{8,0},{16,8},{24,16},{1,25},{9,1},{17,9},{25,17},{2,26},{10... | collective-permute-start | bytes 1572872 | tf_op jit(solution)/shard_map/ppermute | solution.py:251
  154.2 1.9 collective-permute-start.11
  156.1 1.9 collective-permute-start.7
  158.0 7.9 %collective-permute-done.8 = bf16[512,512]{1,0:T(8,128)(2,1)S(1)} collective-permute-done((bf16[512,512]{1,0:T(8,128)(2,1)}, bf16[512,512]{1,0:T(8,128)(2,1)S(1)}, u32[]{:S(2)}, u32[]{:S(2)}) %collective-permute-start.8) | collective-permute-done | bytes 524320 | tf_op jit(solution)/shard_map/ppermute | solution.py:251
  165.9 1.2 add_convert_fusion.3
  167.1 5.3 %collective-permute-start.9 = (bf16[512,512]{1,0:T(8,128)(2,1)S(1)}, bf16[512,512]{1,0:T(8,128)(2,1)S(1)}, u32[]{:S(2)}, u32[]{:S(2)}) collective-permute-start(bf16[512,512]{1,0:T(8,128)(2,1)S(1)} %add_convert_fusion.3), channel_id=1, source_target_pairs={{0,24},{8,0},{16,8},{24,16},{1,25},{9,1},{17,9},{25,17},{2,26},{10... | collective-permute-start | bytes 1572872 | tf_op jit(solution)/shard_map/ppermute | solution.py:257
  172.4 1.9 collective-permute-start.10
  174.3 1.2 add_convert_fusion.1
  175.5 3.4 %collective-permute-start.12 = (bf16[512,512]{1,0:T(8,128)(2,1)S(1)}, bf16[512,512]{1,0:T(8,128)(2,1)S(1)}, u32[]{:S(2)}, u32[]{:S(2)}) collective-permute-start(bf16[512,512]{1,0:T(8,128)(2,1)S(1)} %add_convert_fusion.1), channel_id=1, source_target_pairs={{0,8},{8,16},{16,24},{24,0},{1,9},{9,17},{17,25},{25,1},{2,10},{10... | collective-permute-start | bytes 1572872 | tf_op jit(solution)/shard_map/ppermute | solution.py:256
  178.9 3.3 %collective-permute-done.7 = bf16[512,512]{1,0:T(8,128)(2,1)S(1)} collective-permute-done((bf16[512,512]{1,0:T(8,128)(2,1)}, bf16[512,512]{1,0:T(8,128)(2,1)S(1)}, u32[]{:S(2)}, u32[]{:S(2)}) %collective-permute-start.7) | collective-permute-done | bytes 524320 | tf_op jit(solution)/shard_map/ppermute | solution.py:252
  183.3 11.1 %collective-permute-done.10 = bf16[512,512]{1,0:T(8,128)(2,1)S(1)} collective-permute-done((bf16[512,512]{1,0:T(8,128)(2,1)}, bf16[512,512]{1,0:T(8,128)(2,1)S(1)}, u32[]{:S(2)}, u32[]{:S(2)}) %collective-permute-start.10) | collective-permute-done | bytes 524320 | tf_op jit(solution)/shard_map/ppermute | solution.py:253
  194.6 11.4 %reduce-scatter.2.cloned.1.call-done = bf16[1,256,512]{2,1,0:T(8,128)(2,1)} async-done(((bf16[8,256,512]{2,1,0:T(8,128)(2,1)}), bf16[1,256,512]{2,1,0:T(8,128)(2,1)}) %reduce-scatter.2.cloned.1.call-update) | async-done | bytes 262160 | tf_op jit(solution)/shard_map/reduce_scatter | solution.py:243
  206.1 2.8 %collective-permute-start.13 = (bf16[512,512]{1,0:T(8,128)(2,1)S(1)}, bf16[512,512]{1,0:T(8,128)(2,1)S(1)}, u32[]{:S(2)}, u32[]{:S(2)}) collective-permute-start(bf16[512,512]{1,0:T(8,128)(2,1)S(1)} %add_convert_fusion.2), channel_id=1, source_target_pairs={{0,32},{32,0},{1,33},{33,1},{2,34},{34,2},{3,35},{35,3},{4,36},{36... | collective-permute-start | bytes 1572872 | tf_op jit(solution)/shard_map/ppermute | solution.py:259
  208.8 13.6 %all_to_all.24 = bf16[8,32,512]{2,1,0:T(8,128)(2,1)S(1)} all-to-all(bf16[8,32,512]{2,1,0:T(8,128)(2,1)} %bitcast.13), channel_id=1, replica_groups=mesh['j'=8,'p'=2,'x'=4,'head'=8] {'head'}, dimensions={0} | all-to-all | bytes 524288 | tf_op jit(solution)/shard_map/all_to_all | solution.py:263
  (50 shorter events, 8.2 us)
Async XLA Ops:
  7.2 123.1 %all-gather.3.cloned.1.call-start = ((), (), s32[]{:S(2)}) async-start(), calls=%async_computation.4 | async-start | bytes 4718592 | tf_op jit(solution)/shard_map/all_gather | solution.py:216
  14.8 30.9 %all-to-all-start = ((f32[8,24,128]{2,1,0:T(8,128)}), f32[8,24,128]{2,1,0:T(8,128)S(1)}, u32[]{:S(2)}, u32[]{:S(2)}) async-start(f32[8,24,128]{2,1,0:T(8,128)} %broadcast_in_dim.14), calls=%async_computation | async-start | bytes 196608 | tf_op jit(solution)/shard_map/all_to_all | solution.py:233
  30.5 175.6 %reduce-scatter.2.cloned.1.call-start = ((), (), s32[]{:S(2)}) async-start(), calls=%async_computation.3 | async-start | bytes 2359296 | tf_op jit(solution)/shard_map/reduce_scatter | solution.py:243
  32.5 97.8 %copy-start = (bf16[512,512]{1,0:T(8,128)(2,1)}, bf16[512,512]{1,0:T(8,128)(2,1)S(1)}, u32[]{:S(2)}) copy-start(bf16[512,512]{1,0:T(8,128)(2,1)S(1)} %constant_dynamic-update-slice_fusion.refs_6_) | copy-start | bytes 1572868
  32.5 44.6 %collective-permute-start = (bf16[512,512]{1,0:T(8,128)(2,1)S(1)}, bf16[512,512]{1,0:T(8,128)(2,1)S(1)}, u32[]{:S(2)}, u32[]{:S(2)}) collective-permute-start(bf16[512,512]{1,0:T(8,128)(2,1)S(1)} %constant_dynamic-update-slice_fusion.refs_6_), channel_id=1, source_target_pairs={{0,32},{32,0},{1,33},{33,1},{2,34},{34,2},{3,35},{35,3},{4,36},{36... | collective-permute-start | bytes 1572872 | tf_op jit(solution)/shard_map/ppermute | solution.py:219
  35.1 49.5 %collective-permute-start.5 = (bf16[512,512]{1,0:T(8,128)(2,1)S(1)}, bf16[512,512]{1,0:T(8,128)(2,1)S(1)}, u32[]{:S(2)}, u32[]{:S(2)}) collective-permute-start(bf16[512,512]{1,0:T(8,128)(2,1)S(1)} %constant_dynamic-update-slice_fusion.refs_6_), channel_id=1, source_target_pairs={{0,8},{8,16},{16,24},{24,0},{1,9},{9,17},{17,25},{25,1},{2,10},{10... | collective-permute-start | bytes 1572872 | tf_op jit(solution)/shard_map/ppermute | solution.py:223
  38.3 51.0 %collective-permute-start.3 = (bf16[512,512]{1,0:T(8,128)(2,1)S(1)}, bf16[512,512]{1,0:T(8,128)(2,1)S(1)}, u32[]{:S(2)}, u32[]{:S(2)}) collective-permute-start(bf16[512,512]{1,0:T(8,128)(2,1)S(1)} %constant_dynamic-update-slice_fusion.refs_6_), channel_id=1, source_target_pairs={{0,16},{8,24},{16,0},{24,8},{1,17},{9,25},{17,1},{25,9},{2,18},{10... | collective-permute-start | bytes 1572872 | tf_op jit(solution)/shard_map/ppermute | solution.py:223
  42.6 46.7 %collective-permute-start.1 = (bf16[512,512]{1,0:T(8,128)(2,1)S(1)}, bf16[512,512]{1,0:T(8,128)(2,1)S(1)}, u32[]{:S(2)}, u32[]{:S(2)}) collective-permute-start(bf16[512,512]{1,0:T(8,128)(2,1)S(1)} %constant_dynamic-update-slice_fusion.refs_6_), channel_id=1, source_target_pairs={{0,24},{8,0},{16,8},{24,16},{1,25},{9,1},{17,9},{25,17},{2,26},{10... | collective-permute-start | bytes 1572872 | tf_op jit(solution)/shard_map/ppermute | solution.py:223
  45.7 84.6 %copy-start.9 = (f32[8,24,128]{2,1,0:T(8,128)}, f32[8,24,128]{2,1,0:T(8,128)S(1)}, u32[]{:S(2)}) copy-start(f32[8,24,128]{2,1,0:T(8,128)S(1)} %all-to-all-done.refs_1_) | copy-start | bytes 294916
  77.1 53.2 %copy-start.3 = (bf16[512,512]{1,0:T(8,128)(2,1)}, bf16[512,512]{1,0:T(8,128)(2,1)S(1)}, u32[]{:S(2)}) copy-start(bf16[512,512]{1,0:T(8,128)(2,1)S(1)} %collective-permute-done.refs_7_) | copy-start | bytes 1572868
  77.1 15.6 %collective-permute-start.6 = (bf16[512,512]{1,0:T(8,128)(2,1)S(1)}, bf16[512,512]{1,0:T(8,128)(2,1)S(1)}, u32[]{:S(2)}, u32[]{:S(2)}) collective-permute-start(bf16[512,512]{1,0:T(8,128)(2,1)S(1)} %collective-permute-done.refs_7_), channel_id=1, source_target_pairs={{0,8},{8,16},{16,24},{24,0},{1,9},{9,17},{17,25},{25,1},{2,10},{10... | collective-permute-start | bytes 1572872 | tf_op jit(solution)/shard_map/ppermute | solution.py:223
  80.2 24.4 %collective-permute-start.4 = (bf16[512,512]{1,0:T(8,128)(2,1)S(1)}, bf16[512,512]{1,0:T(8,128)(2,1)S(1)}, u32[]{:S(2)}, u32[]{:S(2)}) collective-permute-start(bf16[512,512]{1,0:T(8,128)(2,1)S(1)} %collective-permute-done.refs_7_), channel_id=1, source_target_pairs={{0,16},{8,24},{16,0},{24,8},{1,17},{9,25},{17,1},{25,9},{2,18},{10... | collective-permute-start | bytes 1572872 | tf_op jit(solution)/shard_map/ppermute | solution.py:223
  84.7 45.6 %copy-start.4 = (bf16[512,512]{1,0:T(8,128)(2,1)}, bf16[512,512]{1,0:T(8,128)(2,1)S(1)}, u32[]{:S(2)}) copy-start(bf16[512,512]{1,0:T(8,128)(2,1)S(1)} %collective-permute-done.5.refs_12_) | copy-start | bytes 1572868
  84.7 22.1 %collective-permute-start.2 = (bf16[512,512]{1,0:T(8,128)(2,1)S(1)}, bf16[512,512]{1,0:T(8,128)(2,1)}, u32[]{:S(2)}, u32[]{:S(2)}) collective-permute-start(bf16[512,512]{1,0:T(8,128)(2,1)S(1)} %collective-permute-done.refs_7_), channel_id=1, source_target_pairs={{0,24},{8,0},{16,8},{24,16},{1,25},{9,1},{17,9},{25,17},{2,26},{10... | collective-permute-start | bytes 1572872 | tf_op jit(solution)/shard_map/ppermute | solution.py:223
  89.3 41.0 %copy-start.5 = (bf16[512,512]{1,0:T(8,128)(2,1)}, bf16[512,512]{1,0:T(8,128)(2,1)S(1)}, u32[]{:S(2)}) copy-start(bf16[512,512]{1,0:T(8,128)(2,1)S(1)} %collective-permute-done.3.refs_10_) | copy-start | bytes 1572868
  89.3 41.0 %copy-start.6 = (bf16[512,512]{1,0:T(8,128)(2,1)}, bf16[512,512]{1,0:T(8,128)(2,1)S(1)}, u32[]{:S(2)}) copy-start(bf16[512,512]{1,0:T(8,128)(2,1)S(1)} %collective-permute-done.1.refs_8_) | copy-start | bytes 1572868
  92.7 37.6 %copy-start.7 = (bf16[512,512]{1,0:T(8,128)(2,1)}, bf16[512,512]{1,0:T(8,128)(2,1)S(1)}, u32[]{:S(2)}) copy-start(bf16[512,512]{1,0:T(8,128)(2,1)S(1)} %collective-permute-done.6.refs_13_) | copy-start | bytes 1572868
  104.6 0.8 copy-start.8
  147.9 35.2 %copy-start.2 = (f32[512,512]{1,0:T(8,128)S(1)}, f32[512,512]{1,0:T(8,128)}, u32[]{:S(2)}) copy-start(f32[512,512]{1,0:T(8,128)} %get-tuple-element.57) | copy-start | bytes 3145732
  147.9 46.5 %copy-start.1 = (f32[512,512]{1,0:T(8,128)S(1)}, f32[512,512]{1,0:T(8,128)}, u32[]{:S(2)}) copy-start(f32[512,512]{1,0:T(8,128)} %get-tuple-element.61) | copy-start | bytes 3145732
  147.9 18.0 %collective-permute-start.8 = (bf16[512,512]{1,0:T(8,128)(2,1)}, bf16[512,512]{1,0:T(8,128)(2,1)S(1)}, u32[]{:S(2)}, u32[]{:S(2)}) collective-permute-start(bf16[512,512]{1,0:T(8,128)(2,1)} %get-tuple-element.60), channel_id=1, source_target_pairs={{0,24},{8,0},{16,8},{24,16},{1,25},{9,1},{17,9},{25,17},{2,26},{10... | collective-permute-start | bytes 1572872 | tf_op jit(solution)/shard_map/ppermute | solution.py:251
  154.2 20.2 %collective-permute-start.11 = (bf16[512,512]{1,0:T(8,128)(2,1)}, bf16[512,512]{1,0:T(8,128)(2,1)S(1)}, u32[]{:S(2)}, u32[]{:S(2)}) collective-permute-start(bf16[512,512]{1,0:T(8,128)(2,1)} %get-tuple-element.64), channel_id=1, source_target_pairs={{0,8},{8,16},{16,24},{24,0},{1,9},{9,17},{17,25},{25,1},{2,10},{10... | collective-permute-start | bytes 1572872 | tf_op jit(solution)/shard_map/ppermute | solution.py:250
  156.1 26.1 %collective-permute-start.7 = (bf16[512,512]{1,0:T(8,128)(2,1)}, bf16[512,512]{1,0:T(8,128)(2,1)S(1)}, u32[]{:S(2)}, u32[]{:S(2)}) collective-permute-start(bf16[512,512]{1,0:T(8,128)(2,1)} %get-tuple-element.58), channel_id=1, source_target_pairs={{0,8},{8,16},{16,24},{24,0},{1,9},{9,17},{17,25},{25,1},{2,10},{10... | collective-permute-start | bytes 1572872 | tf_op jit(solution)/shard_map/ppermute | solution.py:252
  167.1 16.0 %collective-permute-start.9 = (bf16[512,512]{1,0:T(8,128)(2,1)S(1)}, bf16[512,512]{1,0:T(8,128)(2,1)S(1)}, u32[]{:S(2)}, u32[]{:S(2)}) collective-permute-start(bf16[512,512]{1,0:T(8,128)(2,1)S(1)} %add_convert_fusion.3), channel_id=1, source_target_pairs={{0,24},{8,0},{16,8},{24,16},{1,25},{9,1},{17,9},{25,17},{2,26},{10... | collective-permute-start | bytes 1572872 | tf_op jit(solution)/shard_map/ppermute | solution.py:257
  172.4 22.0 %collective-permute-start.10 = (bf16[512,512]{1,0:T(8,128)(2,1)}, bf16[512,512]{1,0:T(8,128)(2,1)S(1)}, u32[]{:S(2)}, u32[]{:S(2)}) collective-permute-start(bf16[512,512]{1,0:T(8,128)(2,1)} %get-tuple-element.62), channel_id=1, source_target_pairs={{0,24},{8,0},{16,8},{24,16},{1,25},{9,1},{17,9},{25,17},{2,26},{10... | collective-permute-start | bytes 1572872 | tf_op jit(solution)/shard_map/ppermute | solution.py:253
  175.5 18.9 %collective-permute-start.12 = (bf16[512,512]{1,0:T(8,128)(2,1)S(1)}, bf16[512,512]{1,0:T(8,128)(2,1)S(1)}, u32[]{:S(2)}, u32[]{:S(2)}) collective-permute-start(bf16[512,512]{1,0:T(8,128)(2,1)S(1)} %add_convert_fusion.1), channel_id=1, source_target_pairs={{0,8},{8,16},{16,24},{24,0},{1,9},{9,17},{17,25},{25,1},{2,10},{10... | collective-permute-start | bytes 1572872 | tf_op jit(solution)/shard_map/ppermute | solution.py:256
  206.1 17.1 %collective-permute-start.13 = (bf16[512,512]{1,0:T(8,128)(2,1)S(1)}, bf16[512,512]{1,0:T(8,128)(2,1)S(1)}, u32[]{:S(2)}, u32[]{:S(2)}) collective-permute-start(bf16[512,512]{1,0:T(8,128)(2,1)S(1)} %add_convert_fusion.2), channel_id=1, source_target_pairs={{0,32},{32,0},{1,33},{33,1},{2,34},{34,2},{3,35},{35,3},{4,36},{36... | collective-permute-start | bytes 1572872 | tf_op jit(solution)/shard_map/ppermute | solution.py:259
Sparse Core Ops, SparseCore 0:
  10.1 120.1 all-gather.2
  148.0 57.9 reduce-scatter.1

commit v6 on v5

--- a/solution.py
+++ b/solution.py
@@ -228,6 +228,7 @@
         compiler_params=PARAMS,
         name="own",
     )(queries, out_grad, outputs, log_norms.T, keys, values)
+    stats, selected, swapped = lax.optimization_barrier((stats, selected, swapped))
     picks = jnp.pad(selected.reshape(-1).astype(F32), (0, BLOCK * 8 - selected.size))
     info = jnp.concatenate([stats, picks.reshape(8, BLOCK)], axis=0)
     stats = lax.all_to_all(jnp.broadcast_to(info[None], (ring, *info.shape)), "j", 0, 0, tiled=True)

time: 232 us -> 218 us (0.940)
  waiting for transfers between devices: 105 us -> 86.7 us
  starting transfers between devices: 62.9 us -> 68.6 us
    ppermute x1, waiting for transfers between devices: 30.6 us -> 3.52 us  [shards(): lax.ppermute(both, 'p', [(i, (i + 1) % PAIR) for i in range(PAIR)])]
    ppermute x6, waiting for transfers between devices: 16.6 us -> 29.5 us  [shards(): kvs += [lax.ppermute(both, 'x', back), lax.ppermute(swapped, 'x', back)]]
    all_gather x1, waiting for transfers between devices: 23.6 us -> 16.9 us  [shards(): packs = lax.all_gather(pack, 'j')]
    reduce_scatter x1, waiting for transfers between devices: 11.4 us -> 15.4 us  [shards(): sum_q = lax.psum_scatter(part_q, 'j', scatter_dimension=0)]
    all_to_all x1, starting transfers between devices: 15.6 us -> 18.9 us  [shards(): lax.all_to_all(jnp.broadcast_to(info[None], (ring, *info.shape)), 'j', 0,...]
  transfers between devices with their start and end apart: 17 -> 17, of which waited for: 10 -> 11; matrix products, arithmetic and copies ran while one was open for 4% -> 5% of each run, Pallas kernels for 2% -> 2%
where the time goes in v6:
time: 218 us; the launch traced here: 216 us
  waiting for transfers between devices  86.7 us (40%)
  starting transfers between devices  68.6 us (31%)
  Pallas kernels  21.9 us (10%)
  between operations  14.3 us (7%)
  blocking collectives  13.5 us (6%)
  other arithmetic  6.64 us (3%)
  local copies, waits for them, and re-layouts  4.45 us (2%)
    ppermute x6, waiting for transfers between devices, shards(): kvs += [lax.ppermute(both, 'x', back), lax.ppermute(swapped, 'x', back)]  29.5 us
    ppermute x6, starting transfers between devices, shards(): kvs += [lax.ppermute(both, 'x', back), lax.ppermute(swapped, 'x', back)]  20.2 us
    all_to_all x1, starting transfers between devices, shards(): lax.all_to_all(jnp.broadcast_to(info[None], (ring, *info.shape)), 'j', 0,...  18.9 us
    all_gather x1, waiting for transfers between devices, shards(): packs = lax.all_gather(pack, 'j')  16.9 us
    pallas_call x1, Pallas kernels, remote_call(): pl.pallas_call(functools.partial(remote_kernel, blocks, heads, factor, ow...  16.6 us
    reduce_scatter x1, waiting for transfers between devices, shards(): sum_q = lax.psum_scatter(part_q, 'j', scatter_dimension=0)  15.4 us
    all_to_all x1, blocking collectives, shards(): lax.all_to_all(sum_q, 'head', split_axis=0, concat_axis=1, tiled=True)  13.5 us
    ppermute x1, waiting for transfers between devices, shards(): from_last = lax.ppermute(last_a, 'x', behind)  11 us
  transfers between devices with their start and end apart: 17, of which 11 were waited for; matrix products, arithmetic and copies ran while one was open for 5% of the time, Pallas kernels for 2%

profile of v6, /device:TPU:1, one launch (start us, length us, event | category | flops | bytes accessed | tf_op | source)
XLA Modules:
  0.0 216.1 jit_solution(5852151188755641402)
XLA Ops:
  7.2 1.9 pack.1
  11.1 4.4 %collective-permute-start = (bf16[512,512]{1,0:T(8,128)(2,1)S(1)}, bf16[512,512]{1,0:T(8,128)(2,1)S(1)}, u32[]{:S(2)}, u32[]{:S(2)}) collective-permute-start(bf16[512,512]{1,0:T(8,128)(2,1)S(1)} %constant_dynamic-update-slice_fusion.refs_6_), channel_id=1, source_target_pairs={{0,32},{32,0},{1,33},{33,1},{2,34},{34,2},{3,35},{35,3},{4,36},{36... | collective-permute-start | bytes 1572872 | tf_op jit(solution)/shard_map/ppermute | solution.py:219
  15.4 3.5 %own.1 = (f32[16,128]{1,0:T(8,128)}, f32[256,512]{1,0:T(8,128)}, f32[256,512]{1,0:T(8,128)}, f32[256,512]{1,0:T(8,128)}) custom-call(bf16[256,512]{1,0:T(8,128)(2,1)} %q_ref.3, bf16[256,512]{1,0:T(8,128)(2,1)} %g_ref.3, bf16[256,512]{1,0:T(8,128)(2,1)} %o_ref.1, f32[4,256]{1,0:T(4,128)} %bitcast.15, bf16[256,512]{1,0:T(8,128)(2,1)} %k_ref, bf16[256,512]{1,0:T(8,128)(2,1)} %v_ref), custom_call_target="tpu_custom_call" | custom-call | tf_op jit(solution)/shard_map/own/pallas_call | solution.py:225
  19.0 3.5 %collective-permute-done.refs_7_ = bf16[512,512]{1,0:T(8,128)(2,1)S(1)} collective-permute-done((bf16[512,512]{1,0:T(8,128)(2,1)S(1)}, bf16[512,512]{1,0:T(8,128)(2,1)S(1)}, u32[]{:S(2)}, u32[]{:S(2)}) %collective-permute-start) | collective-permute-done | bytes 524320 | tf_op jit(solution)/shard_map/ppermute | solution.py:219
  24.7 18.9 %all-to-all-start = ((f32[8,24,128]{2,1,0:T(8,128)}), f32[8,24,128]{2,1,0:T(8,128)S(1)}, u32[]{:S(2)}, u32[]{:S(2)}) async-start(f32[8,24,128]{2,1,0:T(8,128)} %broadcast_in_dim.14), calls=%async_computation | async-start | bytes 196608 | tf_op jit(solution)/shard_map/all_to_all | solution.py:234
  43.7 3.1 %collective-permute-start.5 = (bf16[512,512]{1,0:T(8,128)(2,1)S(1)}, bf16[512,512]{1,0:T(8,128)(2,1)S(1)}, u32[]{:S(2)}, u32[]{:S(2)}) collective-permute-start(bf16[512,512]{1,0:T(8,128)(2,1)S(1)} %constant_dynamic-update-slice_fusion.refs_6_), channel_id=1, source_target_pairs={{0,8},{8,16},{16,24},{24,0},{1,9},{9,17},{17,25},{25,1},{2,10},{10... | collective-permute-start | bytes 1572872 | tf_op jit(solution)/shard_map/ppermute | solution.py:223
  46.8 4.4 %collective-permute-start.3 = (bf16[512,512]{1,0:T(8,128)(2,1)S(1)}, bf16[512,512]{1,0:T(8,128)(2,1)S(1)}, u32[]{:S(2)}, u32[]{:S(2)}) collective-permute-start(bf16[512,512]{1,0:T(8,128)(2,1)S(1)} %constant_dynamic-update-slice_fusion.refs_6_), channel_id=1, source_target_pairs={{0,16},{8,24},{16,0},{24,8},{1,17},{9,25},{17,1},{25,9},{2,18},{10... | collective-permute-start | bytes 1572872 | tf_op jit(solution)/shard_map/ppermute | solution.py:223
  51.2 3.1 %collective-permute-start.1 = (bf16[512,512]{1,0:T(8,128)(2,1)S(1)}, bf16[512,512]{1,0:T(8,128)(2,1)S(1)}, u32[]{:S(2)}, u32[]{:S(2)}) collective-permute-start(bf16[512,512]{1,0:T(8,128)(2,1)S(1)} %constant_dynamic-update-slice_fusion.refs_6_), channel_id=1, source_target_pairs={{0,24},{8,0},{16,8},{24,16},{1,25},{9,1},{17,9},{25,17},{2,26},{10... | collective-permute-start | bytes 1572872 | tf_op jit(solution)/shard_map/ppermute | solution.py:223
  54.2 2.2 %collective-permute-start.6 = (bf16[512,512]{1,0:T(8,128)(2,1)S(1)}, bf16[512,512]{1,0:T(8,128)(2,1)S(1)}, u32[]{:S(2)}, u32[]{:S(2)}) collective-permute-start(bf16[512,512]{1,0:T(8,128)(2,1)S(1)} %collective-permute-done.refs_7_), channel_id=1, source_target_pairs={{0,8},{8,16},{16,24},{24,0},{1,9},{9,17},{17,25},{25,1},{2,10},{10... | collective-permute-start | bytes 1572872 | tf_op jit(solution)/shard_map/ppermute | solution.py:223
  56.5 2.8 %collective-permute-start.4 = (bf16[512,512]{1,0:T(8,128)(2,1)S(1)}, bf16[512,512]{1,0:T(8,128)(2,1)}, u32[]{:S(2)}, u32[]{:S(2)}) collective-permute-start(bf16[512,512]{1,0:T(8,128)(2,1)S(1)} %collective-permute-done.refs_7_), channel_id=1, source_target_pairs={{0,16},{8,24},{16,0},{24,8},{1,17},{9,25},{17,1},{25,9},{2,18},{10... | collective-permute-start | bytes 1572872 | tf_op jit(solution)/shard_map/ppermute | solution.py:223
  60.1 4.6 %collective-permute-start.2 = (bf16[512,512]{1,0:T(8,128)(2,1)S(1)}, bf16[512,512]{1,0:T(8,128)(2,1)}, u32[]{:S(2)}, u32[]{:S(2)}) collective-permute-start(bf16[512,512]{1,0:T(8,128)(2,1)S(1)} %collective-permute-done.refs_7_), channel_id=1, source_target_pairs={{0,24},{8,0},{16,8},{24,16},{1,25},{9,1},{17,9},{25,17},{2,26},{10... | collective-permute-start | bytes 1572872 | tf_op jit(solution)/shard_map/ppermute | solution.py:223
  65.1 1.3 pad_add_fusion.refs_0_
  66.3 4.4 %collective-permute-done.3.refs_10_ = bf16[512,512]{1,0:T(8,128)(2,1)S(1)} collective-permute-done((bf16[512,512]{1,0:T(8,128)(2,1)S(1)}, bf16[512,512]{1,0:T(8,128)(2,1)S(1)}, u32[]{:S(2)}, u32[]{:S(2)}) %collective-permute-start.3) | collective-permute-done | bytes 524320 | tf_op jit(solution)/shard_map/ppermute | solution.py:223
  70.7 6.3 %collective-permute-done.1.refs_8_ = bf16[512,512]{1,0:T(8,128)(2,1)S(1)} collective-permute-done((bf16[512,512]{1,0:T(8,128)(2,1)S(1)}, bf16[512,512]{1,0:T(8,128)(2,1)S(1)}, u32[]{:S(2)}, u32[]{:S(2)}) %collective-permute-start.1) | collective-permute-done | bytes 524320 | tf_op jit(solution)/shard_map/ppermute | solution.py:223
  77.1 5.6 %collective-permute-done.6.refs_13_ = bf16[512,512]{1,0:T(8,128)(2,1)S(1)} collective-permute-done((bf16[512,512]{1,0:T(8,128)(2,1)S(1)}, bf16[512,512]{1,0:T(8,128)(2,1)S(1)}, u32[]{:S(2)}, u32[]{:S(2)}) %collective-permute-start.6) | collective-permute-done | bytes 524320 | tf_op jit(solution)/shard_map/ppermute | solution.py:223
  82.7 10.5 %collective-permute-done.4.refs_11_ = bf16[512,512]{1,0:T(8,128)(2,1)} collective-permute-done((bf16[512,512]{1,0:T(8,128)(2,1)S(1)}, bf16[512,512]{1,0:T(8,128)(2,1)}, u32[]{:S(2)}, u32[]{:S(2)}) %collective-permute-start.4) | collective-permute-done | bytes 524320 | tf_op jit(solution)/shard_map/ppermute | solution.py:223
  93.2 2.6 %collective-permute-done.2.refs_9_ = bf16[512,512]{1,0:T(8,128)(2,1)} collective-permute-done((bf16[512,512]{1,0:T(8,128)(2,1)S(1)}, bf16[512,512]{1,0:T(8,128)(2,1)}, u32[]{:S(2)}, u32[]{:S(2)}) %collective-permute-start.2) | collective-permute-done | bytes 524320 | tf_op jit(solution)/shard_map/ppermute | solution.py:223
  95.8 16.9 %all-gather.3.cloned.1.call-done = bf16[4096,512]{1,0:T(8,128)(2,1)} async-done(((bf16[512,512]{1,0:T(8,128)(2,1)}), bf16[4096,512]{1,0:T(8,128)(2,1)}) %all-gather.3.cloned.1.call-update) | async-done | bytes 4194320 | tf_op jit(solution)/shard_map/all_gather | solution.py:216
  112.8 16.6 %remote.1 = (bf16[8,256,512]{2,1,0:T(8,128)(2,1)}, f32[512,512]{1,0:T(8,128)}, f32[512,512]{1,0:T(8,128)}, bf16[512,512]{1,0:T(8,128)(2,1)}, bf16[512,512]{1,0:T...) custom-call(s32[130]{0:T(256)} %pad_add_fusion.refs_0_, ...), custom_call_target="tpu_custom_call" | custom-call | tf_op jit(solution)/shard_map/remote/pallas_call | solution.py:181
  129.4 8.2 %collective-permute-start.8 = (bf16[512,512]{1,0:T(8,128)(2,1)}, bf16[512,512]{1,0:T(8,128)(2,1)S(1)}, u32[]{:S(2)}, u32[]{:S(2)}) collective-permute-start(bf16[512,512]{1,0:T(8,128)(2,1)} %get-tuple-element.64), channel_id=1, source_target_pairs={{0,24},{8,0},{16,8},{24,16},{1,25},{9,1},{17,9},{25,17},{2,26},{10... | collective-permute-start | bytes 1572872 | tf_op jit(solution)/shard_map/ppermute | solution.py:252
  137.6 1.9 collective-permute-start.11
  139.5 1.9 collective-permute-start.7
  141.4 7.0 %collective-permute-done.8 = bf16[512,512]{1,0:T(8,128)(2,1)S(1)} collective-permute-done((bf16[512,512]{1,0:T(8,128)(2,1)}, bf16[512,512]{1,0:T(8,128)(2,1)S(1)}, u32[]{:S(2)}, u32[]{:S(2)}) %collective-permute-start.8) | collective-permute-done | bytes 524320 | tf_op jit(solution)/shard_map/ppermute | solution.py:252
  149.6 5.3 %collective-permute-start.9 = (bf16[512,512]{1,0:T(8,128)(2,1)S(1)}, bf16[512,512]{1,0:T(8,128)(2,1)S(1)}, u32[]{:S(2)}, u32[]{:S(2)}) collective-permute-start(bf16[512,512]{1,0:T(8,128)(2,1)S(1)} %add_convert_fusion.3), channel_id=1, source_target_pairs={{0,24},{8,0},{16,8},{24,16},{1,25},{9,1},{17,9},{25,17},{2,26},{10... | collective-permute-start | bytes 1572872 | tf_op jit(solution)/shard_map/ppermute | solution.py:258
  154.9 1.9 collective-permute-start.10
  156.8 1.2 add_convert_fusion.1
  158.0 3.4 %collective-permute-start.12 = (bf16[512,512]{1,0:T(8,128)(2,1)S(1)}, bf16[512,512]{1,0:T(8,128)(2,1)S(1)}, u32[]{:S(2)}, u32[]{:S(2)}) collective-permute-start(bf16[512,512]{1,0:T(8,128)(2,1)S(1)} %add_convert_fusion.1), channel_id=1, source_target_pairs={{0,8},{8,16},{16,24},{24,0},{1,9},{9,17},{17,25},{25,1},{2,10},{10... | collective-permute-start | bytes 1572872 | tf_op jit(solution)/shard_map/ppermute | solution.py:257
  161.4 3.3 %collective-permute-done.7 = bf16[512,512]{1,0:T(8,128)(2,1)S(1)} collective-permute-done((bf16[512,512]{1,0:T(8,128)(2,1)}, bf16[512,512]{1,0:T(8,128)(2,1)S(1)}, u32[]{:S(2)}, u32[]{:S(2)}) %collective-permute-start.7) | collective-permute-done | bytes 524320 | tf_op jit(solution)/shard_map/ppermute | solution.py:253
  164.9 11.0 %collective-permute-done.10 = bf16[512,512]{1,0:T(8,128)(2,1)S(1)} collective-permute-done((bf16[512,512]{1,0:T(8,128)(2,1)}, bf16[512,512]{1,0:T(8,128)(2,1)S(1)}, u32[]{:S(2)}, u32[]{:S(2)}) %collective-permute-start.10) | collective-permute-done | bytes 524320 | tf_op jit(solution)/shard_map/ppermute | solution.py:254
  176.2 15.4 %reduce-scatter.2.cloned.1.call-done = bf16[1,256,512]{2,1,0:T(8,128)(2,1)} async-done(((bf16[8,256,512]{2,1,0:T(8,128)(2,1)}), bf16[1,256,512]{2,1,0:T(8,128)(2,1)}) %reduce-scatter.2.cloned.1.call-update) | async-done | bytes 262160 | tf_op jit(solution)/shard_map/reduce_scatter | solution.py:244
  191.5 2.6 %collective-permute-start.13 = (bf16[512,512]{1,0:T(8,128)(2,1)S(1)}, bf16[512,512]{1,0:T(8,128)(2,1)S(1)}, u32[]{:S(2)}, u32[]{:S(2)}) collective-permute-start(bf16[512,512]{1,0:T(8,128)(2,1)S(1)} %add_convert_fusion.2), channel_id=1, source_target_pairs={{0,32},{32,0},{1,33},{33,1},{2,34},{34,2},{3,35},{35,3},{4,36},{36... | collective-permute-start | bytes 1572872 | tf_op jit(solution)/shard_map/ppermute | solution.py:260
  194.1 13.5 %all_to_all.24 = bf16[8,32,512]{2,1,0:T(8,128)(2,1)S(1)} all-to-all(bf16[8,32,512]{2,1,0:T(8,128)(2,1)} %bitcast.13), channel_id=1, replica_groups=mesh['j'=8,'p'=2,'x'=4,'head'=8] {'head'}, dimensions={0} | all-to-all | bytes 524288 | tf_op jit(solution)/shard_map/all_to_all | solution.py:264
  (48 shorter events, 8.8 us)
Async XLA Ops:
  7.2 105.6 %all-gather.3.cloned.1.call-start = ((), (), s32[]{:S(2)}) async-start(), calls=%async_computation.4 | async-start | bytes 4718592 | tf_op jit(solution)/shard_map/all_gather | solution.py:216
  11.0 101.7 %copy-start = (bf16[512,512]{1,0:T(8,128)(2,1)}, bf16[512,512]{1,0:T(8,128)(2,1)S(1)}, u32[]{:S(2)}) copy-start(bf16[512,512]{1,0:T(8,128)(2,1)S(1)} %constant_dynamic-update-slice_fusion.refs_6_) | copy-start | bytes 1572868
  11.1 11.4 %collective-permute-start = (bf16[512,512]{1,0:T(8,128)(2,1)S(1)}, bf16[512,512]{1,0:T(8,128)(2,1)S(1)}, u32[]{:S(2)}, u32[]{:S(2)}) collective-permute-start(bf16[512,512]{1,0:T(8,128)(2,1)S(1)} %constant_dynamic-update-slice_fusion.refs_6_), channel_id=1, source_target_pairs={{0,32},{32,0},{1,33},{33,1},{2,34},{34,2},{3,35},{35,3},{4,36},{36... | collective-permute-start | bytes 1572872 | tf_op jit(solution)/shard_map/ppermute | solution.py:219
  22.5 90.2 %copy-start.3 = (bf16[512,512]{1,0:T(8,128)(2,1)}, bf16[512,512]{1,0:T(8,128)(2,1)S(1)}, u32[]{:S(2)}) copy-start(bf16[512,512]{1,0:T(8,128)(2,1)S(1)} %collective-permute-done.refs_7_) | copy-start | bytes 1572868
  24.7 34.5 %all-to-all-start = ((f32[8,24,128]{2,1,0:T(8,128)}), f32[8,24,128]{2,1,0:T(8,128)S(1)}, u32[]{:S(2)}, u32[]{:S(2)}) async-start(f32[8,24,128]{2,1,0:T(8,128)} %broadcast_in_dim.14), calls=%async_computation | async-start | bytes 196608 | tf_op jit(solution)/shard_map/all_to_all | solution.py:234
  43.6 147.9 %reduce-scatter.2.cloned.1.call-start = ((), (), s32[]{:S(2)}) async-start(), calls=%async_computation.3 | async-start | bytes 2359296 | tf_op jit(solution)/shard_map/reduce_scatter | solution.py:244
  43.7 16.4 %collective-permute-start.5 = (bf16[512,512]{1,0:T(8,128)(2,1)S(1)}, bf16[512,512]{1,0:T(8,128)(2,1)S(1)}, u32[]{:S(2)}, u32[]{:S(2)}) collective-permute-start(bf16[512,512]{1,0:T(8,128)(2,1)S(1)} %constant_dynamic-update-slice_fusion.refs_6_), channel_id=1, source_target_pairs={{0,8},{8,16},{16,24},{24,0},{1,9},{9,17},{17,25},{25,1},{2,10},{10... | collective-permute-start | bytes 1572872 | tf_op jit(solution)/shard_map/ppermute | solution.py:223
  46.8 23.9 %collective-permute-start.3 = (bf16[512,512]{1,0:T(8,128)(2,1)S(1)}, bf16[512,512]{1,0:T(8,128)(2,1)S(1)}, u32[]{:S(2)}, u32[]{:S(2)}) collective-permute-start(bf16[512,512]{1,0:T(8,128)(2,1)S(1)} %constant_dynamic-update-slice_fusion.refs_6_), channel_id=1, source_target_pairs={{0,16},{8,24},{16,0},{24,8},{1,17},{9,25},{17,1},{25,9},{2,18},{10... | collective-permute-start | bytes 1572872 | tf_op jit(solution)/shard_map/ppermute | solution.py:223
  51.2 25.9 %collective-permute-start.1 = (bf16[512,512]{1,0:T(8,128)(2,1)S(1)}, bf16[512,512]{1,0:T(8,128)(2,1)S(1)}, u32[]{:S(2)}, u32[]{:S(2)}) collective-permute-start(bf16[512,512]{1,0:T(8,128)(2,1)S(1)} %constant_dynamic-update-slice_fusion.refs_6_), channel_id=1, source_target_pairs={{0,24},{8,0},{16,8},{24,16},{1,25},{9,1},{17,9},{25,17},{2,26},{10... | collective-permute-start | bytes 1572872 | tf_op jit(solution)/shard_map/ppermute | solution.py:223
  54.2 28.5 %collective-permute-start.6 = (bf16[512,512]{1,0:T(8,128)(2,1)S(1)}, bf16[512,512]{1,0:T(8,128)(2,1)S(1)}, u32[]{:S(2)}, u32[]{:S(2)}) collective-permute-start(bf16[512,512]{1,0:T(8,128)(2,1)S(1)} %collective-permute-done.refs_7_), channel_id=1, source_target_pairs={{0,8},{8,16},{16,24},{24,0},{1,9},{9,17},{17,25},{25,1},{2,10},{10... | collective-permute-start | bytes 1572872 | tf_op jit(solution)/shard_map/ppermute | solution.py:223
  56.5 36.7 %collective-permute-start.4 = (bf16[512,512]{1,0:T(8,128)(2,1)S(1)}, bf16[512,512]{1,0:T(8,128)(2,1)}, u32[]{:S(2)}, u32[]{:S(2)}) collective-permute-start(bf16[512,512]{1,0:T(8,128)(2,1)S(1)} %collective-permute-done.refs_7_), channel_id=1, source_target_pairs={{0,16},{8,24},{16,0},{24,8},{1,17},{9,25},{17,1},{25,9},{2,18},{10... | collective-permute-start | bytes 1572872 | tf_op jit(solution)/shard_map/ppermute | solution.py:223
  59.3 53.5 %copy-start.8 = (f32[8,24,128]{2,1,0:T(8,128)}, f32[8,24,128]{2,1,0:T(8,128)S(1)}, u32[]{:S(2)}) copy-start(f32[8,24,128]{2,1,0:T(8,128)S(1)} %all-to-all-done.refs_1_) | copy-start | bytes 294916
  60.1 52.6 %copy-start.4 = (bf16[512,512]{1,0:T(8,128)(2,1)}, bf16[512,512]{1,0:T(8,128)(2,1)S(1)}, u32[]{:S(2)}) copy-start(bf16[512,512]{1,0:T(8,128)(2,1)S(1)} %collective-permute-done.5.refs_12_) | copy-start | bytes 1572868
  60.1 35.7 %collective-permute-start.2 = (bf16[512,512]{1,0:T(8,128)(2,1)S(1)}, bf16[512,512]{1,0:T(8,128)(2,1)}, u32[]{:S(2)}, u32[]{:S(2)}) collective-permute-start(bf16[512,512]{1,0:T(8,128)(2,1)S(1)} %collective-permute-done.refs_7_), channel_id=1, source_target_pairs={{0,24},{8,0},{16,8},{24,16},{1,25},{9,1},{17,9},{25,17},{2,26},{10... | collective-permute-start | bytes 1572872 | tf_op jit(solution)/shard_map/ppermute | solution.py:223
  70.7 42.0 %copy-start.5 = (bf16[512,512]{1,0:T(8,128)(2,1)}, bf16[512,512]{1,0:T(8,128)(2,1)S(1)}, u32[]{:S(2)}) copy-start(bf16[512,512]{1,0:T(8,128)(2,1)S(1)} %collective-permute-done.3.refs_10_) | copy-start | bytes 1572868
  77.1 35.7 %copy-start.6 = (bf16[512,512]{1,0:T(8,128)(2,1)}, bf16[512,512]{1,0:T(8,128)(2,1)S(1)}, u32[]{:S(2)}) copy-start(bf16[512,512]{1,0:T(8,128)(2,1)S(1)} %collective-permute-done.1.refs_8_) | copy-start | bytes 1572868
  82.7 30.1 %copy-start.7 = (bf16[512,512]{1,0:T(8,128)(2,1)}, bf16[512,512]{1,0:T(8,128)(2,1)S(1)}, u32[]{:S(2)}) copy-start(bf16[512,512]{1,0:T(8,128)(2,1)S(1)} %collective-permute-done.6.refs_13_) | copy-start | bytes 1572868
  129.3 35.4 %copy-start.2 = (f32[512,512]{1,0:T(8,128)S(1)}, f32[512,512]{1,0:T(8,128)}, u32[]{:S(2)}) copy-start(f32[512,512]{1,0:T(8,128)} %get-tuple-element.61) | copy-start | bytes 3145732
  129.3 46.6 %copy-start.1 = (f32[512,512]{1,0:T(8,128)S(1)}, f32[512,512]{1,0:T(8,128)}, u32[]{:S(2)}) copy-start(f32[512,512]{1,0:T(8,128)} %get-tuple-element.65) | copy-start | bytes 3145732
  129.4 19.1 %collective-permute-start.8 = (bf16[512,512]{1,0:T(8,128)(2,1)}, bf16[512,512]{1,0:T(8,128)(2,1)S(1)}, u32[]{:S(2)}, u32[]{:S(2)}) collective-permute-start(bf16[512,512]{1,0:T(8,128)(2,1)} %get-tuple-element.64), channel_id=1, source_target_pairs={{0,24},{8,0},{16,8},{24,16},{1,25},{9,1},{17,9},{25,17},{2,26},{10... | collective-permute-start | bytes 1572872 | tf_op jit(solution)/shard_map/ppermute | solution.py:252
  137.6 19.3 %collective-permute-start.11 = (bf16[512,512]{1,0:T(8,128)(2,1)}, bf16[512,512]{1,0:T(8,128)(2,1)S(1)}, u32[]{:S(2)}, u32[]{:S(2)}) collective-permute-start(bf16[512,512]{1,0:T(8,128)(2,1)} %get-tuple-element.68), channel_id=1, source_target_pairs={{0,8},{8,16},{16,24},{24,0},{1,9},{9,17},{17,25},{25,1},{2,10},{10... | collective-permute-start | bytes 1572872 | tf_op jit(solution)/shard_map/ppermute | solution.py:251
  139.5 25.2 %collective-permute-start.7 = (bf16[512,512]{1,0:T(8,128)(2,1)}, bf16[512,512]{1,0:T(8,128)(2,1)S(1)}, u32[]{:S(2)}, u32[]{:S(2)}) collective-permute-start(bf16[512,512]{1,0:T(8,128)(2,1)} %get-tuple-element.62), channel_id=1, source_target_pairs={{0,8},{8,16},{16,24},{24,0},{1,9},{9,17},{17,25},{25,1},{2,10},{10... | collective-permute-start | bytes 1572872 | tf_op jit(solution)/shard_map/ppermute | solution.py:253
  149.6 15.1 %collective-permute-start.9 = (bf16[512,512]{1,0:T(8,128)(2,1)S(1)}, bf16[512,512]{1,0:T(8,128)(2,1)S(1)}, u32[]{:S(2)}, u32[]{:S(2)}) collective-permute-start(bf16[512,512]{1,0:T(8,128)(2,1)S(1)} %add_convert_fusion.3), channel_id=1, source_target_pairs={{0,24},{8,0},{16,8},{24,16},{1,25},{9,1},{17,9},{25,17},{2,26},{10... | collective-permute-start | bytes 1572872 | tf_op jit(solution)/shard_map/ppermute | solution.py:258
  154.9 21.0 %collective-permute-start.10 = (bf16[512,512]{1,0:T(8,128)(2,1)}, bf16[512,512]{1,0:T(8,128)(2,1)S(1)}, u32[]{:S(2)}, u32[]{:S(2)}) collective-permute-start(bf16[512,512]{1,0:T(8,128)(2,1)} %get-tuple-element.66), channel_id=1, source_target_pairs={{0,24},{8,0},{16,8},{24,16},{1,25},{9,1},{17,9},{25,17},{2,26},{10... | collective-permute-start | bytes 1572872 | tf_op jit(solution)/shard_map/ppermute | solution.py:254
  158.0 17.9 %collective-permute-start.12 = (bf16[512,512]{1,0:T(8,128)(2,1)S(1)}, bf16[512,512]{1,0:T(8,128)(2,1)S(1)}, u32[]{:S(2)}, u32[]{:S(2)}) collective-permute-start(bf16[512,512]{1,0:T(8,128)(2,1)S(1)} %add_convert_fusion.1), channel_id=1, source_target_pairs={{0,8},{8,16},{16,24},{24,0},{1,9},{9,17},{17,25},{25,1},{2,10},{10... | collective-permute-start | bytes 1572872 | tf_op jit(solution)/shard_map/ppermute | solution.py:257
  191.5 16.8 %collective-permute-start.13 = (bf16[512,512]{1,0:T(8,128)(2,1)S(1)}, bf16[512,512]{1,0:T(8,128)(2,1)S(1)}, u32[]{:S(2)}, u32[]{:S(2)}) collective-permute-start(bf16[512,512]{1,0:T(8,128)(2,1)S(1)} %add_convert_fusion.2), channel_id=1, source_target_pairs={{0,32},{32,0},{1,33},{33,1},{2,34},{34,2},{3,35},{35,3},{4,36},{36... | collective-permute-start | bytes 1572872 | tf_op jit(solution)/shard_map/ppermute | solution.py:260
Sparse Core Ops, SparseCore 0:
  10.1 102.5 all-gather.2
  129.5 61.9 reduce-scatter.1

commit v7 on v6

--- a/solution.py
+++ b/solution.py
@@ -12,7 +12,7 @@
 BLOCK = 128
 PER_PEER = 2
 PAIR = 2
-UNROLL = 8
+TURN_SIZES = (16, 4)
 F32 = jnp.float32
 BF16 = jnp.bfloat16
 PARAMS = pltpu.CompilerParams(vmem_limit_bytes=56 * 1024 * 1024)
@@ -79,7 +79,7 @@
 
 
 def remote_kernel(blocks, heads, factor, owners, *refs):
-    slots_ref, stat_ref, own_q_ref, packs_ref, own_k_ref, own_v_ref = refs[:6]
+    slots_ref, stat_ref, own_q_ref, own_k_ref, own_v_ref, packs_ref = refs[:6]
     kv_refs = refs[6 : 6 + owners]
     dq_out, *part_outs = refs[6 + owners : 7 + 2 * owners]
     dq_ref, acc_ref, far_ref, line_ref, pack_ref, kv_ref, sems = refs[7 + 2 * owners :]
@@ -87,8 +87,6 @@
     span = blocks * owners
     loads = [
         pltpu.make_async_copy(packs_ref, pack_ref, sems.at[owners]),
-        pltpu.make_async_copy(own_k_ref, acc_ref.at[0, pl.ds(0, rows)], sems.at[owners + 1]),
-        pltpu.make_async_copy(own_v_ref, acc_ref.at[0, pl.ds(rows, rows)], sems.at[owners + 2]),
     ]
     for at in range(owners):
         loads.append(pltpu.make_async_copy(kv_refs[at], kv_ref.at[at], sems.at[at]))
@@ -98,14 +96,16 @@
     mine = slots_ref[slots_ref.shape[0] - 1]
     dq_ref[...] = jnp.zeros_like(dq_ref)
     dq_ref[mine] = own_q_ref[...].astype(BF16)
+    acc_ref[0, :rows] = own_k_ref[...]
+    acc_ref[0, rows:] = own_v_ref[...]
     acc_ref[1:] = jnp.zeros((owners - 1, *acc_ref.shape[1:]), F32)
     for load in loads:
         load.wait()
 
-    def turn(step, carry):
+    def turn(first, size):
         done = []
-        for u in range(UNROLL):
-            slot = step * UNROLL + u
+        for u in range(size):
+            slot = first + u
             live = slot < count
             code = slots_ref[1 + jnp.where(live, slot, count - 1)]
             kb, rest = low_bits(code, blocks)
@@ -141,9 +141,18 @@
             total = jnp.where(same, line_ref[...], start) + grad_q
             line_ref[...] = total
             dq_ref[zq, q_at, cols] = total.astype(BF16)
-        return carry
-
-    lax.fori_loop(0, (count + UNROLL - 1) // UNROLL, turn, 0)
+
+    large, small = TURN_SIZES
+    full, rest = low_bits(count, large)[::-1]
+
+    @pl.loop(0, full)
+    def _(step):
+        turn(step * large, large)
+
+    @pl.loop(0, low_bits(rest + small - 1, small)[1])
+    def _(step):
+        turn(full * large + step * small, small)
+
     stores = [pltpu.make_async_copy(dq_ref, dq_out, sems.at[owners])]
     for at in range(PAIR):
         stores.append(pltpu.make_async_copy(acc_ref.at[at], part_outs[at], sems.at[at]))
@@ -181,8 +190,8 @@
     return pl.pallas_call(
         functools.partial(remote_kernel, blocks, heads, factor, owners),
         in_specs=[pl.BlockSpec(memory_space=pltpu.SMEM)]
-        + [pl.BlockSpec(memory_space=pltpu.VMEM)] * 2
-        + [anywhere] * (3 + owners),
+        + [pl.BlockSpec(memory_space=pltpu.VMEM)] * 4
+        + [anywhere] * (1 + owners),
         out_specs=(anywhere,) * (1 + owners),
         out_shape=(jax.ShapeDtypeStruct((ring, rows, width), BF16),)
         + (jax.ShapeDtypeStruct(part, F32),) * PAIR
@@ -194,11 +203,11 @@
             pltpu.VMEM((BLOCK, BLOCK), F32),
             pltpu.VMEM((ring, 2 * rows, width), BF16),
             pltpu.VMEM((owners, *part), BF16),
-            pltpu.SemaphoreType.DMA((owners + 3,)),
+            pltpu.SemaphoreType.DMA((owners + 1,)),
         ],
         compiler_params=PARAMS,
         name="remote",
-    )(codes, stats, own_q, packs, own_k, own_v, *kvs)
+    )(codes, stats, own_q, own_k, own_v, packs, *kvs)
 
 
 def shards(queries, keys, values, out_grad, outputs, log_norms, selected):

time: 218 us -> 217 us (level)
  transfers between devices with their start and end apart: 17 -> 17, of which waited for: 11 -> 12; matrix products, arithmetic and copies ran while one was open for 5% -> 5% of each run, Pallas kernels for 2% -> 2%
where the time goes in v7:
time: 217 us; the launch traced here: 216 us
  waiting for transfers between devices  86.3 us (40%)
  starting transfers between devices  69.9 us (32%)
  Pallas kernels  20.3 us (9%)
  blocking collectives  14.4 us (7%)
  between operations  14.3 us (7%)
  other arithmetic  6.64 us (3%)
  local copies, waits for them, and re-layouts  4.45 us (2%)
    ppermute x6, waiting for transfers between devices, shards(): kvs += [lax.ppermute(both, 'x', back), lax.ppermute(swapped, 'x', back)]  29.5 us
    ppermute x6, starting transfers between devices, shards(): kvs += [lax.ppermute(both, 'x', back), lax.ppermute(swapped, 'x', back)]  20.2 us
    all_to_all x1, starting transfers between devices, shards(): lax.all_to_all(jnp.broadcast_to(info[None], (ring, *info.shape)), 'j', 0,...  18.9 us
    all_gather x1, waiting for transfers between devices, shards(): packs = lax.all_gather(pack, 'j')  16.9 us
    reduce_scatter x1, waiting for transfers between devices, shards(): sum_q = lax.psum_scatter(part_q, 'j', scatter_dimension=0)  15 us
    pallas_call x1, Pallas kernels, remote_call(): pl.pallas_call(functools.partial(remote_kernel, blocks, heads, factor, ow...  14.9 us
    all_to_all x1, blocking collectives, shards(): lax.all_to_all(sum_q, 'head', split_axis=0, concat_axis=1, tiled=True)  14.4 us
    ppermute x1, waiting for transfers between devices, shards(): from_last = lax.ppermute(last_a, 'x', behind)  11 us
  transfers between devices with their start and end apart: 17, of which 12 were waited for; matrix products, arithmetic and copies ran while one was open for 5% of the time, Pallas kernels for 2%

profile of v7, /device:TPU:1, one launch (start us, length us, event | category | flops | bytes accessed | tf_op | source)
XLA Modules:
  0.0 216.2 jit_solution(17531807335670593862)
XLA Ops:
  7.2 1.9 pack.1
  11.1 4.4 %collective-permute-start = (bf16[512,512]{1,0:T(8,128)(2,1)S(1)}, bf16[512,512]{1,0:T(8,128)(2,1)S(1)}, u32[]{:S(2)}, u32[]{:S(2)}) collective-permute-start(bf16[512,512]{1,0:T(8,128)(2,1)S(1)} %constant_dynamic-update-slice_fusion.refs_6_), channel_id=1, source_target_pairs={{0,32},{32,0},{1,33},{33,1},{2,34},{34,2},{3,35},{35,3},{4,36},{36... | collective-permute-start | bytes 1572872 | tf_op jit(solution)/shard_map/ppermute | solution.py:228
  15.4 3.5 %own.1 = (f32[16,128]{1,0:T(8,128)}, f32[256,512]{1,0:T(8,128)}, f32[256,512]{1,0:T(8,128)}, f32[256,512]{1,0:T(8,128)}) custom-call(bf16[256,512]{1,0:T(8,128)(2,1)} %q_ref.3, bf16[256,512]{1,0:T(8,128)(2,1)} %g_ref.3, bf16[256,512]{1,0:T(8,128)(2,1)} %o_ref.1, f32[4,256]{1,0:T(4,128)} %bitcast.15, bf16[256,512]{1,0:T(8,128)(2,1)} %k_ref, bf16[256,512]{1,0:T(8,128)(2,1)} %v_ref), custom_call_target="tpu_custom_call" | custom-call | tf_op jit(solution)/shard_map/own/pallas_call | solution.py:234
  19.0 3.5 %collective-permute-done.refs_7_ = bf16[512,512]{1,0:T(8,128)(2,1)S(1)} collective-permute-done((bf16[512,512]{1,0:T(8,128)(2,1)S(1)}, bf16[512,512]{1,0:T(8,128)(2,1)S(1)}, u32[]{:S(2)}, u32[]{:S(2)}) %collective-permute-start) | collective-permute-done | bytes 524320 | tf_op jit(solution)/shard_map/ppermute | solution.py:228
  24.7 18.9 %all-to-all-start = ((f32[8,24,128]{2,1,0:T(8,128)}), f32[8,24,128]{2,1,0:T(8,128)S(1)}, u32[]{:S(2)}, u32[]{:S(2)}) async-start(f32[8,24,128]{2,1,0:T(8,128)} %broadcast_in_dim.14), calls=%async_computation | async-start | bytes 196608 | tf_op jit(solution)/shard_map/all_to_all | solution.py:243
  43.7 3.1 %collective-permute-start.5 = (bf16[512,512]{1,0:T(8,128)(2,1)S(1)}, bf16[512,512]{1,0:T(8,128)(2,1)S(1)}, u32[]{:S(2)}, u32[]{:S(2)}) collective-permute-start(bf16[512,512]{1,0:T(8,128)(2,1)S(1)} %constant_dynamic-update-slice_fusion.refs_6_), channel_id=1, source_target_pairs={{0,8},{8,16},{16,24},{24,0},{1,9},{9,17},{17,25},{25,1},{2,10},{10... | collective-permute-start | bytes 1572872 | tf_op jit(solution)/shard_map/ppermute | solution.py:232
  46.8 4.4 %collective-permute-start.3 = (bf16[512,512]{1,0:T(8,128)(2,1)S(1)}, bf16[512,512]{1,0:T(8,128)(2,1)S(1)}, u32[]{:S(2)}, u32[]{:S(2)}) collective-permute-start(bf16[512,512]{1,0:T(8,128)(2,1)S(1)} %constant_dynamic-update-slice_fusion.refs_6_), channel_id=1, source_target_pairs={{0,16},{8,24},{16,0},{24,8},{1,17},{9,25},{17,1},{25,9},{2,18},{10... | collective-permute-start | bytes 1572872 | tf_op jit(solution)/shard_map/ppermute | solution.py:232
  51.2 3.1 %collective-permute-start.1 = (bf16[512,512]{1,0:T(8,128)(2,1)S(1)}, bf16[512,512]{1,0:T(8,128)(2,1)S(1)}, u32[]{:S(2)}, u32[]{:S(2)}) collective-permute-start(bf16[512,512]{1,0:T(8,128)(2,1)S(1)} %constant_dynamic-update-slice_fusion.refs_6_), channel_id=1, source_target_pairs={{0,24},{8,0},{16,8},{24,16},{1,25},{9,1},{17,9},{25,17},{2,26},{10... | collective-permute-start | bytes 1572872 | tf_op jit(solution)/shard_map/ppermute | solution.py:232
  54.2 2.2 %collective-permute-start.6 = (bf16[512,512]{1,0:T(8,128)(2,1)S(1)}, bf16[512,512]{1,0:T(8,128)(2,1)S(1)}, u32[]{:S(2)}, u32[]{:S(2)}) collective-permute-start(bf16[512,512]{1,0:T(8,128)(2,1)S(1)} %collective-permute-done.refs_7_), channel_id=1, source_target_pairs={{0,8},{8,16},{16,24},{24,0},{1,9},{9,17},{17,25},{25,1},{2,10},{10... | collective-permute-start | bytes 1572872 | tf_op jit(solution)/shard_map/ppermute | solution.py:232
  56.5 2.8 %collective-permute-start.4 = (bf16[512,512]{1,0:T(8,128)(2,1)S(1)}, bf16[512,512]{1,0:T(8,128)(2,1)}, u32[]{:S(2)}, u32[]{:S(2)}) collective-permute-start(bf16[512,512]{1,0:T(8,128)(2,1)S(1)} %collective-permute-done.refs_7_), channel_id=1, source_target_pairs={{0,16},{8,24},{16,0},{24,8},{1,17},{9,25},{17,1},{25,9},{2,18},{10... | collective-permute-start | bytes 1572872 | tf_op jit(solution)/shard_map/ppermute | solution.py:232
  60.1 4.6 %collective-permute-start.2 = (bf16[512,512]{1,0:T(8,128)(2,1)S(1)}, bf16[512,512]{1,0:T(8,128)(2,1)}, u32[]{:S(2)}, u32[]{:S(2)}) collective-permute-start(bf16[512,512]{1,0:T(8,128)(2,1)S(1)} %collective-permute-done.refs_7_), channel_id=1, source_target_pairs={{0,24},{8,0},{16,8},{24,16},{1,25},{9,1},{17,9},{25,17},{2,26},{10... | collective-permute-start | bytes 1572872 | tf_op jit(solution)/shard_map/ppermute | solution.py:232
  65.1 1.3 pad_add_fusion.refs_0_
  66.3 4.4 %collective-permute-done.3.refs_10_ = bf16[512,512]{1,0:T(8,128)(2,1)S(1)} collective-permute-done((bf16[512,512]{1,0:T(8,128)(2,1)S(1)}, bf16[512,512]{1,0:T(8,128)(2,1)S(1)}, u32[]{:S(2)}, u32[]{:S(2)}) %collective-permute-start.3) | collective-permute-done | bytes 524320 | tf_op jit(solution)/shard_map/ppermute | solution.py:232
  70.7 6.3 %collective-permute-done.1.refs_8_ = bf16[512,512]{1,0:T(8,128)(2,1)S(1)} collective-permute-done((bf16[512,512]{1,0:T(8,128)(2,1)S(1)}, bf16[512,512]{1,0:T(8,128)(2,1)S(1)}, u32[]{:S(2)}, u32[]{:S(2)}) %collective-permute-start.1) | collective-permute-done | bytes 524320 | tf_op jit(solution)/shard_map/ppermute | solution.py:232
  77.1 5.6 %collective-permute-done.6.refs_13_ = bf16[512,512]{1,0:T(8,128)(2,1)S(1)} collective-permute-done((bf16[512,512]{1,0:T(8,128)(2,1)S(1)}, bf16[512,512]{1,0:T(8,128)(2,1)S(1)}, u32[]{:S(2)}, u32[]{:S(2)}) %collective-permute-start.6) | collective-permute-done | bytes 524320 | tf_op jit(solution)/shard_map/ppermute | solution.py:232
  82.7 10.5 %collective-permute-done.4.refs_11_ = bf16[512,512]{1,0:T(8,128)(2,1)} collective-permute-done((bf16[512,512]{1,0:T(8,128)(2,1)S(1)}, bf16[512,512]{1,0:T(8,128)(2,1)}, u32[]{:S(2)}, u32[]{:S(2)}) %collective-permute-start.4) | collective-permute-done | bytes 524320 | tf_op jit(solution)/shard_map/ppermute | solution.py:232
  93.2 2.6 %collective-permute-done.2.refs_9_ = bf16[512,512]{1,0:T(8,128)(2,1)} collective-permute-done((bf16[512,512]{1,0:T(8,128)(2,1)S(1)}, bf16[512,512]{1,0:T(8,128)(2,1)}, u32[]{:S(2)}, u32[]{:S(2)}) %collective-permute-start.2) | collective-permute-done | bytes 524320 | tf_op jit(solution)/shard_map/ppermute | solution.py:232
  95.8 16.9 %all-gather.3.cloned.1.call-done = bf16[4096,512]{1,0:T(8,128)(2,1)} async-done(((bf16[512,512]{1,0:T(8,128)(2,1)}), bf16[4096,512]{1,0:T(8,128)(2,1)}) %all-gather.3.cloned.1.call-update) | async-done | bytes 4194320 | tf_op jit(solution)/shard_map/all_gather | solution.py:225
  112.8 14.9 %remote.1 = (bf16[8,256,512]{2,1,0:T(8,128)(2,1)}, f32[512,512]{1,0:T(8,128)}, f32[512,512]{1,0:T(8,128)}, bf16[512,512]{1,0:T(8,128)(2,1)}, bf16[512,512]{1,0:T...) custom-call(s32[130]{0:T(256)} %pad_add_fusion.refs_0_, ...), custom_call_target="tpu_custom_call" | custom-call | tf_op jit(solution)/shard_map/remote/pallas_call | solution.py:190
  127.7 8.8 %collective-permute-start.8 = (bf16[512,512]{1,0:T(8,128)(2,1)}, bf16[512,512]{1,0:T(8,128)(2,1)S(1)}, u32[]{:S(2)}, u32[]{:S(2)}) collective-permute-start(bf16[512,512]{1,0:T(8,128)(2,1)} %get-tuple-element.64), channel_id=1, source_target_pairs={{0,24},{8,0},{16,8},{24,16},{1,25},{9,1},{17,9},{25,17},{2,26},{10... | collective-permute-start | bytes 1572872 | tf_op jit(solution)/shard_map/ppermute | solution.py:261
  136.6 1.9 collective-permute-start.11
  138.5 1.9 collective-permute-start.7
  140.4 7.0 %collective-permute-done.8 = bf16[512,512]{1,0:T(8,128)(2,1)S(1)} collective-permute-done((bf16[512,512]{1,0:T(8,128)(2,1)}, bf16[512,512]{1,0:T(8,128)(2,1)S(1)}, u32[]{:S(2)}, u32[]{:S(2)}) %collective-permute-start.8) | collective-permute-done | bytes 524320 | tf_op jit(solution)/shard_map/ppermute | solution.py:261
  148.6 5.2 %collective-permute-start.9 = (bf16[512,512]{1,0:T(8,128)(2,1)S(1)}, bf16[512,512]{1,0:T(8,128)(2,1)S(1)}, u32[]{:S(2)}, u32[]{:S(2)}) collective-permute-start(bf16[512,512]{1,0:T(8,128)(2,1)S(1)} %add_convert_fusion.3), channel_id=1, source_target_pairs={{0,24},{8,0},{16,8},{24,16},{1,25},{9,1},{17,9},{25,17},{2,26},{10... | collective-permute-start | bytes 1572872 | tf_op jit(solution)/shard_map/ppermute | solution.py:267
  153.8 1.9 collective-permute-start.10
  155.8 1.2 add_convert_fusion.1
  157.0 3.4 %collective-permute-start.12 = (bf16[512,512]{1,0:T(8,128)(2,1)S(1)}, bf16[512,512]{1,0:T(8,128)(2,1)S(1)}, u32[]{:S(2)}, u32[]{:S(2)}) collective-permute-start(bf16[512,512]{1,0:T(8,128)(2,1)S(1)} %add_convert_fusion.1), channel_id=1, source_target_pairs={{0,8},{8,16},{16,24},{24,0},{1,9},{9,17},{17,25},{25,1},{2,10},{10... | collective-permute-start | bytes 1572872 | tf_op jit(solution)/shard_map/ppermute | solution.py:266
  160.3 3.2 %collective-permute-done.7 = bf16[512,512]{1,0:T(8,128)(2,1)S(1)} collective-permute-done((bf16[512,512]{1,0:T(8,128)(2,1)}, bf16[512,512]{1,0:T(8,128)(2,1)S(1)}, u32[]{:S(2)}, u32[]{:S(2)}) %collective-permute-start.7) | collective-permute-done | bytes 524320 | tf_op jit(solution)/shard_map/ppermute | solution.py:262
  163.8 11.0 %collective-permute-done.10 = bf16[512,512]{1,0:T(8,128)(2,1)S(1)} collective-permute-done((bf16[512,512]{1,0:T(8,128)(2,1)}, bf16[512,512]{1,0:T(8,128)(2,1)S(1)}, u32[]{:S(2)}, u32[]{:S(2)}) %collective-permute-start.10) | collective-permute-done | bytes 524320 | tf_op jit(solution)/shard_map/ppermute | solution.py:263
  175.1 15.0 %reduce-scatter.2.cloned.1.call-done = bf16[1,256,512]{2,1,0:T(8,128)(2,1)} async-done(((bf16[8,256,512]{2,1,0:T(8,128)(2,1)}), bf16[1,256,512]{2,1,0:T(8,128)(2,1)}) %reduce-scatter.2.cloned.1.call-update) | async-done | bytes 262160 | tf_op jit(solution)/shard_map/reduce_scatter | solution.py:253
  190.1 3.2 %collective-permute-start.13 = (bf16[512,512]{1,0:T(8,128)(2,1)S(1)}, bf16[512,512]{1,0:T(8,128)(2,1)S(1)}, u32[]{:S(2)}, u32[]{:S(2)}) collective-permute-start(bf16[512,512]{1,0:T(8,128)(2,1)S(1)} %add_convert_fusion.2), channel_id=1, source_target_pairs={{0,32},{32,0},{1,33},{33,1},{2,34},{34,2},{3,35},{35,3},{4,36},{36... | collective-permute-start | bytes 1572872 | tf_op jit(solution)/shard_map/ppermute | solution.py:269
  193.3 14.4 %all_to_all.24 = bf16[8,32,512]{2,1,0:T(8,128)(2,1)S(1)} all-to-all(bf16[8,32,512]{2,1,0:T(8,128)(2,1)} %bitcast.13), channel_id=1, replica_groups=mesh['j'=8,'p'=2,'x'=4,'head'=8] {'head'}, dimensions={0} | all-to-all | bytes 524288 | tf_op jit(solution)/shard_map/all_to_all | solution.py:273
  (48 shorter events, 8.9 us)
Async XLA Ops:
  7.2 105.6 %all-gather.3.cloned.1.call-start = ((), (), s32[]{:S(2)}) async-start(), calls=%async_computation.4 | async-start | bytes 4718592 | tf_op jit(solution)/shard_map/all_gather | solution.py:225
  11.0 101.7 %copy-start = (bf16[512,512]{1,0:T(8,128)(2,1)}, bf16[512,512]{1,0:T(8,128)(2,1)S(1)}, u32[]{:S(2)}) copy-start(bf16[512,512]{1,0:T(8,128)(2,1)S(1)} %constant_dynamic-update-slice_fusion.refs_6_) | copy-start | bytes 1572868
  11.1 11.4 %collective-permute-start = (bf16[512,512]{1,0:T(8,128)(2,1)S(1)}, bf16[512,512]{1,0:T(8,128)(2,1)S(1)}, u32[]{:S(2)}, u32[]{:S(2)}) collective-permute-start(bf16[512,512]{1,0:T(8,128)(2,1)S(1)} %constant_dynamic-update-slice_fusion.refs_6_), channel_id=1, source_target_pairs={{0,32},{32,0},{1,33},{33,1},{2,34},{34,2},{3,35},{35,3},{4,36},{36... | collective-permute-start | bytes 1572872 | tf_op jit(solution)/shard_map/ppermute | solution.py:228
  22.5 90.2 %copy-start.3 = (bf16[512,512]{1,0:T(8,128)(2,1)}, bf16[512,512]{1,0:T(8,128)(2,1)S(1)}, u32[]{:S(2)}) copy-start(bf16[512,512]{1,0:T(8,128)(2,1)S(1)} %collective-permute-done.refs_7_) | copy-start | bytes 1572868
  24.7 34.5 %all-to-all-start = ((f32[8,24,128]{2,1,0:T(8,128)}), f32[8,24,128]{2,1,0:T(8,128)S(1)}, u32[]{:S(2)}, u32[]{:S(2)}) async-start(f32[8,24,128]{2,1,0:T(8,128)} %broadcast_in_dim.14), calls=%async_computation | async-start | bytes 196608 | tf_op jit(solution)/shard_map/all_to_all | solution.py:243
  43.6 146.5 %reduce-scatter.2.cloned.1.call-start = ((), (), s32[]{:S(2)}) async-start(), calls=%async_computation.3 | async-start | bytes 2359296 | tf_op jit(solution)/shard_map/reduce_scatter | solution.py:253
  43.7 16.4 %collective-permute-start.5 = (bf16[512,512]{1,0:T(8,128)(2,1)S(1)}, bf16[512,512]{1,0:T(8,128)(2,1)S(1)}, u32[]{:S(2)}, u32[]{:S(2)}) collective-permute-start(bf16[512,512]{1,0:T(8,128)(2,1)S(1)} %constant_dynamic-update-slice_fusion.refs_6_), channel_id=1, source_target_pairs={{0,8},{8,16},{16,24},{24,0},{1,9},{9,17},{17,25},{25,1},{2,10},{10... | collective-permute-start | bytes 1572872 | tf_op jit(solution)/shard_map/ppermute | solution.py:232
  46.8 23.9 %collective-permute-start.3 = (bf16[512,512]{1,0:T(8,128)(2,1)S(1)}, bf16[512,512]{1,0:T(8,128)(2,1)S(1)}, u32[]{:S(2)}, u32[]{:S(2)}) collective-permute-start(bf16[512,512]{1,0:T(8,128)(2,1)S(1)} %constant_dynamic-update-slice_fusion.refs_6_), channel_id=1, source_target_pairs={{0,16},{8,24},{16,0},{24,8},{1,17},{9,25},{17,1},{25,9},{2,18},{10... | collective-permute-start | bytes 1572872 | tf_op jit(solution)/shard_map/ppermute | solution.py:232
  51.2 25.9 %collective-permute-start.1 = (bf16[512,512]{1,0:T(8,128)(2,1)S(1)}, bf16[512,512]{1,0:T(8,128)(2,1)S(1)}, u32[]{:S(2)}, u32[]{:S(2)}) collective-permute-start(bf16[512,512]{1,0:T(8,128)(2,1)S(1)} %constant_dynamic-update-slice_fusion.refs_6_), channel_id=1, source_target_pairs={{0,24},{8,0},{16,8},{24,16},{1,25},{9,1},{17,9},{25,17},{2,26},{10... | collective-permute-start | bytes 1572872 | tf_op jit(solution)/shard_map/ppermute | solution.py:232
  54.2 28.5 %collective-permute-start.6 = (bf16[512,512]{1,0:T(8,128)(2,1)S(1)}, bf16[512,512]{1,0:T(8,128)(2,1)S(1)}, u32[]{:S(2)}, u32[]{:S(2)}) collective-permute-start(bf16[512,512]{1,0:T(8,128)(2,1)S(1)} %collective-permute-done.refs_7_), channel_id=1, source_target_pairs={{0,8},{8,16},{16,24},{24,0},{1,9},{9,17},{17,25},{25,1},{2,10},{10... | collective-permute-start | bytes 1572872 | tf_op jit(solution)/shard_map/ppermute | solution.py:232
  56.5 36.7 %collective-permute-start.4 = (bf16[512,512]{1,0:T(8,128)(2,1)S(1)}, bf16[512,512]{1,0:T(8,128)(2,1)}, u32[]{:S(2)}, u32[]{:S(2)}) collective-permute-start(bf16[512,512]{1,0:T(8,128)(2,1)S(1)} %collective-permute-done.refs_7_), channel_id=1, source_target_pairs={{0,16},{8,24},{16,0},{24,8},{1,17},{9,25},{17,1},{25,9},{2,18},{10... | collective-permute-start | bytes 1572872 | tf_op jit(solution)/shard_map/ppermute | solution.py:232
  59.3 53.5 %copy-start.8 = (f32[8,24,128]{2,1,0:T(8,128)}, f32[8,24,128]{2,1,0:T(8,128)S(1)}, u32[]{:S(2)}) copy-start(f32[8,24,128]{2,1,0:T(8,128)S(1)} %all-to-all-done.refs_1_) | copy-start | bytes 294916
  60.1 52.6 %copy-start.4 = (bf16[512,512]{1,0:T(8,128)(2,1)}, bf16[512,512]{1,0:T(8,128)(2,1)S(1)}, u32[]{:S(2)}) copy-start(bf16[512,512]{1,0:T(8,128)(2,1)S(1)} %collective-permute-done.5.refs_12_) | copy-start | bytes 1572868
  60.1 35.7 %collective-permute-start.2 = (bf16[512,512]{1,0:T(8,128)(2,1)S(1)}, bf16[512,512]{1,0:T(8,128)(2,1)}, u32[]{:S(2)}, u32[]{:S(2)}) collective-permute-start(bf16[512,512]{1,0:T(8,128)(2,1)S(1)} %collective-permute-done.refs_7_), channel_id=1, source_target_pairs={{0,24},{8,0},{16,8},{24,16},{1,25},{9,1},{17,9},{25,17},{2,26},{10... | collective-permute-start | bytes 1572872 | tf_op jit(solution)/shard_map/ppermute | solution.py:232
  70.7 42.0 %copy-start.5 = (bf16[512,512]{1,0:T(8,128)(2,1)}, bf16[512,512]{1,0:T(8,128)(2,1)S(1)}, u32[]{:S(2)}) copy-start(bf16[512,512]{1,0:T(8,128)(2,1)S(1)} %collective-permute-done.3.refs_10_) | copy-start | bytes 1572868
  77.1 35.7 %copy-start.6 = (bf16[512,512]{1,0:T(8,128)(2,1)}, bf16[512,512]{1,0:T(8,128)(2,1)S(1)}, u32[]{:S(2)}) copy-start(bf16[512,512]{1,0:T(8,128)(2,1)S(1)} %collective-permute-done.1.refs_8_) | copy-start | bytes 1572868
  82.7 30.1 %copy-start.7 = (bf16[512,512]{1,0:T(8,128)(2,1)}, bf16[512,512]{1,0:T(8,128)(2,1)S(1)}, u32[]{:S(2)}) copy-start(bf16[512,512]{1,0:T(8,128)(2,1)S(1)} %collective-permute-done.6.refs_13_) | copy-start | bytes 1572868
  127.7 35.9 %copy-start.2 = (f32[512,512]{1,0:T(8,128)S(1)}, f32[512,512]{1,0:T(8,128)}, u32[]{:S(2)}) copy-start(f32[512,512]{1,0:T(8,128)} %get-tuple-element.61) | copy-start | bytes 3145732
  127.7 47.2 %copy-start.1 = (f32[512,512]{1,0:T(8,128)S(1)}, f32[512,512]{1,0:T(8,128)}, u32[]{:S(2)}) copy-start(f32[512,512]{1,0:T(8,128)} %get-tuple-element.65) | copy-start | bytes 3145732
  127.7 19.7 %collective-permute-start.8 = (bf16[512,512]{1,0:T(8,128)(2,1)}, bf16[512,512]{1,0:T(8,128)(2,1)S(1)}, u32[]{:S(2)}, u32[]{:S(2)}) collective-permute-start(bf16[512,512]{1,0:T(8,128)(2,1)} %get-tuple-element.64), channel_id=1, source_target_pairs={{0,24},{8,0},{16,8},{24,16},{1,25},{9,1},{17,9},{25,17},{2,26},{10... | collective-permute-start | bytes 1572872 | tf_op jit(solution)/shard_map/ppermute | solution.py:261
  136.6 19.2 %collective-permute-start.11 = (bf16[512,512]{1,0:T(8,128)(2,1)}, bf16[512,512]{1,0:T(8,128)(2,1)S(1)}, u32[]{:S(2)}, u32[]{:S(2)}) collective-permute-start(bf16[512,512]{1,0:T(8,128)(2,1)} %get-tuple-element.68), channel_id=1, source_target_pairs={{0,8},{8,16},{16,24},{24,0},{1,9},{9,17},{17,25},{25,1},{2,10},{10... | collective-permute-start | bytes 1572872 | tf_op jit(solution)/shard_map/ppermute | solution.py:260
  138.5 25.1 %collective-permute-start.7 = (bf16[512,512]{1,0:T(8,128)(2,1)}, bf16[512,512]{1,0:T(8,128)(2,1)S(1)}, u32[]{:S(2)}, u32[]{:S(2)}) collective-permute-start(bf16[512,512]{1,0:T(8,128)(2,1)} %get-tuple-element.62), channel_id=1, source_target_pairs={{0,8},{8,16},{16,24},{24,0},{1,9},{9,17},{17,25},{25,1},{2,10},{10... | collective-permute-start | bytes 1572872 | tf_op jit(solution)/shard_map/ppermute | solution.py:262
  148.6 15.0 %collective-permute-start.9 = (bf16[512,512]{1,0:T(8,128)(2,1)S(1)}, bf16[512,512]{1,0:T(8,128)(2,1)S(1)}, u32[]{:S(2)}, u32[]{:S(2)}) collective-permute-start(bf16[512,512]{1,0:T(8,128)(2,1)S(1)} %add_convert_fusion.3), channel_id=1, source_target_pairs={{0,24},{8,0},{16,8},{24,16},{1,25},{9,1},{17,9},{25,17},{2,26},{10... | collective-permute-start | bytes 1572872 | tf_op jit(solution)/shard_map/ppermute | solution.py:267
  153.8 21.0 %collective-permute-start.10 = (bf16[512,512]{1,0:T(8,128)(2,1)}, bf16[512,512]{1,0:T(8,128)(2,1)S(1)}, u32[]{:S(2)}, u32[]{:S(2)}) collective-permute-start(bf16[512,512]{1,0:T(8,128)(2,1)} %get-tuple-element.66), channel_id=1, source_target_pairs={{0,24},{8,0},{16,8},{24,16},{1,25},{9,1},{17,9},{25,17},{2,26},{10... | collective-permute-start | bytes 1572872 | tf_op jit(solution)/shard_map/ppermute | solution.py:263
  157.0 18.0 %collective-permute-start.12 = (bf16[512,512]{1,0:T(8,128)(2,1)S(1)}, bf16[512,512]{1,0:T(8,128)(2,1)S(1)}, u32[]{:S(2)}, u32[]{:S(2)}) collective-permute-start(bf16[512,512]{1,0:T(8,128)(2,1)S(1)} %add_convert_fusion.1), channel_id=1, source_target_pairs={{0,8},{8,16},{16,24},{24,0},{1,9},{9,17},{17,25},{25,1},{2,10},{10... | collective-permute-start | bytes 1572872 | tf_op jit(solution)/shard_map/ppermute | solution.py:266
  190.1 18.3 %collective-permute-start.13 = (bf16[512,512]{1,0:T(8,128)(2,1)S(1)}, bf16[512,512]{1,0:T(8,128)(2,1)S(1)}, u32[]{:S(2)}, u32[]{:S(2)}) collective-permute-start(bf16[512,512]{1,0:T(8,128)(2,1)S(1)} %add_convert_fusion.2), channel_id=1, source_target_pairs={{0,32},{32,0},{1,33},{33,1},{2,34},{34,2},{3,35},{35,3},{4,36},{36... | collective-permute-start | bytes 1572872 | tf_op jit(solution)/shard_map/ppermute | solution.py:269
Sparse Core Ops, SparseCore 0:
  10.1 102.5 all-gather.2
  127.8 62.2 reduce-scatter.1

commit v8 on v7

--- a/solution.py
+++ b/solution.py
@@ -81,8 +81,10 @@
 def remote_kernel(blocks, heads, factor, owners, *refs):
     slots_ref, stat_ref, own_q_ref, own_k_ref, own_v_ref, packs_ref = refs[:6]
     kv_refs = refs[6 : 6 + owners]
-    dq_out, *part_outs = refs[6 + owners : 7 + 2 * owners]
-    dq_ref, acc_ref, far_ref, line_ref, pack_ref, kv_ref, sems = refs[7 + 2 * owners :]
+    ring = packs_ref.shape[0]
+    outs = refs[6 + owners : -7]
+    dq_outs, part_outs = outs[: ring + 1], outs[ring + 1 :]
+    dq_ref, acc_ref, far_ref, line_ref, pack_ref, kv_ref, sems = refs[-7:]
     rows = blocks * BLOCK
     span = blocks * owners
     loads = [
@@ -95,7 +97,6 @@
     count = slots_ref[0]
     mine = slots_ref[slots_ref.shape[0] - 1]
     dq_ref[...] = jnp.zeros_like(dq_ref)
-    dq_ref[mine] = own_q_ref[...].astype(BF16)
     acc_ref[0, :rows] = own_k_ref[...]
     acc_ref[0, rows:] = own_v_ref[...]
     acc_ref[1:] = jnp.zeros((owners - 1, *acc_ref.shape[1:]), F32)
@@ -137,10 +138,9 @@
         for same, zq, q_at, cols, kx, k_at, v_at, (grad_q, grad_k, grad_v) in done:
             acc_ref[kx, k_at, cols] += grad_k
             acc_ref[kx, v_at, cols] += grad_v
-            start = jnp.where(zq == mine, own_q_ref[q_at, cols], 0.0)
-            total = jnp.where(same, line_ref[...], start) + grad_q
+            total = jnp.where(same, line_ref[...], 0.0) + grad_q
             line_ref[...] = total
-            dq_ref[zq, q_at, cols] = total.astype(BF16)
+            dq_ref[(zq - mine) & (ring - 1), q_at, cols] = total
 
     large, small = TURN_SIZES
     full, rest = low_bits(count, large)[::-1]
@@ -153,11 +153,18 @@
     def _(step):
         turn(full * large + step * small, small)
 
-    stores = [pltpu.make_async_copy(dq_ref, dq_out, sems.at[owners])]
+    stores = []
     for at in range(PAIR):
         stores.append(pltpu.make_async_copy(acc_ref.at[at], part_outs[at], sems.at[at]))
     for store in stores:
         store.start()
+    half = rows // 2
+    dq_outs[0][...] = dq_ref[0] + own_q_ref[...]
+    for at in range(1, ring // 2):
+        dq_outs[at][...] = dq_ref[at].astype(BF16)
+        dq_outs[ring // 2 + at][...] = dq_ref[ring // 2 + at].astype(BF16)
+    dq_outs[ring // 2][...] = dq_ref[ring // 2, :half].astype(BF16)
+    dq_outs[ring][...] = dq_ref[ring // 2, half:].astype(BF16)
     for at in range(PAIR, owners):
         far_ref[at - PAIR] = acc_ref[at].astype(BF16)
         turned = pltpu.make_async_copy(far_ref.at[at - PAIR], part_outs[at], sems.at[at])
@@ -192,12 +199,16 @@
         in_specs=[pl.BlockSpec(memory_space=pltpu.SMEM)]
         + [pl.BlockSpec(memory_space=pltpu.VMEM)] * 4
         + [anywhere] * (1 + owners),
-        out_specs=(anywhere,) * (1 + owners),
-        out_shape=(jax.ShapeDtypeStruct((ring, rows, width), BF16),)
+        out_specs=(pl.BlockSpec(memory_space=pltpu.VMEM),) * (ring + 1) + (anywhere,) * owners,
+        out_shape=(jax.ShapeDtypeStruct((rows, width), F32),)
+        + (jax.ShapeDtypeStruct((rows, width), BF16),) * (ring // 2 - 1)
+        + (jax.ShapeDtypeStruct((rows // 2, width), BF16),)
+        + (jax.ShapeDtypeStruct((rows, width), BF16),) * (ring // 2 - 1)
+        + (jax.ShapeDtypeStruct((rows // 2, width), BF16),)
         + (jax.ShapeDtypeStruct(part, F32),) * PAIR
         + (jax.ShapeDtypeStruct(part, BF16),) * (owners - PAIR),
         scratch_shapes=[
-            pltpu.VMEM((ring, rows, width), BF16),
+            pltpu.VMEM((ring, rows, width), F32),
             pltpu.VMEM((owners, *part), F32),
             pltpu.VMEM((owners - PAIR, *part), BF16),
             pltpu.VMEM((BLOCK, BLOCK), F32),
@@ -247,15 +258,34 @@
     packs, kvs, codes, stats, own_q, own_k, own_v = lax.optimization_barrier(
         (packs, kvs, codes, stats, own_q, own_k, own_v)
     )
-    part_q, near, near_other, next_a, next_b, far_a, far_b, last_a, last_b = remote_call(
+    outs = remote_call(
         codes, stats, own_q, packs, own_k, own_v, kvs, blocks, heads, factor, rows, width, ring, owners
     )
-    sum_q = lax.psum_scatter(part_q, "j", scatter_dimension=0)
+    near_q, *far_q = outs[: ring + 1]
+    near, near_other, next_a, next_b, far_a, far_b, last_a, last_b = outs[ring + 1 :]
     ahead = [(i, (i + 1) % X_SIZE) for i in range(X_SIZE)]
     behind = [(i, (i - 1) % X_SIZE) for i in range(X_SIZE)]
 
     def wide(part):
         return part.astype(F32)
+
+    up = [(i, (i + 1) % ring) for i in range(ring)]
+    down = [(i, (i - 1) % ring) for i in range(ring)]
+    middle, half = ring // 2, rows // 2
+    rising = lax.ppermute(far_q[middle - 1], "j", up)
+    falling = lax.ppermute(far_q[ring - 1], "j", down)
+    part = far_q[middle - 2]
+    rising = jnp.concatenate([(wide(part[:half]) + wide(rising)).astype(BF16), part[half:]])
+    part = far_q[middle]
+    falling = jnp.concatenate([part[:half], (wide(part[half:]) + wide(falling)).astype(BF16)])
+    for step in range(1, middle - 1):
+        rising = lax.ppermute(rising, "j", up)
+        falling = lax.ppermute(falling, "j", down)
+        rising = (wide(far_q[middle - 2 - step]) + wide(rising)).astype(BF16)
+        falling = (wide(far_q[middle + step]) + wide(falling)).astype(BF16)
+    rising = lax.ppermute(rising, "j", up)
+    falling = lax.ppermute(falling, "j", down)
+    sum_q = (near_q + wide(rising) + wide(falling)).astype(BF16)
 
     through_a = lax.ppermute(far_a, "x", ahead)
     through_b = lax.ppermute(far_b, "x", behind)

time: 217 us -> 243 us (1.12)
  starting transfers between devices: 69.9 us -> 98.2 us
  waiting for transfers between devices: 86.3 us -> 80.1 us
    ppermute x0 -> x8, starting transfers between devices: none -> 29.6 us  [the longest x3 15.8 us: shards(): falling = lax.ppermute(falling, 'j', down)]
    ppermute x0 -> x8, waiting for transfers between devices: none -> 23.8 us  [the longest x3 22.2 us: shards(): rising = lax.ppermute(rising, 'j', up)]
    reduce_scatter x1 -> x0, waiting for transfers between devices: 15 us -> none  [shards(): sum_q = lax.psum_scatter(part_q, 'j', scatter_dimension=0)]
    ppermute x1, waiting for transfers between devices: 11 us -> 0.01 us  [shards(): from_last = lax.ppermute(last_a, 'x', behind)]
    ppermute x1, waiting for transfers between devices: 7.02 us -> 0.01 us  [shards(): through_b = lax.ppermute(far_b, 'x', behind)]
    ppermute x1, waiting for transfers between devices: 0.1 us -> 6.36 us  [shards(): sum_own = near + wide(from_last) + wide(lax.ppermute(next_a, 'x', ahead))]
    convert_element_type x0 -> x7, other arithmetic: none -> 4.15 us  [the longest x2 1.08 us: shards(): rising = (wide(far_q[middle - 2 - step]) + wide(rising)).astype(BF16)]
    ppermute x1, waiting for transfers between devices: 3.25 us -> 0.01 us  [shards(): from_next = lax.ppermute(next_b, 'x', ahead)]
  transfers between devices with their start and end apart: 17 -> 24, of which waited for: 12 -> 12; matrix products, arithmetic and copies ran while one was open for 5% -> 6% of each run, Pallas kernels for 2% -> 1%
where the time goes in v8:
time: 243 us; the launch traced here: 242 us
  starting transfers between devices  98.2 us (40%)
  waiting for transfers between devices  80.1 us (33%)
  Pallas kernels  20 us (8%)
  between operations  14.6 us (6%)
  blocking collectives  14.1 us (6%)
  other arithmetic  8.69 us (4%)
  local copies, waits for them, and re-layouts  6.36 us (3%)
    ppermute x6, waiting for transfers between devices, shards(): kvs += [lax.ppermute(both, 'x', back), lax.ppermute(swapped, 'x', back)]  29.4 us
    ppermute x3, waiting for transfers between devices, shards(): rising = lax.ppermute(rising, 'j', up)  22.2 us
    ppermute x6, starting transfers between devices, shards(): kvs += [lax.ppermute(both, 'x', back), lax.ppermute(swapped, 'x', back)]  20.2 us
    all_to_all x1, starting transfers between devices, shards(): lax.all_to_all(jnp.broadcast_to(info[None], (ring, *info.shape)), 'j', 0,...  18.9 us
    all_gather x1, waiting for transfers between devices, shards(): packs = lax.all_gather(pack, 'j')  16.8 us
    ppermute x3, starting transfers between devices, shards(): falling = lax.ppermute(falling, 'j', down)  15.8 us
    pallas_call x1, Pallas kernels, remote_call(): pl.pallas_call(functools.partial(remote_kernel, blocks, heads, factor, ow...  14.6 us
    all_to_all x1, blocking collectives, shards(): lax.all_to_all(sum_q, 'head', split_axis=0, concat_axis=1, tiled=True)  14.1 us
  transfers between devices with their start and end apart: 24, of which 12 were waited for; matrix products, arithmetic and copies ran while one was open for 6% of the time, Pallas kernels for 1%

profile of v8, /device:TPU:1, one launch (start us, length us, event | category | flops | bytes accessed | tf_op | source)
XLA Modules:
  0.0 241.9 jit_solution(14829265931050946319)
XLA Ops:
  11.1 4.4 %collective-permute-start = (bf16[512,512]{1,0:T(8,128)(2,1)S(1)}, bf16[512,512]{1,0:T(8,128)(2,1)S(1)}, u32[]{:S(2)}, u32[]{:S(2)}) collective-permute-start(bf16[512,512]{1,0:T(8,128)(2,1)S(1)} %constant_dynamic-update-slice_fusion.refs_6_), channel_id=1, source_target_pairs={{0,32},{32,0},{1,33},{33,1},{2,34},{34,2},{3,35},{35,3},{4,36},{36... | collective-permute-start | bytes 1572872 | tf_op jit(solution)/shard_map/ppermute | solution.py:239
  15.5 3.5 %own.1 = (f32[16,128]{1,0:T(8,128)}, f32[256,512]{1,0:T(8,128)}, f32[256,512]{1,0:T(8,128)}, f32[256,512]{1,0:T(8,128)}) custom-call(bf16[256,512]{1,0:T(8,128)(2,1)} %q_ref.3, bf16[256,512]{1,0:T(8,128)(2,1)} %g_ref.3, bf16[256,512]{1,0:T(8,128)(2,1)} %o_ref.1, f32[4,256]{1,0:T(4,128)} %bitcast.14, bf16[256,512]{1,0:T(8,128)(2,1)} %k_ref, bf16[256,512]{1,0:T(8,128)(2,1)} %v_ref), custom_call_target="tpu_custom_call" | custom-call | tf_op jit(solution)/shard_map/own/pallas_call | solution.py:245
  18.9 3.6 %collective-permute-done.refs_7_ = bf16[512,512]{1,0:T(8,128)(2,1)S(1)} collective-permute-done((bf16[512,512]{1,0:T(8,128)(2,1)S(1)}, bf16[512,512]{1,0:T(8,128)(2,1)S(1)}, u32[]{:S(2)}, u32[]{:S(2)}) %collective-permute-start) | collective-permute-done | bytes 524320 | tf_op jit(solution)/shard_map/ppermute | solution.py:239
  24.7 18.9 %all-to-all-start = ((f32[8,24,128]{2,1,0:T(8,128)}), f32[8,24,128]{2,1,0:T(8,128)S(1)}, u32[]{:S(2)}, u32[]{:S(2)}) async-start(f32[8,24,128]{2,1,0:T(8,128)} %broadcast_in_dim.14), calls=%async_computation | async-start | bytes 196608 | tf_op jit(solution)/shard_map/all_to_all | solution.py:254
  43.6 3.1 %collective-permute-start.5 = (bf16[512,512]{1,0:T(8,128)(2,1)S(1)}, bf16[512,512]{1,0:T(8,128)(2,1)S(1)}, u32[]{:S(2)}, u32[]{:S(2)}) collective-permute-start(bf16[512,512]{1,0:T(8,128)(2,1)S(1)} %constant_dynamic-update-slice_fusion.refs_6_), channel_id=1, source_target_pairs={{0,8},{8,16},{16,24},{24,0},{1,9},{9,17},{17,25},{25,1},{2,10},{10... | collective-permute-start | bytes 1572872 | tf_op jit(solution)/shard_map/ppermute | solution.py:243
  46.8 4.4 %collective-permute-start.3 = (bf16[512,512]{1,0:T(8,128)(2,1)S(1)}, bf16[512,512]{1,0:T(8,128)(2,1)S(1)}, u32[]{:S(2)}, u32[]{:S(2)}) collective-permute-start(bf16[512,512]{1,0:T(8,128)(2,1)S(1)} %constant_dynamic-update-slice_fusion.refs_6_), channel_id=1, source_target_pairs={{0,16},{8,24},{16,0},{24,8},{1,17},{9,25},{17,1},{25,9},{2,18},{10... | collective-permute-start | bytes 1572872 | tf_op jit(solution)/shard_map/ppermute | solution.py:243
  51.1 3.1 %collective-permute-start.1 = (bf16[512,512]{1,0:T(8,128)(2,1)S(1)}, bf16[512,512]{1,0:T(8,128)(2,1)S(1)}, u32[]{:S(2)}, u32[]{:S(2)}) collective-permute-start(bf16[512,512]{1,0:T(8,128)(2,1)S(1)} %constant_dynamic-update-slice_fusion.refs_6_), channel_id=1, source_target_pairs={{0,24},{8,0},{16,8},{24,16},{1,25},{9,1},{17,9},{25,17},{2,26},{10... | collective-permute-start | bytes 1572872 | tf_op jit(solution)/shard_map/ppermute | solution.py:243
  54.2 2.2 collective-permute-start.6
  56.4 2.8 %collective-permute-start.4 = (bf16[512,512]{1,0:T(8,128)(2,1)S(1)}, bf16[512,512]{1,0:T(8,128)(2,1)}, u32[]{:S(2)}, u32[]{:S(2)}) collective-permute-start(bf16[512,512]{1,0:T(8,128)(2,1)S(1)} %collective-permute-done.refs_7_), channel_id=1, source_target_pairs={{0,16},{8,24},{16,0},{24,8},{1,17},{9,25},{17,1},{25,9},{2,18},{10... | collective-permute-start | bytes 1572872 | tf_op jit(solution)/shard_map/ppermute | solution.py:243
  60.0 4.7 %collective-permute-start.2 = (bf16[512,512]{1,0:T(8,128)(2,1)S(1)}, bf16[512,512]{1,0:T(8,128)(2,1)}, u32[]{:S(2)}, u32[]{:S(2)}) collective-permute-start(bf16[512,512]{1,0:T(8,128)(2,1)S(1)} %collective-permute-done.refs_7_), channel_id=1, source_target_pairs={{0,24},{8,0},{16,8},{24,16},{1,25},{9,1},{17,9},{25,17},{2,26},{10... | collective-permute-start | bytes 1572872 | tf_op jit(solution)/shard_map/ppermute | solution.py:243
  66.3 4.4 %collective-permute-done.3.refs_10_ = bf16[512,512]{1,0:T(8,128)(2,1)S(1)} collective-permute-done((bf16[512,512]{1,0:T(8,128)(2,1)S(1)}, bf16[512,512]{1,0:T(8,128)(2,1)S(1)}, u32[]{:S(2)}, u32[]{:S(2)}) %collective-permute-start.3) | collective-permute-done | bytes 524320 | tf_op jit(solution)/shard_map/ppermute | solution.py:243
  70.7 6.4 %collective-permute-done.1.refs_8_ = bf16[512,512]{1,0:T(8,128)(2,1)S(1)} collective-permute-done((bf16[512,512]{1,0:T(8,128)(2,1)S(1)}, bf16[512,512]{1,0:T(8,128)(2,1)S(1)}, u32[]{:S(2)}, u32[]{:S(2)}) %collective-permute-start.1) | collective-permute-done | bytes 524320 | tf_op jit(solution)/shard_map/ppermute | solution.py:243
  77.1 5.6 %collective-permute-done.6.refs_13_ = bf16[512,512]{1,0:T(8,128)(2,1)S(1)} collective-permute-done((bf16[512,512]{1,0:T(8,128)(2,1)S(1)}, bf16[512,512]{1,0:T(8,128)(2,1)S(1)}, u32[]{:S(2)}, u32[]{:S(2)}) %collective-permute-start.6) | collective-permute-done | bytes 524320 | tf_op jit(solution)/shard_map/ppermute | solution.py:243
  82.7 10.5 %collective-permute-done.4.refs_11_ = bf16[512,512]{1,0:T(8,128)(2,1)} collective-permute-done((bf16[512,512]{1,0:T(8,128)(2,1)S(1)}, bf16[512,512]{1,0:T(8,128)(2,1)}, u32[]{:S(2)}, u32[]{:S(2)}) %collective-permute-start.4) | collective-permute-done | bytes 524320 | tf_op jit(solution)/shard_map/ppermute | solution.py:243
  93.2 2.6 %collective-permute-done.2.refs_9_ = bf16[512,512]{1,0:T(8,128)(2,1)} collective-permute-done((bf16[512,512]{1,0:T(8,128)(2,1)S(1)}, bf16[512,512]{1,0:T(8,128)(2,1)}, u32[]{:S(2)}, u32[]{:S(2)}) %collective-permute-start.2) | collective-permute-done | bytes 524320 | tf_op jit(solution)/shard_map/ppermute | solution.py:243
  95.8 16.8 %all-gather.3.cloned.1.call-done = bf16[4096,512]{1,0:T(8,128)(2,1)} async-done(((bf16[512,512]{1,0:T(8,128)(2,1)}), bf16[4096,512]{1,0:T(8,128)(2,1)}) %all-gather.3.cloned.1.call-update) | async-done | bytes 4194320 | tf_op jit(solution)/shard_map/all_gather | solution.py:236
  112.7 14.6 %remote.1 = (f32[256,512]{1,0:T(8,128)}, bf16[256,512]{1,0:T(8,128)(2,1)}, bf16[256,512]{1,0:T(8,128)(2,1)}, bf16[256,512]{1,0:T(8,128)(2,1)}, bf16[128,512]{1,0...) custom-call(s32[130]{0:T(256)} %pad_add_fusion.refs_0_, ...), custom_call_target="tpu_custom_call" | custom-call | tf_op jit(solution)/shard_map/remote/pallas_call | solution.py:197
  127.3 2.1 collective-permute-start.17
  131.2 4.3 %collective-permute-start.13 = (bf16[128,512]{1,0:T(8,128)(2,1)}, bf16[128,512]{1,0:T(8,128)(2,1)S(1)}, u32[]{:S(2)}, u32[]{:S(2)}) collective-permute-start(bf16[128,512]{1,0:T(8,128)(2,1)} %get-tuple-element.81), channel_id=1, source_target_pairs={{0,64},{64,128},{128,192},{192,256},{256,320},{320,384},{384,448},... | collective-permute-start | bytes 393224 | tf_op jit(solution)/shard_map/ppermute | solution.py:275
  135.5 7.4 %collective-permute-start.8 = (bf16[512,512]{1,0:T(8,128)(2,1)}, bf16[512,512]{1,0:T(8,128)(2,1)S(1)}, u32[]{:S(2)}, u32[]{:S(2)}) collective-permute-start(bf16[512,512]{1,0:T(8,128)(2,1)} %get-tuple-element.72), channel_id=1, source_target_pairs={{0,24},{8,0},{16,8},{24,16},{1,25},{9,1},{17,9},{25,17},{2,26},{10... | collective-permute-start | bytes 1572872 | tf_op jit(solution)/shard_map/ppermute | solution.py:291
  143.9 3.3 %collective-permute-start.18 = (bf16[256,512]{1,0:T(8,128)(2,1)S(1)}, bf16[256,512]{1,0:T(8,128)(2,1)S(1)}, u32[]{:S(2)}, u32[]{:S(2)}) collective-permute-start(bf16[256,512]{1,0:T(8,128)(2,1)S(1)} %pad_maximum_fusion.1), channel_id=1, source_target_pairs={{0,448},{64,0},{128,64},{192,128},{256,192},{320,256},{384,320},{4... | collective-permute-start | bytes 786440 | tf_op jit(solution)/shard_map/ppermute | solution.py:283
  148.2 3.7 %collective-permute-start.14 = (bf16[256,512]{1,0:T(8,128)(2,1)S(1)}, bf16[256,512]{1,0:T(8,128)(2,1)S(1)}, u32[]{:S(2)}, u32[]{:S(2)}) collective-permute-start(bf16[256,512]{1,0:T(8,128)(2,1)S(1)} %pad_maximum_fusion), channel_id=1, source_target_pairs={{0,64},{64,128},{128,192},{192,256},{256,320},{320,384},{384,448},... | collective-permute-start | bytes 786440 | tf_op jit(solution)/shard_map/ppermute | solution.py:282
  153.8 4.6 %collective-permute-start.10 = (bf16[512,512]{1,0:T(8,128)(2,1)}, bf16[512,512]{1,0:T(8,128)(2,1)S(1)}, u32[]{:S(2)}, u32[]{:S(2)}) collective-permute-start(bf16[512,512]{1,0:T(8,128)(2,1)} %get-tuple-element.74), channel_id=1, source_target_pairs={{0,24},{8,0},{16,8},{24,16},{1,25},{9,1},{17,9},{25,17},{2,26},{10... | collective-permute-start | bytes 1572872 | tf_op jit(solution)/shard_map/ppermute | solution.py:293
  161.3 8.1 %collective-permute-start.19 = (bf16[256,512]{1,0:T(8,128)(2,1)S(1)}, bf16[256,512]{1,0:T(8,128)(2,1)S(1)}, u32[]{:S(2)}, u32[]{:S(2)}) collective-permute-start(bf16[256,512]{1,0:T(8,128)(2,1)S(1)} %add_convert_fusion.6), channel_id=1, source_target_pairs={{0,448},{64,0},{128,64},{192,128},{256,192},{320,256},{384,320},{4... | collective-permute-start | bytes 786440 | tf_op jit(solution)/shard_map/ppermute | solution.py:283
  170.4 1.9 collective-permute-start.15
  172.8 2.9 %collective-permute-start.9 = (bf16[512,512]{1,0:T(8,128)(2,1)S(1)}, bf16[512,512]{1,0:T(8,128)(2,1)S(1)}, u32[]{:S(2)}, u32[]{:S(2)}) collective-permute-start(bf16[512,512]{1,0:T(8,128)(2,1)S(1)} %add_convert_fusion.3), channel_id=1, source_target_pairs={{0,24},{8,0},{16,8},{24,16},{1,25},{9,1},{17,9},{25,17},{2,26},{10... | collective-permute-start | bytes 1572872 | tf_op jit(solution)/shard_map/ppermute | solution.py:297
  175.8 5.0 %collective-permute-done.15 = bf16[256,512]{1,0:T(8,128)(2,1)S(1)} collective-permute-done((bf16[256,512]{1,0:T(8,128)(2,1)S(1)}, bf16[256,512]{1,0:T(8,128)(2,1)S(1)}, u32[]{:S(2)}, u32[]{:S(2)}) %collective-permute-start.15) | collective-permute-done | bytes 262176 | tf_op jit(solution)/shard_map/ppermute | solution.py:282
  180.7 4.4 %collective-permute-start.20 = (bf16[256,512]{1,0:T(8,128)(2,1)S(1)}, bf16[256,512]{1,0:T(8,128)(2,1)S(1)}, u32[]{:S(2)}, u32[]{:S(2)}) collective-permute-start(bf16[256,512]{1,0:T(8,128)(2,1)S(1)} %add_convert_fusion.5), channel_id=1, source_target_pairs={{0,448},{64,0},{128,64},{192,128},{256,192},{320,256},{384,320},{4... | collective-permute-start | bytes 786440 | tf_op jit(solution)/shard_map/ppermute | solution.py:287
  190.7 17.2 %collective-permute-done.16 = bf16[256,512]{1,0:T(8,128)(2,1)S(1)} collective-permute-done((bf16[256,512]{1,0:T(8,128)(2,1)S(1)}, bf16[256,512]{1,0:T(8,128)(2,1)S(1)}, u32[]{:S(2)}, u32[]{:S(2)}) %collective-permute-start.16) | collective-permute-done | bytes 262176 | tf_op jit(solution)/shard_map/ppermute | solution.py:286
  208.2 6.4 %collective-permute-done.12 = bf16[512,512]{1,0:T(8,128)(2,1)S(1)} collective-permute-done((bf16[512,512]{1,0:T(8,128)(2,1)S(1)}, bf16[512,512]{1,0:T(8,128)(2,1)S(1)}, u32[]{:S(2)}, u32[]{:S(2)}) %collective-permute-start.12) | collective-permute-done | bytes 524320 | tf_op jit(solution)/shard_map/ppermute | solution.py:296
  214.8 4.4 %collective-permute-start.21 = (bf16[512,512]{1,0:T(8,128)(2,1)S(1)}, bf16[512,512]{1,0:T(8,128)(2,1)S(1)}, u32[]{:S(2)}, u32[]{:S(2)}) collective-permute-start(bf16[512,512]{1,0:T(8,128)(2,1)S(1)} %add_convert_fusion.2), channel_id=1, source_target_pairs={{0,32},{32,0},{1,33},{33,1},{2,34},{34,2},{3,35},{35,3},{4,36},{36... | collective-permute-start | bytes 1572872 | tf_op jit(solution)/shard_map/ppermute | solution.py:299
  219.3 14.1 %all_to_all.24 = bf16[8,32,512]{2,1,0:T(8,128)(2,1)S(1)} all-to-all(bf16[8,32,512]{2,1,0:T(8,128)(2,1)S(1)} %bitcast.11), channel_id=1, replica_groups=mesh['j'=8,'p'=2,'x'=4,'head'=8] {'head'}, dimensions={0} | all-to-all | bytes 524288 | tf_op jit(solution)/shard_map/all_to_all | solution.py:303
  (82 shorter events, 26.3 us)
Async XLA Ops:
  7.2 105.4 %all-gather.3.cloned.1.call-start = ((), (), s32[]{:S(2)}) async-start(), calls=%async_computation.2 | async-start | bytes 4718592 | tf_op jit(solution)/shard_map/all_gather | solution.py:236
  11.1 101.5 %copy-start = (bf16[512,512]{1,0:T(8,128)(2,1)}, bf16[512,512]{1,0:T(8,128)(2,1)S(1)}, u32[]{:S(2)}) copy-start(bf16[512,512]{1,0:T(8,128)(2,1)S(1)} %constant_dynamic-update-slice_fusion.refs_6_) | copy-start | bytes 1572868
  11.1 11.4 %collective-permute-start = (bf16[512,512]{1,0:T(8,128)(2,1)S(1)}, bf16[512,512]{1,0:T(8,128)(2,1)S(1)}, u32[]{:S(2)}, u32[]{:S(2)}) collective-permute-start(bf16[512,512]{1,0:T(8,128)(2,1)S(1)} %constant_dynamic-update-slice_fusion.refs_6_), channel_id=1, source_target_pairs={{0,32},{32,0},{1,33},{33,1},{2,34},{34,2},{3,35},{35,3},{4,36},{36... | collective-permute-start | bytes 1572872 | tf_op jit(solution)/shard_map/ppermute | solution.py:239
  22.5 90.1 %copy-start.6 = (bf16[512,512]{1,0:T(8,128)(2,1)}, bf16[512,512]{1,0:T(8,128)(2,1)S(1)}, u32[]{:S(2)}) copy-start(bf16[512,512]{1,0:T(8,128)(2,1)S(1)} %collective-permute-done.refs_7_) | copy-start | bytes 1572868
  24.7 34.5 %all-to-all-start = ((f32[8,24,128]{2,1,0:T(8,128)}), f32[8,24,128]{2,1,0:T(8,128)S(1)}, u32[]{:S(2)}, u32[]{:S(2)}) async-start(f32[8,24,128]{2,1,0:T(8,128)} %broadcast_in_dim.14), calls=%async_computation | async-start | bytes 196608 | tf_op jit(solution)/shard_map/all_to_all | solution.py:254
  43.6 16.4 %collective-permute-start.5 = (bf16[512,512]{1,0:T(8,128)(2,1)S(1)}, bf16[512,512]{1,0:T(8,128)(2,1)S(1)}, u32[]{:S(2)}, u32[]{:S(2)}) collective-permute-start(bf16[512,512]{1,0:T(8,128)(2,1)S(1)} %constant_dynamic-update-slice_fusion.refs_6_), channel_id=1, source_target_pairs={{0,8},{8,16},{16,24},{24,0},{1,9},{9,17},{17,25},{25,1},{2,10},{10... | collective-permute-start | bytes 1572872 | tf_op jit(solution)/shard_map/ppermute | solution.py:243
  46.8 23.9 %collective-permute-start.3 = (bf16[512,512]{1,0:T(8,128)(2,1)S(1)}, bf16[512,512]{1,0:T(8,128)(2,1)S(1)}, u32[]{:S(2)}, u32[]{:S(2)}) collective-permute-start(bf16[512,512]{1,0:T(8,128)(2,1)S(1)} %constant_dynamic-update-slice_fusion.refs_6_), channel_id=1, source_target_pairs={{0,16},{8,24},{16,0},{24,8},{1,17},{9,25},{17,1},{25,9},{2,18},{10... | collective-permute-start | bytes 1572872 | tf_op jit(solution)/shard_map/ppermute | solution.py:243
  51.1 25.9 %collective-permute-start.1 = (bf16[512,512]{1,0:T(8,128)(2,1)S(1)}, bf16[512,512]{1,0:T(8,128)(2,1)S(1)}, u32[]{:S(2)}, u32[]{:S(2)}) collective-permute-start(bf16[512,512]{1,0:T(8,128)(2,1)S(1)} %constant_dynamic-update-slice_fusion.refs_6_), channel_id=1, source_target_pairs={{0,24},{8,0},{16,8},{24,16},{1,25},{9,1},{17,9},{25,17},{2,26},{10... | collective-permute-start | bytes 1572872 | tf_op jit(solution)/shard_map/ppermute | solution.py:243
  54.2 28.5 %collective-permute-start.6 = (bf16[512,512]{1,0:T(8,128)(2,1)S(1)}, bf16[512,512]{1,0:T(8,128)(2,1)S(1)}, u32[]{:S(2)}, u32[]{:S(2)}) collective-permute-start(bf16[512,512]{1,0:T(8,128)(2,1)S(1)} %collective-permute-done.refs_7_), channel_id=1, source_target_pairs={{0,8},{8,16},{16,24},{24,0},{1,9},{9,17},{17,25},{25,1},{2,10},{10... | collective-permute-start | bytes 1572872 | tf_op jit(solution)/shard_map/ppermute | solution.py:243
  56.4 36.7 %collective-permute-start.4 = (bf16[512,512]{1,0:T(8,128)(2,1)S(1)}, bf16[512,512]{1,0:T(8,128)(2,1)}, u32[]{:S(2)}, u32[]{:S(2)}) collective-permute-start(bf16[512,512]{1,0:T(8,128)(2,1)S(1)} %collective-permute-done.refs_7_), channel_id=1, source_target_pairs={{0,16},{8,24},{16,0},{24,8},{1,17},{9,25},{17,1},{25,9},{2,18},{10... | collective-permute-start | bytes 1572872 | tf_op jit(solution)/shard_map/ppermute | solution.py:243
  59.2 53.4 %copy-start.11 = (f32[8,24,128]{2,1,0:T(8,128)}, f32[8,24,128]{2,1,0:T(8,128)S(1)}, u32[]{:S(2)}) copy-start(f32[8,24,128]{2,1,0:T(8,128)S(1)} %all-to-all-done.refs_1_) | copy-start | bytes 294916
  60.0 52.6 %copy-start.7 = (bf16[512,512]{1,0:T(8,128)(2,1)}, bf16[512,512]{1,0:T(8,128)(2,1)S(1)}, u32[]{:S(2)}) copy-start(bf16[512,512]{1,0:T(8,128)(2,1)S(1)} %collective-permute-done.5.refs_12_) | copy-start | bytes 1572868
  60.0 35.7 %collective-permute-start.2 = (bf16[512,512]{1,0:T(8,128)(2,1)S(1)}, bf16[512,512]{1,0:T(8,128)(2,1)}, u32[]{:S(2)}, u32[]{:S(2)}) collective-permute-start(bf16[512,512]{1,0:T(8,128)(2,1)S(1)} %collective-permute-done.refs_7_), channel_id=1, source_target_pairs={{0,24},{8,0},{16,8},{24,16},{1,25},{9,1},{17,9},{25,17},{2,26},{10... | collective-permute-start | bytes 1572872 | tf_op jit(solution)/shard_map/ppermute | solution.py:243
  127.3 57.9 %copy-start.12 = (bf16[256,512]{1,0:T(8,128)(2,1)S(1)}, bf16[256,512]{1,0:T(8,128)(2,1)}, u32[]{:S(2)}) copy-start(bf16[256,512]{1,0:T(8,128)(2,1)} %get-tuple-element.78) | copy-start | bytes 786436
  127.3 59.9 %copy-start.3 = (bf16[512,512]{1,0:T(8,128)(2,1)S(1)}, bf16[512,512]{1,0:T(8,128)(2,1)}, u32[]{:S(2)}) copy-start(bf16[512,512]{1,0:T(8,128)(2,1)} %get-tuple-element.75) | copy-start | bytes 1572868
  127.3 15.6 %collective-permute-start.17 = (bf16[128,512]{1,0:T(8,128)(2,1)}, bf16[128,512]{1,0:T(8,128)(2,1)S(1)}, u32[]{:S(2)}, u32[]{:S(2)}) collective-permute-start(bf16[128,512]{1,0:T(8,128)(2,1)} %get-tuple-element.85), channel_id=1, source_target_pairs={{0,448},{64,0},{128,64},{192,128},{256,192},{320,256},{384,320},{4... | collective-permute-start | bytes 393224 | tf_op jit(solution)/shard_map/ppermute | solution.py:276
  130.3 77.6 %copy-start.5 = (f32[256,512]{1,0:T(8,128)S(1)}, f32[256,512]{1,0:T(8,128)}, u32[]{:S(2)}) copy-start(f32[256,512]{1,0:T(8,128)} %get-tuple-element.77) | copy-start | bytes 1572868
  131.2 15.9 %collective-permute-start.13 = (bf16[128,512]{1,0:T(8,128)(2,1)}, bf16[128,512]{1,0:T(8,128)(2,1)S(1)}, u32[]{:S(2)}, u32[]{:S(2)}) collective-permute-start(bf16[128,512]{1,0:T(8,128)(2,1)} %get-tuple-element.81), channel_id=1, source_target_pairs={{0,64},{64,128},{128,192},{192,256},{256,320},{320,384},{384,448},... | collective-permute-start | bytes 393224 | tf_op jit(solution)/shard_map/ppermute | solution.py:275
  135.5 34.9 %collective-permute-start.8 = (bf16[512,512]{1,0:T(8,128)(2,1)}, bf16[512,512]{1,0:T(8,128)(2,1)S(1)}, u32[]{:S(2)}, u32[]{:S(2)}) collective-permute-start(bf16[512,512]{1,0:T(8,128)(2,1)} %get-tuple-element.72), channel_id=1, source_target_pairs={{0,24},{8,0},{16,8},{24,16},{1,25},{9,1},{17,9},{25,17},{2,26},{10... | collective-permute-start | bytes 1572872 | tf_op jit(solution)/shard_map/ppermute | solution.py:291
  143.9 64.1 %copy-start.2 = (f32[512,512]{1,0:T(8,128)S(1)}, f32[512,512]{1,0:T(8,128)}, u32[]{:S(2)}) copy-start(f32[512,512]{1,0:T(8,128)} %get-tuple-element.69) | copy-start | bytes 3145732
  143.9 14.5 %collective-permute-start.18 = (bf16[256,512]{1,0:T(8,128)(2,1)S(1)}, bf16[256,512]{1,0:T(8,128)(2,1)S(1)}, u32[]{:S(2)}, u32[]{:S(2)}) collective-permute-start(bf16[256,512]{1,0:T(8,128)(2,1)S(1)} %pad_maximum_fusion.1), channel_id=1, source_target_pairs={{0,448},{64,0},{128,64},{192,128},{256,192},{320,256},{384,320},{4... | collective-permute-start | bytes 786440 | tf_op jit(solution)/shard_map/ppermute | solution.py:283
  148.2 13.2 %collective-permute-start.14 = (bf16[256,512]{1,0:T(8,128)(2,1)S(1)}, bf16[256,512]{1,0:T(8,128)(2,1)S(1)}, u32[]{:S(2)}, u32[]{:S(2)}) collective-permute-start(bf16[256,512]{1,0:T(8,128)(2,1)S(1)} %pad_maximum_fusion), channel_id=1, source_target_pairs={{0,64},{64,128},{128,192},{192,256},{256,320},{320,384},{384,448},... | collective-permute-start | bytes 786440 | tf_op jit(solution)/shard_map/ppermute | solution.py:282
  151.9 56.1 %collective-permute-start.7 = (bf16[512,512]{1,0:T(8,128)(2,1)}, bf16[512,512]{1,0:T(8,128)(2,1)S(1)}, u32[]{:S(2)}, u32[]{:S(2)}) collective-permute-start(bf16[512,512]{1,0:T(8,128)(2,1)} %get-tuple-element.70), channel_id=1, source_target_pairs={{0,8},{8,16},{16,24},{24,0},{1,9},{9,17},{17,25},{25,1},{2,10},{10... | collective-permute-start | bytes 1572872 | tf_op jit(solution)/shard_map/ppermute | solution.py:292
  153.8 54.4 %collective-permute-start.10 = (bf16[512,512]{1,0:T(8,128)(2,1)}, bf16[512,512]{1,0:T(8,128)(2,1)S(1)}, u32[]{:S(2)}, u32[]{:S(2)}) collective-permute-start(bf16[512,512]{1,0:T(8,128)(2,1)} %get-tuple-element.74), channel_id=1, source_target_pairs={{0,24},{8,0},{16,8},{24,16},{1,25},{9,1},{17,9},{25,17},{2,26},{10... | collective-permute-start | bytes 1572872 | tf_op jit(solution)/shard_map/ppermute | solution.py:293
  158.4 26.9 %collective-permute-start.11 = (bf16[512,512]{1,0:T(8,128)(2,1)}, bf16[512,512]{1,0:T(8,128)(2,1)S(1)}, u32[]{:S(2)}, u32[]{:S(2)}) collective-permute-start(bf16[512,512]{1,0:T(8,128)(2,1)} %get-tuple-element.76), channel_id=1, source_target_pairs={{0,8},{8,16},{16,24},{24,0},{1,9},{9,17},{17,25},{25,1},{2,10},{10... | collective-permute-start | bytes 1572872 | tf_op jit(solution)/shard_map/ppermute | solution.py:290
  161.3 11.5 %collective-permute-start.19 = (bf16[256,512]{1,0:T(8,128)(2,1)S(1)}, bf16[256,512]{1,0:T(8,128)(2,1)S(1)}, u32[]{:S(2)}, u32[]{:S(2)}) collective-permute-start(bf16[256,512]{1,0:T(8,128)(2,1)S(1)} %add_convert_fusion.6), channel_id=1, source_target_pairs={{0,448},{64,0},{128,64},{192,128},{256,192},{320,256},{384,320},{4... | collective-permute-start | bytes 786440 | tf_op jit(solution)/shard_map/ppermute | solution.py:283
  170.4 10.3 %collective-permute-start.15 = (bf16[256,512]{1,0:T(8,128)(2,1)S(1)}, bf16[256,512]{1,0:T(8,128)(2,1)S(1)}, u32[]{:S(2)}, u32[]{:S(2)}) collective-permute-start(bf16[256,512]{1,0:T(8,128)(2,1)S(1)} %add_convert_fusion.8), channel_id=1, source_target_pairs={{0,64},{64,128},{128,192},{192,256},{256,320},{320,384},{384,448},... | collective-permute-start | bytes 786440 | tf_op jit(solution)/shard_map/ppermute | solution.py:282
  172.8 35.2 %collective-permute-start.9 = (bf16[512,512]{1,0:T(8,128)(2,1)S(1)}, bf16[512,512]{1,0:T(8,128)(2,1)S(1)}, u32[]{:S(2)}, u32[]{:S(2)}) collective-permute-start(bf16[512,512]{1,0:T(8,128)(2,1)S(1)} %add_convert_fusion.3), channel_id=1, source_target_pairs={{0,24},{8,0},{16,8},{24,16},{1,25},{9,1},{17,9},{25,17},{2,26},{10... | collective-permute-start | bytes 1572872 | tf_op jit(solution)/shard_map/ppermute | solution.py:297
  180.7 8.0 %collective-permute-start.20 = (bf16[256,512]{1,0:T(8,128)(2,1)S(1)}, bf16[256,512]{1,0:T(8,128)(2,1)S(1)}, u32[]{:S(2)}, u32[]{:S(2)}) collective-permute-start(bf16[256,512]{1,0:T(8,128)(2,1)S(1)} %add_convert_fusion.5), channel_id=1, source_target_pairs={{0,448},{64,0},{128,64},{192,128},{256,192},{320,256},{384,320},{4... | collective-permute-start | bytes 786440 | tf_op jit(solution)/shard_map/ppermute | solution.py:287
  185.3 22.6 %collective-permute-start.16 = (bf16[256,512]{1,0:T(8,128)(2,1)S(1)}, bf16[256,512]{1,0:T(8,128)(2,1)S(1)}, u32[]{:S(2)}, u32[]{:S(2)}) collective-permute-start(bf16[256,512]{1,0:T(8,128)(2,1)S(1)} %add_convert_fusion.7), channel_id=1, source_target_pairs={{0,64},{64,128},{128,192},{192,256},{256,320},{320,384},{384,448},... | collective-permute-start | bytes 786440 | tf_op jit(solution)/shard_map/ppermute | solution.py:286
  188.7 25.9 %collective-permute-start.12 = (bf16[512,512]{1,0:T(8,128)(2,1)S(1)}, bf16[512,512]{1,0:T(8,128)(2,1)S(1)}, u32[]{:S(2)}, u32[]{:S(2)}) collective-permute-start(bf16[512,512]{1,0:T(8,128)(2,1)S(1)} %add_convert_fusion.1), channel_id=1, source_target_pairs={{0,8},{8,16},{16,24},{24,0},{1,9},{9,17},{17,25},{25,1},{2,10},{10... | collective-permute-start | bytes 1572872 | tf_op jit(solution)/shard_map/ppermute | solution.py:296
  214.8 19.2 %collective-permute-start.21 = (bf16[512,512]{1,0:T(8,128)(2,1)S(1)}, bf16[512,512]{1,0:T(8,128)(2,1)S(1)}, u32[]{:S(2)}, u32[]{:S(2)}) collective-permute-start(bf16[512,512]{1,0:T(8,128)(2,1)S(1)} %add_convert_fusion.2), channel_id=1, source_target_pairs={{0,32},{32,0},{1,33},{33,1},{2,34},{34,2},{3,35},{35,3},{4,36},{36... | collective-permute-start | bytes 1572872 | tf_op jit(solution)/shard_map/ppermute | solution.py:299
  (6 other events, 243.3 us)
Sparse Core Ops, SparseCore 0:
  10.1 102.4 all-gather.2

commit v9 on v7

--- a/solution.py
+++ b/solution.py
@@ -224,8 +224,9 @@
     )(queries, out_grad)
     packs = lax.all_gather(pack, "j")
     pack, selected, keys, values = lax.optimization_barrier((pack, selected, keys, values))
+    cross = [(i, (i + 1) % PAIR) for i in range(PAIR)]
+    swapped = jnp.concatenate([lax.ppermute(keys, "p", cross), lax.ppermute(values, "p", cross)], axis=0)
     both = jnp.concatenate([keys, values], axis=0)
-    swapped = lax.ppermute(both, "p", [(i, (i + 1) % PAIR) for i in range(PAIR)])
     kvs = [both, swapped]
     for shift in range(1, X_SIZE):
         back = [(i, (i - shift) % X_SIZE) for i in range(X_SIZE)]

time: 217 us -> 217 us (level)
  waiting for transfers between devices: 86.3 us -> 94.2 us
  starting transfers between devices: 69.9 us -> 63.7 us
    ppermute x1, starting transfers between devices: 8.85 us -> 3.49 us  [shards(): through_b = lax.ppermute(far_b, 'x', behind)]
    reduce_scatter x1, waiting for transfers between devices: 15 us -> 19.2 us  [shards(): sum_q = lax.psum_scatter(part_q, 'j', scatter_dimension=0)]
    all_gather x1, waiting for transfers between devices: 16.9 us -> 19.5 us  [shards(): packs = lax.all_gather(pack, 'j')]
    ppermute x1 -> x2, starting transfers between devices: 4.38 us -> 6.3 us  [the longest x1 4.38 us: shards(): lax.ppermute(keys, 'p', cross)]
  transfers between devices with their start and end apart: 17 -> 18, of which waited for: 12 -> 12; matrix products, arithmetic and copies ran while one was open for 5% -> 4% of each run, Pallas kernels for 2% -> 2%
where the time goes in v9:
time: 217 us; the launch traced here: 216 us
  waiting for transfers between devices  94.2 us (43%)
  starting transfers between devices  63.7 us (29%)
  Pallas kernels  20 us (9%)
  between operations  14.4 us (7%)
  blocking collectives  13.9 us (6%)
  other arithmetic  6.75 us (3%)
  local copies, waits for them, and re-layouts  2.59 us (1%)
    ppermute x6, waiting for transfers between devices, shards(): kvs += [lax.ppermute(both, 'x', back), lax.ppermute(swapped, 'x', back)]  30.6 us
    all_gather x1, waiting for transfers between devices, shards(): packs = lax.all_gather(pack, 'j')  19.5 us
    reduce_scatter x1, waiting for transfers between devices, shards(): sum_q = lax.psum_scatter(part_q, 'j', scatter_dimension=0)  19.2 us
    ppermute x6, starting transfers between devices, shards(): kvs += [lax.ppermute(both, 'x', back), lax.ppermute(swapped, 'x', back)]  19 us
    all_to_all x1, starting transfers between devices, shards(): lax.all_to_all(jnp.broadcast_to(info[None], (ring, *info.shape)), 'j', 0,...  18.8 us
    pallas_call x1, Pallas kernels, remote_call(): pl.pallas_call(functools.partial(remote_kernel, blocks, heads, factor, ow...  14.6 us
    all_to_all x1, blocking collectives, shards(): lax.all_to_all(sum_q, 'head', split_axis=0, concat_axis=1, tiled=True)  13.9 us
    ppermute x1, waiting for transfers between devices, shards(): from_last = lax.ppermute(last_a, 'x', behind)  11 us
  transfers between devices with their start and end apart: 18, of which 12 were waited for; matrix products, arithmetic and copies ran while one was open for 4% of the time, Pallas kernels for 2%

profile of v9, /device:TPU:1, one launch (start us, length us, event | category | flops | bytes accessed | tf_op | source)
XLA Modules:
  0.0 215.5 jit_solution(17675179471016898761)
XLA Ops:
  7.2 1.9 pack.1
  9.2 4.4 %collective-permute-start = (bf16[256,512]{1,0:T(8,128)(2,1)}, bf16[256,512]{1,0:T(8,128)(2,1)S(1)}, u32[]{:S(2)}, u32[]{:S(2)}) collective-permute-start(bf16[256,512]{1,0:T(8,128)(2,1)} %k_ref), channel_id=1, source_target_pairs={{0,32},{32,0},{1,33},{33,1},{2,34},{34,2},{3,35},{35,3},{4,36},{36... | collective-permute-start | bytes 786440 | tf_op jit(solution)/shard_map/ppermute | solution.py:228
  13.6 1.9 collective-permute-start.1
  15.5 3.5 %own.1 = (f32[16,128]{1,0:T(8,128)}, f32[256,512]{1,0:T(8,128)}, f32[256,512]{1,0:T(8,128)}, f32[256,512]{1,0:T(8,128)}) custom-call(bf16[256,512]{1,0:T(8,128)(2,1)} %q_ref.3, bf16[256,512]{1,0:T(8,128)(2,1)} %g_ref.3, bf16[256,512]{1,0:T(8,128)(2,1)} %o_ref.1, f32[4,256]{1,0:T(4,128)} %bitcast.15, bf16[256,512]{1,0:T(8,128)(2,1)} %k_ref, bf16[256,512]{1,0:T(8,128)(2,1)} %v_ref), custom_call_target="tpu_custom_call" | custom-call | tf_op jit(solution)/shard_map/own/pallas_call | solution.py:235
  19.0 1.9 collective-permute-done.1
  23.2 18.8 %all-to-all-start = ((f32[8,24,128]{2,1,0:T(8,128)}), f32[8,24,128]{2,1,0:T(8,128)S(1)}, u32[]{:S(2)}, u32[]{:S(2)}) async-start(f32[8,24,128]{2,1,0:T(8,128)} %broadcast_in_dim.14), calls=%async_computation | async-start | bytes 196608 | tf_op jit(solution)/shard_map/all_to_all | solution.py:244
  42.1 3.1 %collective-permute-start.6 = (bf16[512,512]{1,0:T(8,128)(2,1)S(1)}, bf16[512,512]{1,0:T(8,128)(2,1)S(1)}, u32[]{:S(2)}, u32[]{:S(2)}) collective-permute-start(bf16[512,512]{1,0:T(8,128)(2,1)S(1)} %constant_dynamic-update-slice_fusion.refs_6_), channel_id=1, source_target_pairs={{0,8},{8,16},{16,24},{24,0},{1,9},{9,17},{17,25},{25,1},{2,10},{10... | collective-permute-start | bytes 1572872 | tf_op jit(solution)/shard_map/ppermute | solution.py:233
  45.3 4.4 %collective-permute-start.4 = (bf16[512,512]{1,0:T(8,128)(2,1)S(1)}, bf16[512,512]{1,0:T(8,128)(2,1)S(1)}, u32[]{:S(2)}, u32[]{:S(2)}) collective-permute-start(bf16[512,512]{1,0:T(8,128)(2,1)S(1)} %constant_dynamic-update-slice_fusion.refs_6_), channel_id=1, source_target_pairs={{0,16},{8,24},{16,0},{24,8},{1,17},{9,25},{17,1},{25,9},{2,18},{10... | collective-permute-start | bytes 1572872 | tf_op jit(solution)/shard_map/ppermute | solution.py:233
  49.6 3.1 %collective-permute-start.2 = (bf16[512,512]{1,0:T(8,128)(2,1)S(1)}, bf16[512,512]{1,0:T(8,128)(2,1)S(1)}, u32[]{:S(2)}, u32[]{:S(2)}) collective-permute-start(bf16[512,512]{1,0:T(8,128)(2,1)S(1)} %constant_dynamic-update-slice_fusion.refs_6_), channel_id=1, source_target_pairs={{0,24},{8,0},{16,8},{24,16},{1,25},{9,1},{17,9},{25,17},{2,26},{10... | collective-permute-start | bytes 1572872 | tf_op jit(solution)/shard_map/ppermute | solution.py:233
  52.7 2.2 %collective-permute-start.7 = (bf16[512,512]{1,0:T(8,128)(2,1)S(1)}, bf16[512,512]{1,0:T(8,128)(2,1)S(1)}, u32[]{:S(2)}, u32[]{:S(2)}) collective-permute-start(bf16[512,512]{1,0:T(8,128)(2,1)S(1)} %constant_dynamic-update-slice_fusion.2.refs_7_), channel_id=1, source_target_pairs={{0,8},{8,16},{16,24},{24,0},{1,9},{9,17},{17,25},{25,1},{2,10},{10... | collective-permute-start | bytes 1572872 | tf_op jit(solution)/shard_map/ppermute | solution.py:233
  54.9 2.8 %collective-permute-start.5 = (bf16[512,512]{1,0:T(8,128)(2,1)S(1)}, bf16[512,512]{1,0:T(8,128)(2,1)}, u32[]{:S(2)}, u32[]{:S(2)}) collective-permute-start(bf16[512,512]{1,0:T(8,128)(2,1)S(1)} %constant_dynamic-update-slice_fusion.2.refs_7_), channel_id=1, source_target_pairs={{0,16},{8,24},{16,0},{24,8},{1,17},{9,25},{17,1},{25,9},{2,18},{10... | collective-permute-start | bytes 1572872 | tf_op jit(solution)/shard_map/ppermute | solution.py:233
  58.6 3.4 %collective-permute-start.3 = (bf16[512,512]{1,0:T(8,128)(2,1)S(1)}, bf16[512,512]{1,0:T(8,128)(2,1)}, u32[]{:S(2)}, u32[]{:S(2)}) collective-permute-start(bf16[512,512]{1,0:T(8,128)(2,1)S(1)} %constant_dynamic-update-slice_fusion.2.refs_7_), channel_id=1, source_target_pairs={{0,24},{8,0},{16,8},{24,16},{1,25},{9,1},{17,9},{25,17},{2,26},{10... | collective-permute-start | bytes 1572872 | tf_op jit(solution)/shard_map/ppermute | solution.py:233
  62.4 1.3 pad_add_fusion.refs_0_
  63.6 5.6 %collective-permute-done.4.refs_10_ = bf16[512,512]{1,0:T(8,128)(2,1)S(1)} collective-permute-done((bf16[512,512]{1,0:T(8,128)(2,1)S(1)}, bf16[512,512]{1,0:T(8,128)(2,1)S(1)}, u32[]{:S(2)}, u32[]{:S(2)}) %collective-permute-start.4) | collective-permute-done | bytes 524320 | tf_op jit(solution)/shard_map/ppermute | solution.py:233
  69.2 4.6 %collective-permute-done.2.refs_8_ = bf16[512,512]{1,0:T(8,128)(2,1)S(1)} collective-permute-done((bf16[512,512]{1,0:T(8,128)(2,1)S(1)}, bf16[512,512]{1,0:T(8,128)(2,1)S(1)}, u32[]{:S(2)}, u32[]{:S(2)}) %collective-permute-start.2) | collective-permute-done | bytes 524320 | tf_op jit(solution)/shard_map/ppermute | solution.py:233
  73.8 7.4 %collective-permute-done.7.refs_13_ = bf16[512,512]{1,0:T(8,128)(2,1)S(1)} collective-permute-done((bf16[512,512]{1,0:T(8,128)(2,1)S(1)}, bf16[512,512]{1,0:T(8,128)(2,1)S(1)}, u32[]{:S(2)}, u32[]{:S(2)}) %collective-permute-start.7) | collective-permute-done | bytes 524320 | tf_op jit(solution)/shard_map/ppermute | solution.py:233
  81.2 10.5 %collective-permute-done.5.refs_11_ = bf16[512,512]{1,0:T(8,128)(2,1)} collective-permute-done((bf16[512,512]{1,0:T(8,128)(2,1)S(1)}, bf16[512,512]{1,0:T(8,128)(2,1)}, u32[]{:S(2)}, u32[]{:S(2)}) %collective-permute-start.5) | collective-permute-done | bytes 524320 | tf_op jit(solution)/shard_map/ppermute | solution.py:233
  91.7 2.6 %collective-permute-done.3.refs_9_ = bf16[512,512]{1,0:T(8,128)(2,1)} collective-permute-done((bf16[512,512]{1,0:T(8,128)(2,1)S(1)}, bf16[512,512]{1,0:T(8,128)(2,1)}, u32[]{:S(2)}, u32[]{:S(2)}) %collective-permute-start.3) | collective-permute-done | bytes 524320 | tf_op jit(solution)/shard_map/ppermute | solution.py:233
  94.3 19.5 %all-gather.3.cloned.1.call-done = bf16[4096,512]{1,0:T(8,128)(2,1)} async-done(((bf16[512,512]{1,0:T(8,128)(2,1)}), bf16[4096,512]{1,0:T(8,128)(2,1)}) %all-gather.3.cloned.1.call-update) | async-done | bytes 4194320 | tf_op jit(solution)/shard_map/all_gather | solution.py:225
  113.8 14.6 %remote.1 = (bf16[8,256,512]{2,1,0:T(8,128)(2,1)}, f32[512,512]{1,0:T(8,128)}, f32[512,512]{1,0:T(8,128)}, bf16[512,512]{1,0:T(8,128)(2,1)}, bf16[512,512]{1,0:T...) custom-call(s32[130]{0:T(256)} %pad_add_fusion.refs_0_, ...), custom_call_target="tpu_custom_call" | custom-call | tf_op jit(solution)/shard_map/remote/pallas_call | solution.py:190
  128.5 3.5 %collective-permute-start.9 = (bf16[512,512]{1,0:T(8,128)(2,1)}, bf16[512,512]{1,0:T(8,128)(2,1)S(1)}, u32[]{:S(2)}, u32[]{:S(2)}) collective-permute-start(bf16[512,512]{1,0:T(8,128)(2,1)} %get-tuple-element.64), channel_id=1, source_target_pairs={{0,24},{8,0},{16,8},{24,16},{1,25},{9,1},{17,9},{25,17},{2,26},{10... | collective-permute-start | bytes 1572872 | tf_op jit(solution)/shard_map/ppermute | solution.py:262
  132.0 1.9 collective-permute-start.12
  133.9 2.9 %collective-permute-start.8 = (bf16[512,512]{1,0:T(8,128)(2,1)}, bf16[512,512]{1,0:T(8,128)(2,1)S(1)}, u32[]{:S(2)}, u32[]{:S(2)}) collective-permute-start(bf16[512,512]{1,0:T(8,128)(2,1)} %get-tuple-element.62), channel_id=1, source_target_pairs={{0,8},{8,16},{16,24},{24,0},{1,9},{9,17},{17,25},{25,1},{2,10},{10... | collective-permute-start | bytes 1572872 | tf_op jit(solution)/shard_map/ppermute | solution.py:263
  136.8 7.4 %collective-permute-done.9 = bf16[512,512]{1,0:T(8,128)(2,1)S(1)} collective-permute-done((bf16[512,512]{1,0:T(8,128)(2,1)}, bf16[512,512]{1,0:T(8,128)(2,1)S(1)}, u32[]{:S(2)}, u32[]{:S(2)}) %collective-permute-start.9) | collective-permute-done | bytes 524320 | tf_op jit(solution)/shard_map/ppermute | solution.py:262
  145.5 3.8 %collective-permute-start.10 = (bf16[512,512]{1,0:T(8,128)(2,1)S(1)}, bf16[512,512]{1,0:T(8,128)(2,1)S(1)}, u32[]{:S(2)}, u32[]{:S(2)}) collective-permute-start(bf16[512,512]{1,0:T(8,128)(2,1)S(1)} %add_convert_fusion.3), channel_id=1, source_target_pairs={{0,24},{8,0},{16,8},{24,16},{1,25},{9,1},{17,9},{25,17},{2,26},{10... | collective-permute-start | bytes 1572872 | tf_op jit(solution)/shard_map/ppermute | solution.py:268
  149.3 1.9 collective-permute-start.11
  152.4 3.4 %collective-permute-start.13 = (bf16[512,512]{1,0:T(8,128)(2,1)S(1)}, bf16[512,512]{1,0:T(8,128)(2,1)S(1)}, u32[]{:S(2)}, u32[]{:S(2)}) collective-permute-start(bf16[512,512]{1,0:T(8,128)(2,1)S(1)} %add_convert_fusion.1), channel_id=1, source_target_pairs={{0,8},{8,16},{16,24},{24,0},{1,9},{9,17},{17,25},{25,1},{2,10},{10... | collective-permute-start | bytes 1572872 | tf_op jit(solution)/shard_map/ppermute | solution.py:267
  155.7 3.4 %collective-permute-done.8 = bf16[512,512]{1,0:T(8,128)(2,1)S(1)} collective-permute-done((bf16[512,512]{1,0:T(8,128)(2,1)}, bf16[512,512]{1,0:T(8,128)(2,1)S(1)}, u32[]{:S(2)}, u32[]{:S(2)}) %collective-permute-start.8) | collective-permute-done | bytes 524320 | tf_op jit(solution)/shard_map/ppermute | solution.py:263
  160.4 11.0 %collective-permute-done.11 = bf16[512,512]{1,0:T(8,128)(2,1)S(1)} collective-permute-done((bf16[512,512]{1,0:T(8,128)(2,1)}, bf16[512,512]{1,0:T(8,128)(2,1)S(1)}, u32[]{:S(2)}, u32[]{:S(2)}) %collective-permute-start.11) | collective-permute-done | bytes 524320 | tf_op jit(solution)/shard_map/ppermute | solution.py:264
  171.6 19.2 %reduce-scatter.2.cloned.1.call-done = bf16[1,256,512]{2,1,0:T(8,128)(2,1)} async-done(((bf16[8,256,512]{2,1,0:T(8,128)(2,1)}), bf16[1,256,512]{2,1,0:T(8,128)(2,1)}) %reduce-scatter.2.cloned.1.call-update) | async-done | bytes 262160 | tf_op jit(solution)/shard_map/reduce_scatter | solution.py:254
  190.9 2.2 collective-permute-start.14
  193.0 13.9 %all_to_all.24 = bf16[8,32,512]{2,1,0:T(8,128)(2,1)S(1)} all-to-all(bf16[8,32,512]{2,1,0:T(8,128)(2,1)} %bitcast.13), channel_id=1, replica_groups=mesh['j'=8,'p'=2,'x'=4,'head'=8] {'head'}, dimensions={0} | all-to-all | bytes 524288 | tf_op jit(solution)/shard_map/all_to_all | solution.py:274
  (56 shorter events, 9.3 us)
Async XLA Ops:
  7.2 34.9 %copy-start.4 = (bf16[256,512]{1,0:T(8,128)(2,1)S(1)}, bf16[256,512]{1,0:T(8,128)(2,1)}, u32[]{:S(2)}) copy-start(bf16[256,512]{1,0:T(8,128)(2,1)} %v_ref) | copy-start | bytes 786436
  7.2 34.9 %copy-start.3 = (bf16[256,512]{1,0:T(8,128)(2,1)S(1)}, bf16[256,512]{1,0:T(8,128)(2,1)}, u32[]{:S(2)}) copy-start(bf16[256,512]{1,0:T(8,128)(2,1)} %k_ref) | copy-start | bytes 786436
  7.2 106.6 %all-gather.3.cloned.1.call-start = ((), (), s32[]{:S(2)}) async-start(), calls=%async_computation.4 | async-start | bytes 4718592 | tf_op jit(solution)/shard_map/all_gather | solution.py:225
  9.2 9.8 %collective-permute-start = (bf16[256,512]{1,0:T(8,128)(2,1)}, bf16[256,512]{1,0:T(8,128)(2,1)S(1)}, u32[]{:S(2)}, u32[]{:S(2)}) collective-permute-start(bf16[256,512]{1,0:T(8,128)(2,1)} %k_ref), channel_id=1, source_target_pairs={{0,32},{32,0},{1,33},{33,1},{2,34},{34,2},{3,35},{35,3},{4,36},{36... | collective-permute-start | bytes 786440 | tf_op jit(solution)/shard_map/ppermute | solution.py:228
  13.6 7.4 %collective-permute-start.1 = (bf16[256,512]{1,0:T(8,128)(2,1)}, bf16[256,512]{1,0:T(8,128)(2,1)S(1)}, u32[]{:S(2)}, u32[]{:S(2)}) collective-permute-start(bf16[256,512]{1,0:T(8,128)(2,1)} %v_ref), channel_id=1, source_target_pairs={{0,32},{32,0},{1,33},{33,1},{2,34},{34,2},{3,35},{35,3},{4,36},{36... | collective-permute-start | bytes 786440 | tf_op jit(solution)/shard_map/ppermute | solution.py:228
  21.0 92.8 %copy-start = (bf16[512,512]{1,0:T(8,128)(2,1)}, bf16[512,512]{1,0:T(8,128)(2,1)S(1)}, u32[]{:S(2)}) copy-start(bf16[512,512]{1,0:T(8,128)(2,1)S(1)} %constant_dynamic-update-slice_fusion.2.refs_7_) | copy-start | bytes 1572868
  23.2 34.5 %all-to-all-start = ((f32[8,24,128]{2,1,0:T(8,128)}), f32[8,24,128]{2,1,0:T(8,128)S(1)}, u32[]{:S(2)}, u32[]{:S(2)}) async-start(f32[8,24,128]{2,1,0:T(8,128)} %broadcast_in_dim.14), calls=%async_computation | async-start | bytes 196608 | tf_op jit(solution)/shard_map/all_to_all | solution.py:244
  42.0 148.9 %reduce-scatter.2.cloned.1.call-start = ((), (), s32[]{:S(2)}) async-start(), calls=%async_computation.3 | async-start | bytes 2359296 | tf_op jit(solution)/shard_map/reduce_scatter | solution.py:254
  42.1 71.7 %copy-start.1 = (bf16[512,512]{1,0:T(8,128)(2,1)}, bf16[512,512]{1,0:T(8,128)(2,1)S(1)}, u32[]{:S(2)}) copy-start(bf16[512,512]{1,0:T(8,128)(2,1)S(1)} %constant_dynamic-update-slice_fusion.refs_6_) | copy-start | bytes 1572868
  42.1 16.4 %collective-permute-start.6 = (bf16[512,512]{1,0:T(8,128)(2,1)S(1)}, bf16[512,512]{1,0:T(8,128)(2,1)S(1)}, u32[]{:S(2)}, u32[]{:S(2)}) collective-permute-start(bf16[512,512]{1,0:T(8,128)(2,1)S(1)} %constant_dynamic-update-slice_fusion.refs_6_), channel_id=1, source_target_pairs={{0,8},{8,16},{16,24},{24,0},{1,9},{9,17},{17,25},{25,1},{2,10},{10... | collective-permute-start | bytes 1572872 | tf_op jit(solution)/shard_map/ppermute | solution.py:233
  45.3 23.9 %collective-permute-start.4 = (bf16[512,512]{1,0:T(8,128)(2,1)S(1)}, bf16[512,512]{1,0:T(8,128)(2,1)S(1)}, u32[]{:S(2)}, u32[]{:S(2)}) collective-permute-start(bf16[512,512]{1,0:T(8,128)(2,1)S(1)} %constant_dynamic-update-slice_fusion.refs_6_), channel_id=1, source_target_pairs={{0,16},{8,24},{16,0},{24,8},{1,17},{9,25},{17,1},{25,9},{2,18},{10... | collective-permute-start | bytes 1572872 | tf_op jit(solution)/shard_map/ppermute | solution.py:233
  49.6 24.2 %collective-permute-start.2 = (bf16[512,512]{1,0:T(8,128)(2,1)S(1)}, bf16[512,512]{1,0:T(8,128)(2,1)S(1)}, u32[]{:S(2)}, u32[]{:S(2)}) collective-permute-start(bf16[512,512]{1,0:T(8,128)(2,1)S(1)} %constant_dynamic-update-slice_fusion.refs_6_), channel_id=1, source_target_pairs={{0,24},{8,0},{16,8},{24,16},{1,25},{9,1},{17,9},{25,17},{2,26},{10... | collective-permute-start | bytes 1572872 | tf_op jit(solution)/shard_map/ppermute | solution.py:233
  52.7 28.5 %collective-permute-start.7 = (bf16[512,512]{1,0:T(8,128)(2,1)S(1)}, bf16[512,512]{1,0:T(8,128)(2,1)S(1)}, u32[]{:S(2)}, u32[]{:S(2)}) collective-permute-start(bf16[512,512]{1,0:T(8,128)(2,1)S(1)} %constant_dynamic-update-slice_fusion.2.refs_7_), channel_id=1, source_target_pairs={{0,8},{8,16},{16,24},{24,0},{1,9},{9,17},{17,25},{25,1},{2,10},{10... | collective-permute-start | bytes 1572872 | tf_op jit(solution)/shard_map/ppermute | solution.py:233
  54.9 36.7 %collective-permute-start.5 = (bf16[512,512]{1,0:T(8,128)(2,1)S(1)}, bf16[512,512]{1,0:T(8,128)(2,1)}, u32[]{:S(2)}, u32[]{:S(2)}) collective-permute-start(bf16[512,512]{1,0:T(8,128)(2,1)S(1)} %constant_dynamic-update-slice_fusion.2.refs_7_), channel_id=1, source_target_pairs={{0,16},{8,24},{16,0},{24,8},{1,17},{9,25},{17,1},{25,9},{2,18},{10... | collective-permute-start | bytes 1572872 | tf_op jit(solution)/shard_map/ppermute | solution.py:233
  57.8 56.1 %copy-start.10 = (f32[8,24,128]{2,1,0:T(8,128)}, f32[8,24,128]{2,1,0:T(8,128)S(1)}, u32[]{:S(2)}) copy-start(f32[8,24,128]{2,1,0:T(8,128)S(1)} %all-to-all-done.refs_1_) | copy-start | bytes 294916
  58.6 55.2 %copy-start.6 = (bf16[512,512]{1,0:T(8,128)(2,1)}, bf16[512,512]{1,0:T(8,128)(2,1)S(1)}, u32[]{:S(2)}) copy-start(bf16[512,512]{1,0:T(8,128)(2,1)S(1)} %collective-permute-done.6.refs_12_) | copy-start | bytes 1572868
  58.6 35.7 %collective-permute-start.3 = (bf16[512,512]{1,0:T(8,128)(2,1)S(1)}, bf16[512,512]{1,0:T(8,128)(2,1)}, u32[]{:S(2)}, u32[]{:S(2)}) collective-permute-start(bf16[512,512]{1,0:T(8,128)(2,1)S(1)} %constant_dynamic-update-slice_fusion.2.refs_7_), channel_id=1, source_target_pairs={{0,24},{8,0},{16,8},{24,16},{1,25},{9,1},{17,9},{25,17},{2,26},{10... | collective-permute-start | bytes 1572872 | tf_op jit(solution)/shard_map/ppermute | solution.py:233
  69.2 44.6 %copy-start.7 = (bf16[512,512]{1,0:T(8,128)(2,1)}, bf16[512,512]{1,0:T(8,128)(2,1)S(1)}, u32[]{:S(2)}) copy-start(bf16[512,512]{1,0:T(8,128)(2,1)S(1)} %collective-permute-done.4.refs_10_) | copy-start | bytes 1572868
  73.8 40.0 %copy-start.8 = (bf16[512,512]{1,0:T(8,128)(2,1)}, bf16[512,512]{1,0:T(8,128)(2,1)S(1)}, u32[]{:S(2)}) copy-start(bf16[512,512]{1,0:T(8,128)(2,1)S(1)} %collective-permute-done.2.refs_8_) | copy-start | bytes 1572868
  81.2 32.7 %copy-start.9 = (bf16[512,512]{1,0:T(8,128)(2,1)}, bf16[512,512]{1,0:T(8,128)(2,1)S(1)}, u32[]{:S(2)}) copy-start(bf16[512,512]{1,0:T(8,128)(2,1)S(1)} %collective-permute-done.7.refs_13_) | copy-start | bytes 1572868
  128.4 31.8 %copy-start.5 = (f32[512,512]{1,0:T(8,128)S(1)}, f32[512,512]{1,0:T(8,128)}, u32[]{:S(2)}) copy-start(f32[512,512]{1,0:T(8,128)} %get-tuple-element.61) | copy-start | bytes 3145732
  128.4 43.0 %copy-start.2 = (f32[512,512]{1,0:T(8,128)S(1)}, f32[512,512]{1,0:T(8,128)}, u32[]{:S(2)}) copy-start(f32[512,512]{1,0:T(8,128)} %get-tuple-element.65) | copy-start | bytes 3145732
  128.5 15.8 %collective-permute-start.9 = (bf16[512,512]{1,0:T(8,128)(2,1)}, bf16[512,512]{1,0:T(8,128)(2,1)S(1)}, u32[]{:S(2)}, u32[]{:S(2)}) collective-permute-start(bf16[512,512]{1,0:T(8,128)(2,1)} %get-tuple-element.64), channel_id=1, source_target_pairs={{0,24},{8,0},{16,8},{24,16},{1,25},{9,1},{17,9},{25,17},{2,26},{10... | collective-permute-start | bytes 1572872 | tf_op jit(solution)/shard_map/ppermute | solution.py:262
  132.0 19.2 %collective-permute-start.12 = (bf16[512,512]{1,0:T(8,128)(2,1)}, bf16[512,512]{1,0:T(8,128)(2,1)S(1)}, u32[]{:S(2)}, u32[]{:S(2)}) collective-permute-start(bf16[512,512]{1,0:T(8,128)(2,1)} %get-tuple-element.68), channel_id=1, source_target_pairs={{0,8},{8,16},{16,24},{24,0},{1,9},{9,17},{17,25},{25,1},{2,10},{10... | collective-permute-start | bytes 1572872 | tf_op jit(solution)/shard_map/ppermute | solution.py:261
  133.9 25.2 %collective-permute-start.8 = (bf16[512,512]{1,0:T(8,128)(2,1)}, bf16[512,512]{1,0:T(8,128)(2,1)S(1)}, u32[]{:S(2)}, u32[]{:S(2)}) collective-permute-start(bf16[512,512]{1,0:T(8,128)(2,1)} %get-tuple-element.62), channel_id=1, source_target_pairs={{0,8},{8,16},{16,24},{24,0},{1,9},{9,17},{17,25},{25,1},{2,10},{10... | collective-permute-start | bytes 1572872 | tf_op jit(solution)/shard_map/ppermute | solution.py:263
  145.5 14.7 %collective-permute-start.10 = (bf16[512,512]{1,0:T(8,128)(2,1)S(1)}, bf16[512,512]{1,0:T(8,128)(2,1)S(1)}, u32[]{:S(2)}, u32[]{:S(2)}) collective-permute-start(bf16[512,512]{1,0:T(8,128)(2,1)S(1)} %add_convert_fusion.3), channel_id=1, source_target_pairs={{0,24},{8,0},{16,8},{24,16},{1,25},{9,1},{17,9},{25,17},{2,26},{10... | collective-permute-start | bytes 1572872 | tf_op jit(solution)/shard_map/ppermute | solution.py:268
  149.3 22.2 %collective-permute-start.11 = (bf16[512,512]{1,0:T(8,128)(2,1)}, bf16[512,512]{1,0:T(8,128)(2,1)S(1)}, u32[]{:S(2)}, u32[]{:S(2)}) collective-permute-start(bf16[512,512]{1,0:T(8,128)(2,1)} %get-tuple-element.66), channel_id=1, source_target_pairs={{0,24},{8,0},{16,8},{24,16},{1,25},{9,1},{17,9},{25,17},{2,26},{10... | collective-permute-start | bytes 1572872 | tf_op jit(solution)/shard_map/ppermute | solution.py:264
  152.4 19.1 %collective-permute-start.13 = (bf16[512,512]{1,0:T(8,128)(2,1)S(1)}, bf16[512,512]{1,0:T(8,128)(2,1)S(1)}, u32[]{:S(2)}, u32[]{:S(2)}) collective-permute-start(bf16[512,512]{1,0:T(8,128)(2,1)S(1)} %add_convert_fusion.1), channel_id=1, source_target_pairs={{0,8},{8,16},{16,24},{24,0},{1,9},{9,17},{17,25},{25,1},{2,10},{10... | collective-permute-start | bytes 1572872 | tf_op jit(solution)/shard_map/ppermute | solution.py:267
  190.9 16.8 %collective-permute-start.14 = (bf16[512,512]{1,0:T(8,128)(2,1)S(1)}, bf16[512,512]{1,0:T(8,128)(2,1)S(1)}, u32[]{:S(2)}, u32[]{:S(2)}) collective-permute-start(bf16[512,512]{1,0:T(8,128)(2,1)S(1)} %add_convert_fusion.2), channel_id=1, source_target_pairs={{0,32},{32,0},{1,33},{33,1},{2,34},{34,2},{3,35},{35,3},{4,36},{36... | collective-permute-start | bytes 1572872 | tf_op jit(solution)/shard_map/ppermute | solution.py:270
Sparse Core Ops, SparseCore 0:
  10.1 103.6 all-gather.2
  128.6 62.2 reduce-scatter.1

commit v10 on v7

--- a/solution.py
+++ b/solution.py
@@ -15,6 +15,7 @@
 TURN_SIZES = (16, 4)
 F32 = jnp.float32
 BF16 = jnp.bfloat16
+LARGEST = float(jnp.finfo(jnp.bfloat16).max)
 PARAMS = pltpu.CompilerParams(vmem_limit_bytes=56 * 1024 * 1024)
 
 
@@ -43,6 +44,7 @@
     scores = products[:, :BLOCK] * factor
     weights = jnp.where(keep, jnp.exp(scores - norm), 0.0)
     dscores = weights * (products[:, BLOCK:] - delta)
+    dscores = jnp.clip(dscores, -LARGEST, LARGEST)
     weights_b = weights.astype(BF16)
     dscores_b = dscores.astype(BF16)
     grads = mm(jnp.concatenate([dscores_b, weights_b], axis=1), queries, 1, 0)

time: 217 us -> 217 us (level)
    ppermute x1, waiting for transfers between devices: 7.02 us -> 4.56 us  [shards(): through_b = lax.ppermute(far_b, 'x', behind)]
where the time goes in v10:
time: 217 us; the launch traced here: 216 us
  waiting for transfers between devices  86.7 us (40%)
  starting transfers between devices  68.8 us (32%)
  Pallas kernels  20.9 us (10%)
  between operations  14.3 us (7%)
  blocking collectives  14 us (6%)
  other arithmetic  6.64 us (3%)
  local copies, waits for them, and re-layouts  4.45 us (2%)
    ppermute x6, waiting for transfers between devices, shards(): kvs += [lax.ppermute(both, 'x', back), lax.ppermute(swapped, 'x', back)]  29.5 us
    ppermute x6, starting transfers between devices, shards(): kvs += [lax.ppermute(both, 'x', back), lax.ppermute(swapped, 'x', back)]  20.2 us
    all_to_all x1, starting transfers between devices, shards(): lax.all_to_all(jnp.broadcast_to(info[None], (ring, *info.shape)), 'j', 0,...  18.9 us
    all_gather x1, waiting for transfers between devices, shards(): packs = lax.all_gather(pack, 'j')  16.9 us
    reduce_scatter x1, waiting for transfers between devices, shards(): sum_q = lax.psum_scatter(part_q, 'j', scatter_dimension=0)  16.8 us
    pallas_call x1, Pallas kernels, remote_call(): pl.pallas_call(functools.partial(remote_kernel, blocks, heads, factor, ow...  15.5 us
    all_to_all x1, blocking collectives, shards(): lax.all_to_all(sum_q, 'head', split_axis=0, concat_axis=1, tiled=True)  14 us
    ppermute x1, waiting for transfers between devices, shards(): from_last = lax.ppermute(last_a, 'x', behind)  11 us
  transfers between devices with their start and end apart: 17, of which 12 were waited for; matrix products, arithmetic and copies ran while one was open for 5% of the time, Pallas kernels for 2%

profile of v10, /device:TPU:1, one launch (start us, length us, event | category | flops | bytes accessed | tf_op | source)
XLA Modules:
  0.0 215.8 jit_solution(6709367232898938200)
XLA Ops:
  7.2 1.9 pack.1
  11.1 4.4 %collective-permute-start = (bf16[512,512]{1,0:T(8,128)(2,1)S(1)}, bf16[512,512]{1,0:T(8,128)(2,1)S(1)}, u32[]{:S(2)}, u32[]{:S(2)}) collective-permute-start(bf16[512,512]{1,0:T(8,128)(2,1)S(1)} %constant_dynamic-update-slice_fusion.refs_6_), channel_id=1, source_target_pairs={{0,32},{32,0},{1,33},{33,1},{2,34},{34,2},{3,35},{35,3},{4,36},{36... | collective-permute-start | bytes 1572872 | tf_op jit(solution)/shard_map/ppermute | solution.py:230
  15.4 3.5 %own.1 = (f32[16,128]{1,0:T(8,128)}, f32[256,512]{1,0:T(8,128)}, f32[256,512]{1,0:T(8,128)}, f32[256,512]{1,0:T(8,128)}) custom-call(bf16[256,512]{1,0:T(8,128)(2,1)} %q_ref.3, bf16[256,512]{1,0:T(8,128)(2,1)} %g_ref.3, bf16[256,512]{1,0:T(8,128)(2,1)} %o_ref.1, f32[4,256]{1,0:T(4,128)} %bitcast.15, bf16[256,512]{1,0:T(8,128)(2,1)} %k_ref, bf16[256,512]{1,0:T(8,128)(2,1)} %v_ref), custom_call_target="tpu_custom_call" | custom-call | tf_op jit(solution)/shard_map/own/pallas_call | solution.py:236
  19.0 3.5 %collective-permute-done.refs_7_ = bf16[512,512]{1,0:T(8,128)(2,1)S(1)} collective-permute-done((bf16[512,512]{1,0:T(8,128)(2,1)S(1)}, bf16[512,512]{1,0:T(8,128)(2,1)S(1)}, u32[]{:S(2)}, u32[]{:S(2)}) %collective-permute-start) | collective-permute-done | bytes 524320 | tf_op jit(solution)/shard_map/ppermute | solution.py:230
  24.7 18.9 %all-to-all-start = ((f32[8,24,128]{2,1,0:T(8,128)}), f32[8,24,128]{2,1,0:T(8,128)S(1)}, u32[]{:S(2)}, u32[]{:S(2)}) async-start(f32[8,24,128]{2,1,0:T(8,128)} %broadcast_in_dim.14), calls=%async_computation | async-start | bytes 196608 | tf_op jit(solution)/shard_map/all_to_all | solution.py:245
  43.7 3.1 %collective-permute-start.5 = (bf16[512,512]{1,0:T(8,128)(2,1)S(1)}, bf16[512,512]{1,0:T(8,128)(2,1)S(1)}, u32[]{:S(2)}, u32[]{:S(2)}) collective-permute-start(bf16[512,512]{1,0:T(8,128)(2,1)S(1)} %constant_dynamic-update-slice_fusion.refs_6_), channel_id=1, source_target_pairs={{0,8},{8,16},{16,24},{24,0},{1,9},{9,17},{17,25},{25,1},{2,10},{10... | collective-permute-start | bytes 1572872 | tf_op jit(solution)/shard_map/ppermute | solution.py:234
  46.8 4.4 %collective-permute-start.3 = (bf16[512,512]{1,0:T(8,128)(2,1)S(1)}, bf16[512,512]{1,0:T(8,128)(2,1)S(1)}, u32[]{:S(2)}, u32[]{:S(2)}) collective-permute-start(bf16[512,512]{1,0:T(8,128)(2,1)S(1)} %constant_dynamic-update-slice_fusion.refs_6_), channel_id=1, source_target_pairs={{0,16},{8,24},{16,0},{24,8},{1,17},{9,25},{17,1},{25,9},{2,18},{10... | collective-permute-start | bytes 1572872 | tf_op jit(solution)/shard_map/ppermute | solution.py:234
  51.2 3.1 %collective-permute-start.1 = (bf16[512,512]{1,0:T(8,128)(2,1)S(1)}, bf16[512,512]{1,0:T(8,128)(2,1)S(1)}, u32[]{:S(2)}, u32[]{:S(2)}) collective-permute-start(bf16[512,512]{1,0:T(8,128)(2,1)S(1)} %constant_dynamic-update-slice_fusion.refs_6_), channel_id=1, source_target_pairs={{0,24},{8,0},{16,8},{24,16},{1,25},{9,1},{17,9},{25,17},{2,26},{10... | collective-permute-start | bytes 1572872 | tf_op jit(solution)/shard_map/ppermute | solution.py:234
  54.2 2.2 %collective-permute-start.6 = (bf16[512,512]{1,0:T(8,128)(2,1)S(1)}, bf16[512,512]{1,0:T(8,128)(2,1)S(1)}, u32[]{:S(2)}, u32[]{:S(2)}) collective-permute-start(bf16[512,512]{1,0:T(8,128)(2,1)S(1)} %collective-permute-done.refs_7_), channel_id=1, source_target_pairs={{0,8},{8,16},{16,24},{24,0},{1,9},{9,17},{17,25},{25,1},{2,10},{10... | collective-permute-start | bytes 1572872 | tf_op jit(solution)/shard_map/ppermute | solution.py:234
  56.5 2.8 %collective-permute-start.4 = (bf16[512,512]{1,0:T(8,128)(2,1)S(1)}, bf16[512,512]{1,0:T(8,128)(2,1)}, u32[]{:S(2)}, u32[]{:S(2)}) collective-permute-start(bf16[512,512]{1,0:T(8,128)(2,1)S(1)} %collective-permute-done.refs_7_), channel_id=1, source_target_pairs={{0,16},{8,24},{16,0},{24,8},{1,17},{9,25},{17,1},{25,9},{2,18},{10... | collective-permute-start | bytes 1572872 | tf_op jit(solution)/shard_map/ppermute | solution.py:234
  60.1 4.6 %collective-permute-start.2 = (bf16[512,512]{1,0:T(8,128)(2,1)S(1)}, bf16[512,512]{1,0:T(8,128)(2,1)}, u32[]{:S(2)}, u32[]{:S(2)}) collective-permute-start(bf16[512,512]{1,0:T(8,128)(2,1)S(1)} %collective-permute-done.refs_7_), channel_id=1, source_target_pairs={{0,24},{8,0},{16,8},{24,16},{1,25},{9,1},{17,9},{25,17},{2,26},{10... | collective-permute-start | bytes 1572872 | tf_op jit(solution)/shard_map/ppermute | solution.py:234
  65.1 1.3 pad_add_fusion.refs_0_
  66.3 4.4 %collective-permute-done.3.refs_10_ = bf16[512,512]{1,0:T(8,128)(2,1)S(1)} collective-permute-done((bf16[512,512]{1,0:T(8,128)(2,1)S(1)}, bf16[512,512]{1,0:T(8,128)(2,1)S(1)}, u32[]{:S(2)}, u32[]{:S(2)}) %collective-permute-start.3) | collective-permute-done | bytes 524320 | tf_op jit(solution)/shard_map/ppermute | solution.py:234
  70.7 6.3 %collective-permute-done.1.refs_8_ = bf16[512,512]{1,0:T(8,128)(2,1)S(1)} collective-permute-done((bf16[512,512]{1,0:T(8,128)(2,1)S(1)}, bf16[512,512]{1,0:T(8,128)(2,1)S(1)}, u32[]{:S(2)}, u32[]{:S(2)}) %collective-permute-start.1) | collective-permute-done | bytes 524320 | tf_op jit(solution)/shard_map/ppermute | solution.py:234
  77.1 5.6 %collective-permute-done.6.refs_13_ = bf16[512,512]{1,0:T(8,128)(2,1)S(1)} collective-permute-done((bf16[512,512]{1,0:T(8,128)(2,1)S(1)}, bf16[512,512]{1,0:T(8,128)(2,1)S(1)}, u32[]{:S(2)}, u32[]{:S(2)}) %collective-permute-start.6) | collective-permute-done | bytes 524320 | tf_op jit(solution)/shard_map/ppermute | solution.py:234
  82.7 10.5 %collective-permute-done.4.refs_11_ = bf16[512,512]{1,0:T(8,128)(2,1)} collective-permute-done((bf16[512,512]{1,0:T(8,128)(2,1)S(1)}, bf16[512,512]{1,0:T(8,128)(2,1)}, u32[]{:S(2)}, u32[]{:S(2)}) %collective-permute-start.4) | collective-permute-done | bytes 524320 | tf_op jit(solution)/shard_map/ppermute | solution.py:234
  93.2 2.6 %collective-permute-done.2.refs_9_ = bf16[512,512]{1,0:T(8,128)(2,1)} collective-permute-done((bf16[512,512]{1,0:T(8,128)(2,1)S(1)}, bf16[512,512]{1,0:T(8,128)(2,1)}, u32[]{:S(2)}, u32[]{:S(2)}) %collective-permute-start.2) | collective-permute-done | bytes 524320 | tf_op jit(solution)/shard_map/ppermute | solution.py:234
  95.8 16.9 %all-gather.3.cloned.1.call-done = bf16[4096,512]{1,0:T(8,128)(2,1)} async-done(((bf16[512,512]{1,0:T(8,128)(2,1)}), bf16[4096,512]{1,0:T(8,128)(2,1)}) %all-gather.3.cloned.1.call-update) | async-done | bytes 4194320 | tf_op jit(solution)/shard_map/all_gather | solution.py:227
  112.8 15.5 %remote.1 = (bf16[8,256,512]{2,1,0:T(8,128)(2,1)}, f32[512,512]{1,0:T(8,128)}, f32[512,512]{1,0:T(8,128)}, bf16[512,512]{1,0:T(8,128)(2,1)}, bf16[512,512]{1,0:T...) custom-call(s32[130]{0:T(256)} %pad_add_fusion.refs_0_, ...), custom_call_target="tpu_custom_call" | custom-call | tf_op jit(solution)/shard_map/remote/pallas_call | solution.py:192
  128.3 7.5 %collective-permute-start.8 = (bf16[512,512]{1,0:T(8,128)(2,1)}, bf16[512,512]{1,0:T(8,128)(2,1)S(1)}, u32[]{:S(2)}, u32[]{:S(2)}) collective-permute-start(bf16[512,512]{1,0:T(8,128)(2,1)} %get-tuple-element.64), channel_id=1, source_target_pairs={{0,24},{8,0},{16,8},{24,16},{1,25},{9,1},{17,9},{25,17},{2,26},{10... | collective-permute-start | bytes 1572872 | tf_op jit(solution)/shard_map/ppermute | solution.py:263
  135.9 1.9 collective-permute-start.11
  137.8 3.0 %collective-permute-start.7 = (bf16[512,512]{1,0:T(8,128)(2,1)}, bf16[512,512]{1,0:T(8,128)(2,1)S(1)}, u32[]{:S(2)}, u32[]{:S(2)}) collective-permute-start(bf16[512,512]{1,0:T(8,128)(2,1)} %get-tuple-element.62), channel_id=1, source_target_pairs={{0,8},{8,16},{16,24},{24,0},{1,9},{9,17},{17,25},{25,1},{2,10},{10... | collective-permute-start | bytes 1572872 | tf_op jit(solution)/shard_map/ppermute | solution.py:264
  140.8 4.6 %collective-permute-done.8 = bf16[512,512]{1,0:T(8,128)(2,1)S(1)} collective-permute-done((bf16[512,512]{1,0:T(8,128)(2,1)}, bf16[512,512]{1,0:T(8,128)(2,1)S(1)}, u32[]{:S(2)}, u32[]{:S(2)}) %collective-permute-start.8) | collective-permute-done | bytes 524320 | tf_op jit(solution)/shard_map/ppermute | solution.py:263
  146.6 5.2 %collective-permute-start.9 = (bf16[512,512]{1,0:T(8,128)(2,1)S(1)}, bf16[512,512]{1,0:T(8,128)(2,1)S(1)}, u32[]{:S(2)}, u32[]{:S(2)}) collective-permute-start(bf16[512,512]{1,0:T(8,128)(2,1)S(1)} %add_convert_fusion.3), channel_id=1, source_target_pairs={{0,24},{8,0},{16,8},{24,16},{1,25},{9,1},{17,9},{25,17},{2,26},{10... | collective-permute-start | bytes 1572872 | tf_op jit(solution)/shard_map/ppermute | solution.py:269
  151.8 3.8 %collective-permute-start.10 = (bf16[512,512]{1,0:T(8,128)(2,1)}, bf16[512,512]{1,0:T(8,128)(2,1)S(1)}, u32[]{:S(2)}, u32[]{:S(2)}) collective-permute-start(bf16[512,512]{1,0:T(8,128)(2,1)} %get-tuple-element.66), channel_id=1, source_target_pairs={{0,24},{8,0},{16,8},{24,16},{1,25},{9,1},{17,9},{25,17},{2,26},{10... | collective-permute-start | bytes 1572872 | tf_op jit(solution)/shard_map/ppermute | solution.py:265
  156.8 1.9 collective-permute-start.12
  158.7 2.8 %collective-permute-done.7 = bf16[512,512]{1,0:T(8,128)(2,1)S(1)} collective-permute-done((bf16[512,512]{1,0:T(8,128)(2,1)}, bf16[512,512]{1,0:T(8,128)(2,1)S(1)}, u32[]{:S(2)}, u32[]{:S(2)}) %collective-permute-start.7) | collective-permute-done | bytes 524320 | tf_op jit(solution)/shard_map/ppermute | solution.py:264
  161.5 1.5 collective-permute-done.9
  163.3 11.0 %collective-permute-done.10 = bf16[512,512]{1,0:T(8,128)(2,1)S(1)} collective-permute-done((bf16[512,512]{1,0:T(8,128)(2,1)}, bf16[512,512]{1,0:T(8,128)(2,1)S(1)}, u32[]{:S(2)}, u32[]{:S(2)}) %collective-permute-start.10) | collective-permute-done | bytes 524320 | tf_op jit(solution)/shard_map/ppermute | solution.py:265
  174.5 16.8 %reduce-scatter.2.cloned.1.call-done = bf16[1,256,512]{2,1,0:T(8,128)(2,1)} async-done(((bf16[8,256,512]{2,1,0:T(8,128)(2,1)}), bf16[1,256,512]{2,1,0:T(8,128)(2,1)}) %reduce-scatter.2.cloned.1.call-update) | async-done | bytes 262160 | tf_op jit(solution)/shard_map/reduce_scatter | solution.py:255
  191.3 1.9 collective-permute-start.13
  193.2 14.0 %all_to_all.24 = bf16[8,32,512]{2,1,0:T(8,128)(2,1)S(1)} all-to-all(bf16[8,32,512]{2,1,0:T(8,128)(2,1)} %bitcast.13), channel_id=1, replica_groups=mesh['j'=8,'p'=2,'x'=4,'head'=8] {'head'}, dimensions={0} | all-to-all | bytes 524288 | tf_op jit(solution)/shard_map/all_to_all | solution.py:275
  (48 shorter events, 9.9 us)
Async XLA Ops:
  7.2 105.6 %all-gather.3.cloned.1.call-start = ((), (), s32[]{:S(2)}) async-start(), calls=%async_computation.4 | async-start | bytes 4718592 | tf_op jit(solution)/shard_map/all_gather | solution.py:227
  11.0 101.7 %copy-start = (bf16[512,512]{1,0:T(8,128)(2,1)}, bf16[512,512]{1,0:T(8,128)(2,1)S(1)}, u32[]{:S(2)}) copy-start(bf16[512,512]{1,0:T(8,128)(2,1)S(1)} %constant_dynamic-update-slice_fusion.refs_6_) | copy-start | bytes 1572868
  11.1 11.4 %collective-permute-start = (bf16[512,512]{1,0:T(8,128)(2,1)S(1)}, bf16[512,512]{1,0:T(8,128)(2,1)S(1)}, u32[]{:S(2)}, u32[]{:S(2)}) collective-permute-start(bf16[512,512]{1,0:T(8,128)(2,1)S(1)} %constant_dynamic-update-slice_fusion.refs_6_), channel_id=1, source_target_pairs={{0,32},{32,0},{1,33},{33,1},{2,34},{34,2},{3,35},{35,3},{4,36},{36... | collective-permute-start | bytes 1572872 | tf_op jit(solution)/shard_map/ppermute | solution.py:230
  22.5 90.2 %copy-start.3 = (bf16[512,512]{1,0:T(8,128)(2,1)}, bf16[512,512]{1,0:T(8,128)(2,1)S(1)}, u32[]{:S(2)}) copy-start(bf16[512,512]{1,0:T(8,128)(2,1)S(1)} %collective-permute-done.refs_7_) | copy-start | bytes 1572868
  24.7 34.5 %all-to-all-start = ((f32[8,24,128]{2,1,0:T(8,128)}), f32[8,24,128]{2,1,0:T(8,128)S(1)}, u32[]{:S(2)}, u32[]{:S(2)}) async-start(f32[8,24,128]{2,1,0:T(8,128)} %broadcast_in_dim.14), calls=%async_computation | async-start | bytes 196608 | tf_op jit(solution)/shard_map/all_to_all | solution.py:245
  43.6 147.7 %reduce-scatter.2.cloned.1.call-start = ((), (), s32[]{:S(2)}) async-start(), calls=%async_computation.3 | async-start | bytes 2359296 | tf_op jit(solution)/shard_map/reduce_scatter | solution.py:255
  43.7 16.4 %collective-permute-start.5 = (bf16[512,512]{1,0:T(8,128)(2,1)S(1)}, bf16[512,512]{1,0:T(8,128)(2,1)S(1)}, u32[]{:S(2)}, u32[]{:S(2)}) collective-permute-start(bf16[512,512]{1,0:T(8,128)(2,1)S(1)} %constant_dynamic-update-slice_fusion.refs_6_), channel_id=1, source_target_pairs={{0,8},{8,16},{16,24},{24,0},{1,9},{9,17},{17,25},{25,1},{2,10},{10... | collective-permute-start | bytes 1572872 | tf_op jit(solution)/shard_map/ppermute | solution.py:234
  46.8 23.9 %collective-permute-start.3 = (bf16[512,512]{1,0:T(8,128)(2,1)S(1)}, bf16[512,512]{1,0:T(8,128)(2,1)S(1)}, u32[]{:S(2)}, u32[]{:S(2)}) collective-permute-start(bf16[512,512]{1,0:T(8,128)(2,1)S(1)} %constant_dynamic-update-slice_fusion.refs_6_), channel_id=1, source_target_pairs={{0,16},{8,24},{16,0},{24,8},{1,17},{9,25},{17,1},{25,9},{2,18},{10... | collective-permute-start | bytes 1572872 | tf_op jit(solution)/shard_map/ppermute | solution.py:234
  51.2 25.9 %collective-permute-start.1 = (bf16[512,512]{1,0:T(8,128)(2,1)S(1)}, bf16[512,512]{1,0:T(8,128)(2,1)S(1)}, u32[]{:S(2)}, u32[]{:S(2)}) collective-permute-start(bf16[512,512]{1,0:T(8,128)(2,1)S(1)} %constant_dynamic-update-slice_fusion.refs_6_), channel_id=1, source_target_pairs={{0,24},{8,0},{16,8},{24,16},{1,25},{9,1},{17,9},{25,17},{2,26},{10... | collective-permute-start | bytes 1572872 | tf_op jit(solution)/shard_map/ppermute | solution.py:234
  54.2 28.5 %collective-permute-start.6 = (bf16[512,512]{1,0:T(8,128)(2,1)S(1)}, bf16[512,512]{1,0:T(8,128)(2,1)S(1)}, u32[]{:S(2)}, u32[]{:S(2)}) collective-permute-start(bf16[512,512]{1,0:T(8,128)(2,1)S(1)} %collective-permute-done.refs_7_), channel_id=1, source_target_pairs={{0,8},{8,16},{16,24},{24,0},{1,9},{9,17},{17,25},{25,1},{2,10},{10... | collective-permute-start | bytes 1572872 | tf_op jit(solution)/shard_map/ppermute | solution.py:234
  56.5 36.7 %collective-permute-start.4 = (bf16[512,512]{1,0:T(8,128)(2,1)S(1)}, bf16[512,512]{1,0:T(8,128)(2,1)}, u32[]{:S(2)}, u32[]{:S(2)}) collective-permute-start(bf16[512,512]{1,0:T(8,128)(2,1)S(1)} %collective-permute-done.refs_7_), channel_id=1, source_target_pairs={{0,16},{8,24},{16,0},{24,8},{1,17},{9,25},{17,1},{25,9},{2,18},{10... | collective-permute-start | bytes 1572872 | tf_op jit(solution)/shard_map/ppermute | solution.py:234
  59.3 53.5 %copy-start.8 = (f32[8,24,128]{2,1,0:T(8,128)}, f32[8,24,128]{2,1,0:T(8,128)S(1)}, u32[]{:S(2)}) copy-start(f32[8,24,128]{2,1,0:T(8,128)S(1)} %all-to-all-done.refs_1_) | copy-start | bytes 294916
  60.1 52.6 %copy-start.4 = (bf16[512,512]{1,0:T(8,128)(2,1)}, bf16[512,512]{1,0:T(8,128)(2,1)S(1)}, u32[]{:S(2)}) copy-start(bf16[512,512]{1,0:T(8,128)(2,1)S(1)} %collective-permute-done.5.refs_12_) | copy-start | bytes 1572868
  60.1 35.7 %collective-permute-start.2 = (bf16[512,512]{1,0:T(8,128)(2,1)S(1)}, bf16[512,512]{1,0:T(8,128)(2,1)}, u32[]{:S(2)}, u32[]{:S(2)}) collective-permute-start(bf16[512,512]{1,0:T(8,128)(2,1)S(1)} %collective-permute-done.refs_7_), channel_id=1, source_target_pairs={{0,24},{8,0},{16,8},{24,16},{1,25},{9,1},{17,9},{25,17},{2,26},{10... | collective-permute-start | bytes 1572872 | tf_op jit(solution)/shard_map/ppermute | solution.py:234
  70.7 42.0 %copy-start.5 = (bf16[512,512]{1,0:T(8,128)(2,1)}, bf16[512,512]{1,0:T(8,128)(2,1)S(1)}, u32[]{:S(2)}) copy-start(bf16[512,512]{1,0:T(8,128)(2,1)S(1)} %collective-permute-done.3.refs_10_) | copy-start | bytes 1572868
  77.1 35.7 %copy-start.6 = (bf16[512,512]{1,0:T(8,128)(2,1)}, bf16[512,512]{1,0:T(8,128)(2,1)S(1)}, u32[]{:S(2)}) copy-start(bf16[512,512]{1,0:T(8,128)(2,1)S(1)} %collective-permute-done.1.refs_8_) | copy-start | bytes 1572868
  82.7 30.1 %copy-start.7 = (bf16[512,512]{1,0:T(8,128)(2,1)}, bf16[512,512]{1,0:T(8,128)(2,1)S(1)}, u32[]{:S(2)}) copy-start(bf16[512,512]{1,0:T(8,128)(2,1)S(1)} %collective-permute-done.6.refs_13_) | copy-start | bytes 1572868
  128.3 34.8 %copy-start.2 = (f32[512,512]{1,0:T(8,128)S(1)}, f32[512,512]{1,0:T(8,128)}, u32[]{:S(2)}) copy-start(f32[512,512]{1,0:T(8,128)} %get-tuple-element.61) | copy-start | bytes 3145732
  128.3 46.0 %copy-start.1 = (f32[512,512]{1,0:T(8,128)S(1)}, f32[512,512]{1,0:T(8,128)}, u32[]{:S(2)}) copy-start(f32[512,512]{1,0:T(8,128)} %get-tuple-element.65) | copy-start | bytes 3145732
  128.3 17.1 %collective-permute-start.8 = (bf16[512,512]{1,0:T(8,128)(2,1)}, bf16[512,512]{1,0:T(8,128)(2,1)S(1)}, u32[]{:S(2)}, u32[]{:S(2)}) collective-permute-start(bf16[512,512]{1,0:T(8,128)(2,1)} %get-tuple-element.64), channel_id=1, source_target_pairs={{0,24},{8,0},{16,8},{24,16},{1,25},{9,1},{17,9},{25,17},{2,26},{10... | collective-permute-start | bytes 1572872 | tf_op jit(solution)/shard_map/ppermute | solution.py:263
  135.9 19.7 %collective-permute-start.11 = (bf16[512,512]{1,0:T(8,128)(2,1)}, bf16[512,512]{1,0:T(8,128)(2,1)S(1)}, u32[]{:S(2)}, u32[]{:S(2)}) collective-permute-start(bf16[512,512]{1,0:T(8,128)(2,1)} %get-tuple-element.68), channel_id=1, source_target_pairs={{0,8},{8,16},{16,24},{24,0},{1,9},{9,17},{17,25},{25,1},{2,10},{10... | collective-permute-start | bytes 1572872 | tf_op jit(solution)/shard_map/ppermute | solution.py:262
  137.8 23.8 %collective-permute-start.7 = (bf16[512,512]{1,0:T(8,128)(2,1)}, bf16[512,512]{1,0:T(8,128)(2,1)S(1)}, u32[]{:S(2)}, u32[]{:S(2)}) collective-permute-start(bf16[512,512]{1,0:T(8,128)(2,1)} %get-tuple-element.62), channel_id=1, source_target_pairs={{0,8},{8,16},{16,24},{24,0},{1,9},{9,17},{17,25},{25,1},{2,10},{10... | collective-permute-start | bytes 1572872 | tf_op jit(solution)/shard_map/ppermute | solution.py:264
  146.6 16.5 %collective-permute-start.9 = (bf16[512,512]{1,0:T(8,128)(2,1)S(1)}, bf16[512,512]{1,0:T(8,128)(2,1)S(1)}, u32[]{:S(2)}, u32[]{:S(2)}) collective-permute-start(bf16[512,512]{1,0:T(8,128)(2,1)S(1)} %add_convert_fusion.3), channel_id=1, source_target_pairs={{0,24},{8,0},{16,8},{24,16},{1,25},{9,1},{17,9},{25,17},{2,26},{10... | collective-permute-start | bytes 1572872 | tf_op jit(solution)/shard_map/ppermute | solution.py:269
  151.8 22.5 %collective-permute-start.10 = (bf16[512,512]{1,0:T(8,128)(2,1)}, bf16[512,512]{1,0:T(8,128)(2,1)S(1)}, u32[]{:S(2)}, u32[]{:S(2)}) collective-permute-start(bf16[512,512]{1,0:T(8,128)(2,1)} %get-tuple-element.66), channel_id=1, source_target_pairs={{0,24},{8,0},{16,8},{24,16},{1,25},{9,1},{17,9},{25,17},{2,26},{10... | collective-permute-start | bytes 1572872 | tf_op jit(solution)/shard_map/ppermute | solution.py:265
  156.8 17.5 %collective-permute-start.12 = (bf16[512,512]{1,0:T(8,128)(2,1)S(1)}, bf16[512,512]{1,0:T(8,128)(2,1)S(1)}, u32[]{:S(2)}, u32[]{:S(2)}) collective-permute-start(bf16[512,512]{1,0:T(8,128)(2,1)S(1)} %add_convert_fusion.1), channel_id=1, source_target_pairs={{0,8},{8,16},{16,24},{24,0},{1,9},{9,17},{17,25},{25,1},{2,10},{10... | collective-permute-start | bytes 1572872 | tf_op jit(solution)/shard_map/ppermute | solution.py:268
  191.3 16.6 %collective-permute-start.13 = (bf16[512,512]{1,0:T(8,128)(2,1)S(1)}, bf16[512,512]{1,0:T(8,128)(2,1)S(1)}, u32[]{:S(2)}, u32[]{:S(2)}) collective-permute-start(bf16[512,512]{1,0:T(8,128)(2,1)S(1)} %add_convert_fusion.2), channel_id=1, source_target_pairs={{0,32},{32,0},{1,33},{33,1},{2,34},{34,2},{3,35},{35,3},{4,36},{36... | collective-permute-start | bytes 1572872 | tf_op jit(solution)/shard_map/ppermute | solution.py:271
Sparse Core Ops, SparseCore 0:
  10.1 102.5 all-gather.2
  128.4 62.8 reduce-scatter.1
